TPU v7x, 32 devices: a whole 2x2x4 slice. The times are simulated.
32 devices in a mesh: seq: 4 (over x, core), chan: 8 (over z, y).
Axes of the slice: x: 2, y: 2, z: 4, core: 2. Of those that a mesh axis runs over, the one named last changes fastest.
Arguments:
- tokens: bfloat16 [8, 1024, 2048], P(None, ('seq', 'chan')), may hold values from -6 to 6
- norm_gain: bfloat16 [2048], P(('chan', 'seq')), may hold values from 0.5 to 1.5
- mlp_gain: bfloat16 [2048], P(('chan', 'seq')), may hold values from 0.5 to 1.5
- recur_proj: bfloat16 [2048, 2560], P('seq', 'chan'), may hold values from -0.125 to 0.125
- branch_proj: bfloat16 [2048, 2560], P('seq', 'chan'), may hold values from -0.125 to 0.125
- out_proj: bfloat16 [2560, 2048], P('chan', 'seq'), may hold values from -0.25 to 0.25
- gate_proj: bfloat16 [2048, 6144], P('seq', 'chan'), may hold values from -0.125 to 0.125
- up_proj: bfloat16 [2048, 6144], P('seq', 'chan'), may hold values from -0.125 to 0.125
- down_proj: bfloat16 [6144, 2048], P('chan', 'seq'), may hold values from -0.15625 to 0.15625
- recur_gate: bfloat16 [16, 160, 160], P('chan', 'seq'), may hold values from -0.5 to 0.5
- input_gate: bfloat16 [16, 160, 160], P('chan', 'seq'), may hold values from -0.5 to 0.5
- recur_bias: bfloat16 [2560], P(('chan', 'seq')), may hold values from -3 to 3
- input_bias: bfloat16 [2560], P(('chan', 'seq')), may hold values from -3 to 3
- decay_param: bfloat16 [2560], P(('chan', 'seq')), may hold values from 4.5 to 13
- conv_bias: bfloat16 [2560], P(('chan', 'seq')), may hold values from -3 to 3
- conv_weight: bfloat16 [4, 2560], P(None, ('chan', 'seq')), may hold values from -3 to 3
- init_state: bfloat16 [8, 2560], P(None, ('chan', 'seq')), may hold values from -6 to 6
- init_tail: bfloat16 [8, 3, 2560], P(None, None, ('chan', 'seq')), may hold values from -6 to 6
- reset_flags: int32 [8], replicated, may hold values from 0 to 1
- cotangent: bfloat16 [8, 1024, 2048], P(None, ('seq', 'chan')), may hold values from -6 to 6
Outputs:
- mixed: bfloat16 [8, 1024, 2048], P(None, ('seq', 'chan'))
- tokens_grad: float32 [8, 1024, 2048], P(None, ('seq', 'chan'))
- norm_gain_grad: float32 [2048], P(('chan', 'seq'))
- mlp_gain_grad: float32 [2048], P(('chan', 'seq'))
- recur_proj_grad: float32 [2048, 2560], P('seq', 'chan')
- branch_proj_grad: float32 [2048, 2560], P('seq', 'chan')
- out_proj_grad: float32 [2560, 2048], P('chan', 'seq')
- gate_proj_grad: float32 [2048, 6144], P('seq', 'chan')
- up_proj_grad: float32 [2048, 6144], P('seq', 'chan')
- down_proj_grad: float32 [6144, 2048], P('chan', 'seq')
- recur_gate_grad: float32 [16, 160, 160], P('chan', 'seq')
- input_gate_grad: float32 [16, 160, 160], P('chan', 'seq')
- recur_bias_grad: float32 [2560], P(('chan', 'seq'))
- input_bias_grad: float32 [2560], P(('chan', 'seq'))
- decay_grad: float32 [2560], P(('chan', 'seq'))
- conv_bias_grad: float32 [2560], P(('chan', 'seq'))
- conv_weight_grad: float32 [4, 2560], P(None, ('chan', 'seq'))
- state_grad: float32 [8, 2560], P(None, ('chan', 'seq'))
- tail_grad: float32 [8, 3, 2560], P(None, None, ('chan', 'seq'))
- group_states: float32 [4, 8, 2560], P('seq', None, 'chan')
- group_tails: bfloat16 [4, 8, 3, 2560], P('seq', None, None, 'chan')
All inputs are finite; a program needn't handle non-finite values.
Results may differ from a plain program's by a relative error of at most 0.02.
Values may be sent and summed in bfloat16 or wider, within the bound.
No kernel may reach another device: no remote copies, remote signals or barrier semaphores. Data moves between devices by JAX's collectives and lax.ppermute only.
A program may use at most 384 MiB of HBM per device.

v0:
```python
import jax
import jax.numpy as jnp
from jax import lax
from jax.sharding import PartitionSpec as P


def from_behind(block, axis, distance):
    devices = range(lax.axis_size(axis))
    route = [(i - distance, i) for i in devices if i - distance in devices]
    return lax.ppermute(block, axis, route)


def prefix(value, axis, join, neutral, backward):
    count, mine = (lax.axis_size(axis), lax.axis_index(axis))
    pieces = jax.tree.map(lambda part: lax.all_gather(part, axis), value)
    if backward:
        pieces = jax.tree.map(lambda part: part[::-1], pieces)
        mine = count - 1 - mine
    total = jax.tree.map(
        lambda part, zero: jnp.full_like(part, 0) + jnp.asarray(zero, part.dtype), value, neutral
    )

    def hop(position, total):
        longer = join(total, jax.tree.map(lambda part: part[position], pieces))
        return jax.tree.map(lambda new, old: jnp.where(position < mine, new, old), longer, total)

    return lax.fori_loop(0, count - 1, hop, total)


def affine_pair(earlier, later):
    return (earlier[0] * later[0], later[0] * earlier[1] + later[1])


def matmul(left, right):
    return jnp.dot(left, right, preferred_element_type=jnp.float32)


def contract_tokens(left, right):
    return lax.dot_general(
        left, right, (((0, 1), (0, 1)), ((), ())), preferred_element_type=jnp.float32
    )


def times_transpose(left, right):
    return lax.dot_general(
        left, right, (((2,), (1,)), ((), ())), preferred_element_type=jnp.float32
    )


def norm_back(grad_norm, normed, inv_root, gain):
    scaled = grad_norm * gain
    mean_term = jnp.mean(scaled * normed, axis=-1, keepdims=True)
    return inv_root * (scaled - normed * mean_term)


def own_rows(value, start, share):
    return lax.dynamic_slice_in_dim(value, start, share, 1)


def shards(
    tokens,
    norm_gain,
    mlp_gain,
    recur_proj,
    branch_proj,
    out_proj,
    gate_proj,
    up_proj,
    down_proj,
    recur_gate,
    input_gate,
    recur_bias,
    input_bias,
    decay_param,
    conv_bias,
    conv_weight,
    init_state,
    init_tail,
    reset_flags,
    cotangent,
):
    (
        full_recur,
        full_branch,
        full_out,
        full_gate,
        full_up,
        full_down,
        blocks_recur,
        blocks_input,
        shift_recur,
        shift_input,
        decay_local,
        conv_shift,
        conv_taps,
        state_start,
        tail_start,
        gain_norm,
        gain_mlp,
    ) = (
        lax.all_gather(recur_proj, "seq", axis=0, tiled=True),
        lax.all_gather(branch_proj, "seq", axis=0, tiled=True),
        lax.all_gather(out_proj, "seq", axis=1, tiled=True),
        lax.all_gather(gate_proj, "seq", axis=0, tiled=True),
        lax.all_gather(up_proj, "seq", axis=0, tiled=True),
        lax.all_gather(down_proj, "seq", axis=1, tiled=True),
        lax.all_gather(recur_gate, "seq", axis=1, tiled=True),
        lax.all_gather(input_gate, "seq", axis=1, tiled=True),
        lax.all_gather(recur_bias, "seq", axis=0, tiled=True),
        lax.all_gather(input_bias, "seq", axis=0, tiled=True),
        lax.all_gather(decay_param, "seq", axis=0, tiled=True),
        lax.all_gather(conv_bias, "seq", axis=0, tiled=True),
        lax.all_gather(conv_weight, "seq", axis=1, tiled=True),
        lax.all_gather(init_state, "seq", axis=1, tiled=True),
        lax.all_gather(init_tail, "seq", axis=2, tiled=True),
        lax.all_gather(norm_gain, "seq", axis=0, tiled=True),
        lax.all_gather(mlp_gain, "seq", axis=0, tiled=True),
    )
    full_group, gain_one, gain_two = (
        lax.all_gather(tokens, "chan", axis=1, tiled=True),
        lax.all_gather(gain_norm, "chan", axis=0, tiled=True),
        lax.all_gather(gain_mlp, "chan", axis=0, tiled=True),
    )
    rows = tokens.shape[0]
    share = tokens.shape[1]
    group = full_group.shape[1]
    taps = conv_taps.shape[0]
    lag = taps - 1
    heads = blocks_recur.shape[0]
    start = lax.axis_index("chan") * share
    first = lax.axis_index("seq") == 0
    keep = (1 - reset_flags).astype(jnp.float32)[:, None]
    gain_one32 = gain_one.astype(jnp.float32)
    gain_two32 = gain_two.astype(jnp.float32)
    inputs32 = full_group.astype(jnp.float32)
    inv_one = lax.rsqrt(jnp.mean(inputs32 * inputs32, axis=-1, keepdims=True) + 1e-06)
    normed_one = inputs32 * inv_one
    normal_in = (normed_one * gain_one32).astype(jnp.bfloat16)
    conv_in = matmul(normal_in, full_recur).astype(jnp.bfloat16)
    branch_pre = matmul(normal_in, full_branch)
    branch_act, branch_pull = jax.vjp(jax.nn.gelu, branch_pre)
    edge = from_behind(conv_in[:, group - lag :], "seq", 1)
    tail_kept = (tail_start.astype(jnp.float32) * keep[:, :, None]).astype(jnp.bfloat16)
    edge = jnp.where(first, tail_kept, edge)
    padded = jnp.concatenate([edge, conv_in], axis=1).astype(jnp.float32)
    taps32 = conv_taps.astype(jnp.float32)
    conv_out = conv_shift.astype(jnp.float32) + sum(
        (taps32[offset] * padded[:, lag - offset : lag - offset + group] for offset in range(taps))
    )
    conv_low = conv_out.astype(jnp.bfloat16)
    split_v = conv_low.reshape(rows, group, heads, -1)
    recur_pre = jnp.einsum(
        "rchb,hbe->rche", split_v, blocks_recur, preferred_element_type=jnp.float32
    ).reshape(rows, group, -1) + shift_recur.astype(jnp.float32)
    input_pre = jnp.einsum(
        "rchb,hbe->rche", split_v, blocks_input, preferred_element_type=jnp.float32
    ).reshape(rows, group, -1) + shift_input.astype(jnp.float32)
    recur_rate = jax.nn.sigmoid(recur_pre)
    input_rate = jax.nn.sigmoid(input_pre)
    decay32 = decay_local.astype(jnp.float32)
    soft_decay = jax.nn.softplus(-decay32)
    log_decay = -8.0 * recur_rate * soft_decay
    decay = jnp.exp(log_decay)
    root = jnp.sqrt(-jnp.expm1(2.0 * log_decay))
    conv_val = conv_low.astype(jnp.float32)
    drive = conv_val * input_rate * root
    prod_decay, zero_state = lax.associative_scan(affine_pair, (decay, drive), axis=1)
    group_decay = prod_decay[:, -1]
    group_drive = zero_state[:, -1]
    unit = jnp.ones_like(group_decay)
    empty = jnp.zeros_like(group_decay)
    before_decay, before_drive = prefix(
        (group_decay, group_drive), "seq", affine_pair, (unit, empty), False
    )
    enter_state = before_decay * (state_start.astype(jnp.float32) * keep) + before_drive
    states = zero_state + prod_decay * enter_state[:, None]
    mixed_rec = (states * branch_act).astype(jnp.bfloat16)
    branch_terms = matmul(mixed_rec, full_out)
    resid = inputs32 + lax.psum(branch_terms, "chan")
    inv_two = lax.rsqrt(jnp.mean(resid * resid, axis=-1, keepdims=True) + 1e-06)
    normed_two = resid * inv_two
    normal_mid = (normed_two * gain_two32).astype(jnp.bfloat16)
    resid_fwd_own = own_rows(resid, start, share)
    normed_two_own = own_rows(normed_two, start, share)
    gate_pre = matmul(normal_mid, full_gate)
    up_pre = matmul(normal_mid, full_up)
    gate_act, gate_pull = jax.vjp(jax.nn.gelu, gate_pre)
    hidden = (gate_act * up_pre).astype(jnp.bfloat16)
    mlp_out = lax.psum_scatter(
        matmul(hidden, full_down).astype(jnp.bfloat16), "chan", scatter_dimension=1, tiled=True
    ).astype(jnp.float32)
    mixed = (resid_fwd_own + mlp_out).astype(jnp.bfloat16)
    grad_full = lax.all_gather(cotangent, "chan", axis=1, tiled=True)
    grad_hidden = times_transpose(grad_full, full_down)
    gate_slope = gate_pull(jnp.ones_like(gate_pre))[0]
    grad_gate = (grad_hidden * up_pre * gate_slope).astype(jnp.bfloat16)
    grad_up = (grad_hidden * gate_act).astype(jnp.bfloat16)
    down_grad = contract_tokens(hidden, grad_full)
    gate_grad = contract_tokens(normal_mid, grad_gate)
    up_grad = contract_tokens(normal_mid, grad_up)
    mid_terms = times_transpose(grad_gate, full_gate) + times_transpose(grad_up, full_up)
    mid_sum = lax.psum(mid_terms, "chan")
    resid_grad = grad_full.astype(jnp.float32) + norm_back(mid_sum, normed_two, inv_two, gain_two32)
    resid_low = resid_grad.astype(jnp.bfloat16)
    resid_own = own_rows(resid_grad, start, share)
    mid_own = own_rows(mid_sum, start, share)
    gain_two_part = jnp.sum(mid_own * normed_two_own, axis=(0, 1))
    out_grad = contract_tokens(mixed_rec, resid_low)
    grad_mixed = times_transpose(resid_low, full_out)
    grad_states = grad_mixed * branch_act
    grad_branch = branch_pull(grad_mixed * states)[0].astype(jnp.bfloat16)
    next_decay = jnp.concatenate([decay[:, 1:], jnp.ones_like(decay[:, :1])], axis=1)
    rev_decay, rev_grad = lax.associative_scan(
        affine_pair, (next_decay, grad_states), axis=1, reverse=True
    )
    local_enter = decay[:, 0] * rev_grad[:, 0]
    later_decay, end_grad = prefix(
        (group_decay, local_enter), "seq", affine_pair, (unit, empty), True
    )
    total_grad = rev_grad + rev_decay * end_grad[:, None]
    prev_states = jnp.concatenate([enter_state[:, None], states[:, :-1]], axis=1)
    grad_log = (
        total_grad * prev_states * decay - total_grad * conv_val * input_rate * decay * decay / root
    )
    decay_grad = jnp.sum(grad_log * recur_rate, axis=(0, 1)) * 8.0 * jax.nn.sigmoid(-decay32)
    grad_recur_pre = (grad_log * -8.0 * soft_decay * recur_rate * (1.0 - recur_rate)).astype(
        jnp.bfloat16
    )
    grad_input_pre = (total_grad * conv_val * root * input_rate * (1.0 - input_rate)).astype(
        jnp.bfloat16
    )
    recur_bias_grad = jnp.sum(grad_recur_pre.astype(jnp.float32), axis=(0, 1))
    input_bias_grad = jnp.sum(grad_input_pre.astype(jnp.float32), axis=(0, 1))
    recur_split = grad_recur_pre.reshape(rows, group, heads, -1)
    input_split = grad_input_pre.reshape(rows, group, heads, -1)
    blocks_recur_grad = jnp.einsum(
        "rchb,rche->hbe", split_v, recur_split, preferred_element_type=jnp.float32
    )
    blocks_input_grad = jnp.einsum(
        "rchb,rche->hbe", split_v, input_split, preferred_element_type=jnp.float32
    )
    grad_conv = total_grad * input_rate * root
    grad_conv = grad_conv + jnp.einsum(
        "rche,hbe->rchb", recur_split, blocks_recur, preferred_element_type=jnp.float32
    ).reshape(rows, group, -1)
    grad_conv = grad_conv + jnp.einsum(
        "rche,hbe->rchb", input_split, blocks_input, preferred_element_type=jnp.float32
    ).reshape(rows, group, -1)
    conv_shift_grad = jnp.sum(grad_conv, axis=(0, 1))
    taps_grad = jnp.stack(
        [
            jnp.sum(grad_conv * padded[:, lag - offset : lag - offset + group], axis=(0, 1))
            for offset in range(taps)
        ]
    )
    grad_padded = sum(
        (
            jnp.pad(taps32[offset] * grad_conv, ((0, 0), (lag - offset, offset), (0, 0)))
            for offset in range(taps)
        )
    )
    edge_back = from_behind(grad_padded[:, :lag], "seq", -1)
    grad_conv_in = grad_padded[:, lag:] + jnp.pad(edge_back, ((0, 0), (group - lag, 0), (0, 0)))
    tail_grad = jnp.where(first, grad_padded[:, :lag] * keep[:, :, None], 0.0)
    state_grad = keep * before_decay * local_enter
    grad_in_low = grad_conv_in.astype(jnp.bfloat16)
    recur_proj_grad = contract_tokens(normal_in, grad_in_low)
    branch_proj_grad = contract_tokens(normal_in, grad_branch)
    first_terms = times_transpose(grad_in_low, full_recur) + times_transpose(
        grad_branch, full_branch
    )
    gain_one_part = jnp.sum(first_terms * normed_one, axis=(0, 1))
    first_own, gain_one_share, gain_two_share = (
        lax.psum_scatter(
            first_terms.astype(jnp.bfloat16), "chan", scatter_dimension=1, tiled=True
        ).astype(jnp.float32),
        lax.psum_scatter(
            gain_one_part.astype(jnp.bfloat16), "chan", scatter_dimension=0, tiled=True
        ).astype(jnp.float32),
        lax.psum_scatter(
            gain_two_part.astype(jnp.bfloat16), "chan", scatter_dimension=0, tiled=True
        ).astype(jnp.float32),
    )
    tokens_grad = resid_own + norm_back(
        first_own, own_rows(normed_one, start, share), own_rows(inv_one, start, share), gain_one32
    )
    results = (
        lax.psum_scatter(
            recur_proj_grad.astype(jnp.bfloat16), "seq", scatter_dimension=0, tiled=True
        ).astype(jnp.float32),
        lax.psum_scatter(
            branch_proj_grad.astype(jnp.bfloat16), "seq", scatter_dimension=0, tiled=True
        ).astype(jnp.float32),
        lax.psum_scatter(
            out_grad.astype(jnp.bfloat16), "seq", scatter_dimension=1, tiled=True
        ).astype(jnp.float32),
        lax.psum_scatter(
            gate_grad.astype(jnp.bfloat16), "seq", scatter_dimension=0, tiled=True
        ).astype(jnp.float32),
        lax.psum_scatter(
            up_grad.astype(jnp.bfloat16), "seq", scatter_dimension=0, tiled=True
        ).astype(jnp.float32),
        lax.psum_scatter(
            down_grad.astype(jnp.bfloat16), "seq", scatter_dimension=1, tiled=True
        ).astype(jnp.float32),
        lax.psum_scatter(
            blocks_recur_grad.astype(jnp.bfloat16), "seq", scatter_dimension=1, tiled=True
        ).astype(jnp.float32),
        lax.psum_scatter(
            blocks_input_grad.astype(jnp.bfloat16), "seq", scatter_dimension=1, tiled=True
        ).astype(jnp.float32),
        lax.psum_scatter(
            recur_bias_grad.astype(jnp.bfloat16), "seq", scatter_dimension=0, tiled=True
        ).astype(jnp.float32),
        lax.psum_scatter(
            input_bias_grad.astype(jnp.bfloat16), "seq", scatter_dimension=0, tiled=True
        ).astype(jnp.float32),
        lax.psum_scatter(
            decay_grad.astype(jnp.bfloat16), "seq", scatter_dimension=0, tiled=True
        ).astype(jnp.float32),
        lax.psum_scatter(
            conv_shift_grad.astype(jnp.bfloat16), "seq", scatter_dimension=0, tiled=True
        ).astype(jnp.float32),
        lax.psum_scatter(
            taps_grad.astype(jnp.bfloat16), "seq", scatter_dimension=1, tiled=True
        ).astype(jnp.float32),
        lax.psum_scatter(
            state_grad.astype(jnp.bfloat16), "seq", scatter_dimension=1, tiled=True
        ).astype(jnp.float32),
        lax.psum_scatter(
            tail_grad.astype(jnp.bfloat16), "seq", scatter_dimension=2, tiled=True
        ).astype(jnp.float32),
        lax.psum_scatter(
            gain_one_share.astype(jnp.bfloat16), "seq", scatter_dimension=0, tiled=True
        ).astype(jnp.float32),
        lax.psum_scatter(
            gain_two_share.astype(jnp.bfloat16), "seq", scatter_dimension=0, tiled=True
        ).astype(jnp.float32),
    )
    group_states = states[:, -1][None]
    group_tails = conv_in[:, group - lag :][None]
    return (
        mixed,
        tokens_grad,
        results[15],
        results[16],
        results[0],
        results[1],
        results[2],
        results[3],
        results[4],
        results[5],
        results[6],
        results[7],
        results[8],
        results[9],
        results[10],
        results[11],
        results[12],
        results[13],
        results[14],
        group_states,
        group_tails,
    )


def solution(mesh):
    in_specs = (
        P(None, ("seq", "chan"), None),
        P(("chan", "seq")),
        P(("chan", "seq")),
        P("seq", "chan"),
        P("seq", "chan"),
        P("chan", "seq"),
        P("seq", "chan"),
        P("seq", "chan"),
        P("chan", "seq"),
        P("chan", "seq", None),
        P("chan", "seq", None),
        P(("chan", "seq")),
        P(("chan", "seq")),
        P(("chan", "seq")),
        P(("chan", "seq")),
        P(None, ("chan", "seq")),
        P(None, ("chan", "seq")),
        P(None, None, ("chan", "seq")),
        P(),
        P(None, ("seq", "chan"), None),
    )
    out_specs = (
        P(None, ("seq", "chan"), None),
        P(None, ("seq", "chan"), None),
        P(("chan", "seq")),
        P(("chan", "seq")),
        P("seq", "chan"),
        P("seq", "chan"),
        P("chan", "seq"),
        P("seq", "chan"),
        P("seq", "chan"),
        P("chan", "seq"),
        P("chan", "seq", None),
        P("chan", "seq", None),
        P(("chan", "seq")),
        P(("chan", "seq")),
        P(("chan", "seq")),
        P(("chan", "seq")),
        P(None, ("chan", "seq")),
        P(None, ("chan", "seq")),
        P(None, None, ("chan", "seq")),
        P("seq", None, "chan"),
        P("seq", None, None, "chan"),
    )
    return jax.shard_map(shards, mesh=mesh, in_specs=in_specs, out_specs=out_specs, check_vma=False)
```

profile of v0, /device:TPU:0, one launch (start us, length us, event | category | flops | bytes accessed | tf_op | source)
XLA Modules:
  0.0 2939.7 jit_solution(5408602317793672434)
XLA Ops:
  35.7 21.2 all-gather.4
  81.5 56.4 %all-gather.16.cloned.1.call-done = bf16[8,256,2048]{2,1,0:T(8,128)(2,1)} async-done(((bf16[8,32,2048]{2,1,0:T(8,128)(2,1)}), bf16[8,256,2048]{2,1,0:T(8,128)(2,1)}) %all-gather.16.cloned.1.call-update) | async-done | bytes 8388624 | tf_op jit(solution)/shard_map/all_gather | solution.py:120
  364.3 15.4 pad.245
  387.6 22.8 pad.230
  410.4 29.8 %pad.231 = f32[8,128,320]{2,0,1:T(8,128)} pad(f32[8,64,320]{2,0,1:T(8,128)} %add.597, f32[]{:T(128)} %constant.90.clone.1), padding=0_0_0x1_0_1x0_0_0 | pad | bytes 1966084 | tf_op jit(solution)/shard_map/pad | solution.py:167
  440.2 29.8 %pad.247 = f32[8,128,320]{2,0,1:T(8,128)} pad(f32[8,64,320]{2,0,1:T(8,128)} %add.607, f32[]{:T(128)} %constant.90.clone.1), padding=0_0_0x1_0_1x0_0_0 | pad | bytes 1966084 | tf_op jit(solution)/shard_map/pad | solution.py:167
  477.3 39.9 %pad.248 = f32[8,256,320]{2,0,1:T(8,128)} pad(f32[8,128,320]{2,0,1:T(8,128)S(1)} %pad_maximum_fusion.1, f32[]{:T(128)} %constant.90.clone.1), padding=0_0_0x0_1_1x0_0_0 | pad | bytes 3932164 | tf_op jit(solution)/shard_map/pad | solution.py:167
  518.7 40.0 %pad.232 = f32[8,256,320]{2,0,1:T(8,128)} pad(f32[8,128,320]{2,0,1:T(8,128)S(1)} %pad_maximum_fusion, f32[]{:T(128)} %constant.90.clone.1), padding=0_0_0x0_1_1x0_0_0 | pad | bytes 3932164 | tf_op jit(solution)/shard_map/pad | solution.py:167
  558.7 39.9 %pad.233 = f32[8,256,320]{2,0,1:T(8,128)} pad(f32[8,128,320]{2,0,1:T(8,128)S(1)} %add.599, f32[]{:T(128)} %constant.90.clone.1), padding=0_0_0x1_0_1x0_0_0 | pad | bytes 3932164 | tf_op jit(solution)/shard_map/pad | solution.py:167
  604.9 57.8 %pad.249 = f32[8,256,320]{2,0,1:T(8,128)} pad(f32[8,128,320]{2,0,1:T(8,128)} %add.608, f32[]{:T(128)} %constant.90.clone.1), padding=0_0_0x1_0_1x0_0_0 | pad | bytes 3932164 | tf_op jit(solution)/shard_map/pad | solution.py:167
  691.0 20.8 all-gather.6
  711.9 486.2 %all-reduce.95.cloned.1.call-done = f32[8,256,2048]{2,1,0:T(8,128)} async-done(((f32[8,256,2048]{2,1,0:T(8,128)}), f32[8,256,2048]{2,1,0:T(8,128)}) %all-reduce.95.cloned.1.call-update) | async-done | bytes 16777232 | tf_op jit(solution)/shard_map/psum | solution.py:179
  1238.9 18.4 all-gather.24.cloned.1.call-done
  1268.9 18.5 all-gather.28.cloned.1.call-done
  1287.4 127.1 %all-gather.30.cloned.1.call-done = bf16[8,256,2048]{2,1,0:T(8,128)(2,1)} async-done(((bf16[8,32,2048]{2,1,0:T(8,128)(2,1)}), bf16[8,256,2048]{2,1,0:T(8,128)(2,1)}) %all-gather.30.cloned.1.call-update) | async-done | bytes 8388624 | tf_op jit(solution)/shard_map/all_gather | solution.py:193
  1414.6 16.9 multiply_convert_fusion.2
  1516.0 447.3 %all-reduce.97.cloned.1.call-done = f32[8,256,2048]{2,1,0:T(8,128)} async-done(((f32[8,256,2048]{2,1,0:T(8,128)}), f32[8,256,2048]{2,1,0:T(8,128)}) %all-reduce.97.cloned.1.call-update) | async-done | bytes 16777232 | tf_op jit(solution)/shard_map/psum | solution.py:202
  2150.6 15.4 pad.277
  2166.0 15.4 pad.261
  2189.7 29.8 %pad.262 = f32[8,128,320]{2,0,1:T(8,128)} pad(f32[8,64,320]{2,0,1:T(8,128)} %pad_maximum_fusion.5, f32[]{:T(128)} %constant.90.clone.1), padding=0_0_0x0_1_1x0_0_0 | pad | bytes 1966084 | tf_op jit(solution)/shard_map/pad | solution.py:213
  2221.6 29.8 %pad.278 = f32[8,128,320]{2,0,1:T(8,128)} pad(f32[8,64,320]{2,0,1:T(8,128)} %pad_maximum_fusion.6, f32[]{:T(128)} %constant.90.clone.1), padding=0_0_0x0_1_1x0_0_0 | pad | bytes 1966084 | tf_op jit(solution)/shard_map/pad | solution.py:213
  2251.4 29.8 %pad.279 = f32[8,128,320]{2,0,1:T(8,128)} pad(f32[8,64,320]{2,0,1:T(8,128)} %add.650, f32[]{:T(128)} %constant.90.clone.1), padding=0_0_0x1_0_1x0_0_0 | pad | bytes 1966084 | tf_op jit(solution)/shard_map/pad | solution.py:213
  2281.2 29.8 %pad.263 = f32[8,128,320]{2,0,1:T(8,128)} pad(f32[8,64,320]{2,0,1:T(8,128)} %add.640, f32[]{:T(128)} %constant.90.clone.1), padding=0_0_0x1_0_1x0_0_0 | pad | bytes 1966084 | tf_op jit(solution)/shard_map/pad | solution.py:213
  2320.3 57.8 %pad.264 = f32[8,256,320]{2,0,1:T(8,128)} pad(f32[8,128,320]{2,0,1:T(8,128)} %pad_maximum_fusion.2, f32[]{:T(128)} %constant.90.clone.1), padding=0_0_0x0_1_1x0_0_0 | pad | bytes 3932164 | tf_op jit(solution)/shard_map/pad | solution.py:213
  2378.1 57.8 %pad.265 = f32[8,256,320]{2,0,1:T(8,128)} pad(f32[8,128,320]{2,0,1:T(8,128)} %add.642, f32[]{:T(128)} %constant.90.clone.1), padding=0_0_0x1_0_1x0_0_0 | pad | bytes 3932164 | tf_op jit(solution)/shard_map/pad | solution.py:213
  2448.5 40.1 %pad.280 = f32[8,256,320]{2,0,1:T(8,128)} pad(f32[8,128,320]{2,0,1:T(8,128)S(1)} %concatenate.122, f32[]{:T(128)} %constant.90.clone.1), padding=0_0_0x0_1_1x0_0_0 | pad | bytes 3932164 | tf_op jit(solution)/shard_map/pad | solution.py:213
  2488.6 39.9 %pad.281 = f32[8,256,320]{2,0,1:T(8,128)} pad(f32[8,128,320]{2,0,1:T(8,128)S(1)} %copy-done.31, f32[]{:T(128)} %constant.90.clone.1), padding=0_0_0x1_0_1x0_0_0 | pad | bytes 3932164 | tf_op jit(solution)/shard_map/pad | solution.py:213
  2641.1 16.4 multiply_reduce_fusion
  2680.1 19.1 all-reduce.87
  2716.1 27.2 reduce-scatter.26.cloned.1.call-done
  2745.2 27.8 reduce-scatter.24.cloned.1.call-done
  2774.9 151.3 %reduce-scatter.22.cloned.1.call-done = bf16[8,32,2048]{2,1,0:T(8,128)(2,1)} async-done(((bf16[8,256,2048]{2,1,0:T(8,128)(2,1)}), bf16[8,32,2048]{2,1,0:T(8,128)(2,1)}) %reduce-scatter.22.cloned.1.call-update) | async-done | bytes 1048592 | tf_op jit(solution)/shard_map/reduce_scatter | solution.py:274
  (610 shorter events, 846.3 us)
Async XLA Ops:
  7.2 130.7 %all-gather.16.cloned.1.call-start = ((), (), s32[]{:S(2)}) async-start(), calls=%async_computation.11 | async-start | bytes 9437184 | tf_op jit(solution)/shard_map/all_gather | solution.py:120
  7.9 147.9 %all-gather.18.cloned.1.call-start = ((), (), s32[]{:S(2)}) async-start(), calls=%async_computation.12 | async-start | bytes 1638400 | tf_op jit(solution)/shard_map/all_gather | solution.py:101
  8.7 167.0 %all-gather.20.cloned.1.call-start = ((), (), s32[]{:S(2)}) async-start(), calls=%async_computation.13 | async-start | bytes 1638400 | tf_op jit(solution)/shard_map/all_gather | solution.py:102
  9.4 668.8 %all-gather.22.cloned.1.call-start = ((), (), s32[]{:S(2)}) async-start(), calls=%async_computation.14 | async-start | bytes 1638400 | tf_op jit(solution)/shard_map/all_gather | solution.py:103
  10.0 1188.1 %all-reduce.95.cloned.1.call-start = ((), (), s32[]{:S(2)}) async-start(), calls=%async_computation.15 | async-start | bytes 33554432 | tf_op jit(solution)/shard_map/psum | solution.py:179
  13.4 174.6 %copy-start.100 = (f32[8]{0:T(128)}, f32[8]{0:T(128)S(1)}, u32[]{:S(2)}) copy-start(f32[8]{0:T(128)S(1)} %subtract_convert_fusion) | copy-start | bytes 100
  35.7 173.6 %copy-start.70 = (f32[320]{0:T(512)}, f32[320]{0:T(512)S(1)}, u32[]{:S(2)}) copy-start(f32[320]{0:T(512)S(1)} %get-tuple-element.356) | copy-start | bytes 3844
  35.7 173.6 %copy-start.72 = (f32[320]{0:T(512)}, f32[320]{0:T(512)S(1)}, u32[]{:S(2)}) copy-start(f32[320]{0:T(512)S(1)} %get-tuple-element.357) | copy-start | bytes 3844
  35.7 173.6 %copy-start.74 = (f32[320]{0:T(512)}, f32[320]{0:T(512)S(1)}, u32[]{:S(2)}) copy-start(f32[320]{0:T(512)S(1)} %get-tuple-element.358) | copy-start | bytes 3844
  56.9 118.8 %copy-start.68 = (f32[8,1,256]{2,1,0:T(1,128)}, f32[8,1,256]{2,1,0:T(1,128)S(1)}, u32[]{:S(2)}) copy-start(f32[8,1,256]{2,1,0:T(1,128)S(1)} %convert_element_type.276) | copy-start | bytes 24580
  69.4 125.3 %copy-start.47 = (bf16[2,160,160]{2,1,0:T(8,128)(2,1)}, bf16[2,160,160]{2,1,0:T(8,128)(2,1)S(1)}, u32[]{:S(2)}) copy-start(bf16[2,160,160]{2,1,0:T(8,128)(2,1)S(1)} %all_gather.83) | copy-start | bytes 307204
  75.1 126.9 %copy-start.45 = (bf16[2,160,160]{2,1,0:T(8,128)(2,1)}, bf16[2,160,160]{2,1,0:T(8,128)(2,1)S(1)}, u32[]{:S(2)}) copy-start(bf16[2,160,160]{2,1,0:T(8,128)(2,1)S(1)} %all_gather.81) | copy-start | bytes 307204
  164.5 23.4 collective-permute-start
  688.2 539.0 %all-gather.26.cloned.1.call-start = ((), (), s32[]{:S(2)}) async-start(), calls=%async_computation.17 | async-start | bytes 3932160 | tf_op jit(solution)/shard_map/all_gather | solution.py:105
  688.7 568.6 %all-gather.24.cloned.1.call-start = ((), (), s32[]{:S(2)}) async-start(), calls=%async_computation.16 | async-start | bytes 3932160 | tf_op jit(solution)/shard_map/all_gather | solution.py:104
  689.5 597.9 %all-gather.28.cloned.1.call-start = ((), (), s32[]{:S(2)}) async-start(), calls=%async_computation.18 | async-start | bytes 3932160 | tf_op jit(solution)/shard_map/all_gather | solution.py:106
  690.2 724.3 %all-gather.30.cloned.1.call-start = ((), (), s32[]{:S(2)}) async-start(), calls=%async_computation.20 | async-start | bytes 9437184 | tf_op jit(solution)/shard_map/all_gather | solution.py:193
  691.0 1272.3 %all-reduce.97.cloned.1.call-start = ((), (), s32[]{:S(2)}) async-start(), calls=%async_computation.21 | async-start | bytes 33554432 | tf_op jit(solution)/shard_map/psum | solution.py:202
  1268.9 162.5 %copy-start.107 = (bf16[2048,768]{1,0:T(8,128)(2,1)S(1)}, bf16[2048,768]{1,0:T(8,128)(2,1)}, u32[]{:S(2)}) copy-start(bf16[2048,768]{1,0:T(8,128)(2,1)} %all-gather.24.cloned.1.call-done) | copy-start | bytes 9437188
  1455.4 1207.3 %reduce-scatter.32.cloned.1.call-start = ((), (), s32[]{:S(2)}) async-start(), calls=%async_computation.27 | async-start | bytes 3932160 | tf_op jit(solution)/shard_map/reduce_scatter | solution.py:300
  1468.2 1196.9 %reduce-scatter.30.cloned.1.call-start = ((), (), s32[]{:S(2)}) async-start(), calls=%async_computation.26 | async-start | bytes 3932160 | tf_op jit(solution)/shard_map/reduce_scatter | solution.py:297
  1480.9 1186.6 %reduce-scatter.34.cloned.1.call-start = ((), (), s32[]{:S(2)}) async-start(), calls=%async_computation.28 | async-start | bytes 3932160 | tf_op jit(solution)/shard_map/reduce_scatter | solution.py:303
  1493.2 1179.3 %reduce-scatter.20.cloned.1.call-start = ((), (), s32[]{:S(2)}) async-start(), calls=%async_computation.19 | async-start | bytes 9437184 | tf_op jit(solution)/shard_map/reduce_scatter | solution.py:189
  1516.0 1159.7 %reduce-scatter.36.cloned.1.call-start = ((), (), s32[]{:S(2)}) async-start(), calls=%async_computation.29 | async-start | bytes 102400
  2587.0 90.1 %reduce-scatter.38.cloned.1.call-start = ((), (), s32[]{:S(2)}) async-start(), calls=%async_computation.30 | async-start | bytes 102400
  2590.7 87.8 %reduce-scatter.40.cloned.1.call-start = ((), (), s32[]{:S(2)}) async-start(), calls=%async_computation.31 | async-start | bytes 102400
  2592.7 116.3 %all-reduce.99.cloned.1.call-start = ((), (), s32[]{:S(2)}) async-start(), calls=%async_computation.32 | async-start | bytes 655360
  2595.7 118.5 %reduce-scatter.28.cloned.1.call-start = ((), (), s32[]{:S(2)}) async-start(), calls=%async_computation.25 | async-start | bytes 1638400 | tf_op jit(solution)/shard_map/reduce_scatter | solution.py:294
  2605.9 137.4 %reduce-scatter.26.cloned.1.call-start = ((), (), s32[]{:S(2)}) async-start(), calls=%async_computation.24 | async-start | bytes 1638400 | tf_op jit(solution)/shard_map/reduce_scatter | solution.py:291
  2616.7 156.3 %reduce-scatter.24.cloned.1.call-start = ((), (), s32[]{:S(2)}) async-start(), calls=%async_computation.23 | async-start | bytes 1638400 | tf_op jit(solution)/shard_map/reduce_scatter | solution.py:288
  2616.7 5.7 collective-permute-start.1
  2631.4 294.8 %reduce-scatter.22.cloned.1.call-start = ((), (), s32[]{:S(2)}) async-start(), calls=%async_computation.22 | async-start | bytes 9437184 | tf_op jit(solution)/shard_map/reduce_scatter | solution.py:274
  (108 other events, 983.7 us)
Sparse Core Ops, SparseCore 0:
  10.2 127.6 all-gather.15
  139.4 16.3 all-gather.17
  157.4 18.1 all-gather.19
  177.1 18.3 all-gather.21
  688.3 509.7 all-reduce.94
  1199.5 27.6 all-gather.25
  1228.7 28.5 all-gather.23
  1258.8 28.5 all-gather.27
  1289.6 124.9 all-gather.29
  1455.6 507.6 all-reduce.96
  1965.8 36.9 reduce-scatter.31
  2005.4 37.9 reduce-scatter.29
  2046.0 37.9 reduce-scatter.33
  2087.9 149.0 reduce-scatter.19
  2587.1 17.8 reduce-scatter.35
  2607.9 19.4 reduce-scatter.37
  2630.2 19.4 reduce-scatter.39
  2652.5 32.4 all-reduce.98
  2687.6 26.5 reduce-scatter.27
  2716.7 26.5 reduce-scatter.25
  2746.4 26.5 reduce-scatter.23
  2777.1 149.0 reduce-scatter.21
where the time goes:
time: 3000 us; the launch traced here: 2940 us
  waiting for transfers between devices  1390 us (46%)
  local copies, waits for them, and re-layouts  937 us (31%)
  other arithmetic  264 us (9%)
  matrix products  200 us (7%)
  blocking collectives  120 us (4%)
    psum x1, waiting for transfers between devices, shards(): resid = inputs32 + lax.psum(branch_terms, 'chan')  486 us
    psum x1, waiting for transfers between devices, shards(): mid_sum = lax.psum(mid_terms, 'chan')  447 us
    pad x28, local copies, waits for them, and re-layouts, shards(): lax.associative_scan(affine_pair, (next_decay, grad_states), axis=1, reve...  438 us
    pad x28, local copies, waits for them, and re-layouts, shards(): lax.associative_scan(affine_pair, (decay, drive), axis=1)  383 us
    reduce_scatter x1, waiting for transfers between devices, shards(): lax.psum_scatter(first_terms.astype(jnp.bfloat16), 'chan', scatter_dimens...  151 us
    all_gather x1, waiting for transfers between devices, shards(): grad_full = lax.all_gather(cotangent, 'chan', axis=1, tiled=True)  127 us
    dot_general x6, matrix products, times_transpose(): lax.dot_general(left, right, (((2,), (1,)), ((), ())), preferred_element_...  71.3 us
  transfers between devices with their start and end apart: 24, of which 13 were waited for; matrix products, arithmetic and copies ran while one was open for 45% of the time, Pallas kernels for 0%

commit v1 on v0

v1 whole, which is shorter than its diff:
```python
import functools

import jax
import jax.numpy as jnp
from jax import lax
from jax.experimental import pallas as pl
from jax.experimental.pallas import tpu as pltpu
from jax.sharding import Mesh
from jax.sharding import PartitionSpec as P

BF = jnp.bfloat16
F32 = jnp.float32
BLOCKS = ("sx", "sc", "co")
PEERS = ("ca", "cb")
EVERY = ("co", "ca", "cb", "sx", "sc")
PEER = 4
GELU_C = 0.7978845608028654
GELU_K = 0.044715


def shift(value, axis, step):
    count = lax.axis_size(axis)
    return lax.ppermute(value, axis, [(i, (i + step) % count) for i in range(count)])


def peer(value, step):
    return lax.ppermute(value, PEERS, [(i, i ^ step) for i in range(PEER)])


def block_shift(value, step):
    count = lax.axis_size(BLOCKS)
    route = [(i, i + step) for i in range(count) if 0 <= i + step < count]
    return lax.ppermute(value, BLOCKS, route)


def chunk_roll(value, step):
    count = lax.axis_size("co")
    step = step % count
    if step == 0:
        return value
    width = value.shape[-1] // count
    cut = width * (count - step)
    return jnp.concatenate([value[..., cut:], value[..., :cut]], axis=-1)


def feature_order(value):
    nsx, nsc = lax.axis_size("sx"), lax.axis_size("sc")
    sx, sc = lax.axis_index("sx"), lax.axis_index("sc")
    width = value.shape[-1] // (nsx * nsc)
    parts = []
    for rc in range(nsc):
        for rx in range(nsx):
            owner = lax.rem(sx - rx + nsx, nsx) * nsc + lax.rem(sc - rc + nsc, nsc)
            parts.append(lax.dynamic_slice_in_dim(value, owner * width, width, value.ndim - 1))
    return jnp.concatenate(parts, axis=-1)


def feature_restore(value):
    nsx, nsc = lax.axis_size("sx"), lax.axis_size("sc")
    sx, sc = lax.axis_index("sx"), lax.axis_index("sc")
    width = value.shape[-1] // (nsx * nsc)
    parts = []
    for owner in range(nsx * nsc):
        rx = lax.rem(sx - owner // nsc + nsx, nsx)
        rc = lax.rem(sc - owner % nsc + nsc, nsc)
        parts.append(
            lax.dynamic_slice_in_dim(value, (rc * nsx + rx) * width, width, value.ndim - 1)
        )
    return jnp.concatenate(parts, axis=-1)


def chunk_order(value, axis):
    count, mine = lax.axis_size("co"), lax.axis_index("co")
    return jnp.concatenate(
        [
            lax.dynamic_slice_in_dim(value, lax.rem(mine - r + count, count), 1, axis)
            for r in range(count)
        ],
        axis=axis,
    )


def gather_weight(shard, join):
    held = join([shard] + [shift(shard, "co", r) for r in range(1, lax.axis_size("co"))])
    rows = [held] + [shift(held, "sx", r) for r in range(1, lax.axis_size("sx"))]
    return rows + [shift(item, "sc", 1) for item in rows]


def scatter_weight(grad, cut, axis):
    nsx = lax.axis_size("sx")
    half = grad.shape[axis] // 2
    mine = lax.slice_in_dim(grad, 0, half, axis=axis).astype(F32)
    mine = mine + shift(lax.slice_in_dim(grad, half, 2 * half, axis=axis), "sc", -1).astype(F32)
    width = half // nsx
    total = lax.slice_in_dim(mine, 0, width, axis=axis)
    for r in range(1, nsx):
        part = lax.slice_in_dim(mine, r * width, (r + 1) * width, axis=axis).astype(BF)
        total = total + shift(part, "sx", -r).astype(F32)
    parts = cut(total)
    total = parts[0]
    for r in range(1, len(parts)):
        total = total + shift(parts[r].astype(BF), "co", -r).astype(F32)
    return total


def matmul(left, right):
    return jnp.dot(left, right, preferred_element_type=F32)


def over_tokens(left, right):
    return lax.dot_general(left, right, (((0,), (0,)), ((), ())), preferred_element_type=F32)


def times_transpose(left, right):
    return lax.dot_general(left, right, (((1,), (1,)), ((), ())), preferred_element_type=F32)


def collect(value):
    return [value] + [peer(value, k) for k in range(1, PEER)]


def hand_back(pieces):
    total = pieces[0]
    for k in range(1, PEER):
        total = total + peer(pieces[k].astype(BF), k).astype(F32)
    return total


def gelu_parts(value):
    square = value * value
    wave = jnp.tanh(GELU_C * (value + GELU_K * value * square))
    half = 0.5 * (1.0 + wave)
    slope = half + 0.5 * value * (1.0 - wave * wave) * (GELU_C * (1.0 + 3.0 * GELU_K * square))
    return value * half, slope


def minus_expm1(value):
    series = 1.0 + value * (1.0 / 7.0)
    for order in (6.0, 5.0, 4.0, 3.0, 2.0):
        series = 1.0 + value * (1.0 / order) * series
    return -jnp.where(value > -0.3, value * series, jnp.exp(value) - 1.0)


def decay_terms(rate, soft):
    log_decay = -8.0 * rate * soft
    return jnp.exp(log_decay), jnp.sqrt(minus_expm1(2.0 * log_decay))


def gates_kernel(
    ci, u_ref, edge_ref, gate_ref, vec_ref, v_ref, ra_ref, ri_ref, a_ref, e_ref, before_ref, end_ref,
    pad, held,
):
    step = pl.program_id(0)
    rows = held.shape[0] // 2
    size = u_ref.shape[0]
    lag = edge_ref.shape[0]
    width = u_ref.shape[1]

    @pl.when(step == 0)
    def _():
        pad[0:lag, :] = edge_ref[...].astype(F32)
        held[0:rows, :] = jnp.ones((rows, width), F32)
        held[rows:, :] = jnp.zeros((rows, width), F32)

    @pl.when(step > 0)
    def _():
        pad[0:lag, :] = pad[size : size + lag, :]

    pad[lag:, :] = u_ref[...].astype(BF).astype(F32)
    before_ref[...] = pad[0:lag, :]
    taps = lag // rows + 1
    conv = vec_ref[taps : taps + 1, :] + vec_ref[0:1, :] * pad[lag : lag + size, :]
    for k in range(1, taps):
        conv = conv + vec_ref[k : k + 1, :] * pad[lag - rows * k : lag - rows * k + size, :]
    low = conv.astype(BF)
    v_ref[...] = low
    pre = jnp.dot(low, gate_ref[...], preferred_element_type=F32)
    ra = jax.nn.sigmoid(pre[:, :width] + vec_ref[taps + 1 : taps + 2, :])
    ri = jax.nn.sigmoid(pre[:, width:] + vec_ref[taps + 2 : taps + 3, :])
    decay, root = decay_terms(ra, vec_ref[taps + 3 : taps + 4, :])
    ra_ref[...] = ra
    ri_ref[...] = ri
    a_ref[...] = decay
    e_ref[...] = low.astype(F32) * ri * root
    prod = held[0:rows, :]
    state = held[rows:, :]
    for t in range(size // rows):
        now = a_ref[t * rows : (t + 1) * rows, :]
        state = now * state + e_ref[t * rows : (t + 1) * rows, :]
        prod = prod * now
    held[0:rows, :] = prod
    held[rows:, :] = state
    end_ref[0:rows, :] = prod
    end_ref[rows:, :] = state


def states_kernel(ci, a_ref, e_ref, yp_ref, enter_ref, h_ref, z_ref, before_ref, end_ref, held):
    step = pl.program_id(0)
    rows = held.shape[0]

    @pl.when(step == 0)
    def _():
        held[...] = enter_ref[...]

    state = held[...]
    before_ref[...] = state
    for t in range(a_ref.shape[0] // rows):
        at = slice(t * rows, (t + 1) * rows)
        state = a_ref[at, :] * state + e_ref[at, :]
        h_ref[at, :] = state
    held[...] = state
    end_ref[...] = state
    act, _ = gelu_parts(yp_ref[...])
    z_ref[...] = (h_ref[...] * act).astype(BF)


def back_kernel(ci, dz_ref, yp_ref, h_ref, a_ref, dh_ref, dyp_ref, end_ref, held):
    step = pl.program_id(0)
    rows = held.shape[0]

    @pl.when(step == 0)
    def _():
        held[...] = jnp.zeros(held.shape, F32)

    act, slope = gelu_parts(yp_ref[...])
    dz = dz_ref[...]
    dh_ref[...] = dz * act
    dyp_ref[...] = (dz * h_ref[...] * slope).astype(BF)
    carry = held[...]
    for t in reversed(range(a_ref.shape[0] // rows)):
        at = slice(t * rows, (t + 1) * rows)
        carry = a_ref[at, :] * (dh_ref[at, :] + carry)
    held[...] = carry
    end_ref[...] = carry


def grads_kernel(
    ci, dh_ref, a_ref, ra_ref, ri_ref, v_ref, h_ref, hb_ref, u_ref, ub_ref, gate_ref, vec_ref,
    late_ref, gates_ref, du_ref, edge_ref, last_ref, sums_ref, end_ref, held, pad, spad, hpad, upad,
):
    step = pl.program_id(0)
    rows = held.shape[0]
    size = dh_ref.shape[0]
    width = dh_ref.shape[1]
    lag = ub_ref.shape[0]
    taps = lag // rows + 1

    @pl.when(step == 0)
    def _():
        held[...] = late_ref[...]
        pad[size:, :] = jnp.zeros((lag, width), F32)
        sums_ref[...] = jnp.zeros(sums_ref.shape, F32)

    @pl.when(step > 0)
    def _():
        pad[size:, :] = pad[0:lag, :]

    carry = held[...]
    for t in reversed(range(size // rows)):
        at = slice(t * rows, (t + 1) * rows)
        now = dh_ref[at, :] + carry
        spad[at, :] = now
        carry = a_ref[at, :] * now
    held[...] = carry
    end_ref[...] = carry
    hpad[0:rows, :] = hb_ref[...]
    hpad[rows:, :] = h_ref[...]
    upad[0:lag, :] = ub_ref[...]
    upad[lag:, :] = u_ref[...].astype(BF).astype(F32)
    s = spad[...]
    ra = ra_ref[...]
    ri = ri_ref[...]
    soft = vec_ref[taps + 3 : taps + 4, :]
    decay, root = decay_terms(ra, soft)
    v = v_ref[...].astype(F32)
    sv = s * v
    grad_log = decay * (s * hpad[0:size, :] - sv * ri * decay / root)
    rated = grad_log * ra
    dap = (-8.0 * soft * rated * (1.0 - ra)).astype(BF)
    dip = (sv * root * ri * (1.0 - ri)).astype(BF)
    gates_ref[:, :width] = dap
    gates_ref[:, width:] = dip
    dv = s * ri * root + lax.dot_general(
        gates_ref[...], gate_ref[...], (((1,), (1,)), ((), ())), preferred_element_type=F32
    )
    pad[0:size, :] = dv

    def fold(value):
        return jnp.sum(value.reshape(size // rows, rows, width), axis=0)

    terms = [dap.astype(F32), dip.astype(F32), rated, dv]
    terms = terms + [dv * upad[lag - rows * k : lag - rows * k + size, :] for k in range(taps)]
    for i, term in enumerate(terms):
        sums_ref[i * rows : (i + 1) * rows, :] += fold(term)
    du = vec_ref[0:1, :] * dv
    for k in range(1, taps):
        du = du + vec_ref[k : k + 1, :] * pad[rows * k : rows * k + size, :]
    du_ref[...] = du.astype(BF)

    @pl.when(step == 0)
    def _():
        last_ref[...] = du[size - lag :, :]

    for t in range(taps - 1):
        row = jnp.zeros((rows, width), F32)
        for k in range(taps - 1 - t, taps):
            at = (t + k - (taps - 1)) * rows
            row = row + vec_ref[k : k + 1, :] * pad[at : at + rows, :]
        edge_ref[t * rows : (t + 1) * rows, :] = row


def gates_call(ci, uy, edge, gate, vec, rows):
    steps, size, wide = uy.shape
    width = wide // 2
    lag = edge.shape[0]
    here = pl.BlockSpec((None, size, width), lambda j, c: (j, 0, 0))
    whole = lambda shape: pl.BlockSpec(shape, lambda j, c: (0,) * len(shape))
    full = jax.ShapeDtypeStruct((steps, size, width), F32)
    return pl.pallas_call(
        gates_kernel,
        out_shape=(
            jax.ShapeDtypeStruct((steps, size, width), BF),
            full,
            full,
            full,
            full,
            jax.ShapeDtypeStruct((steps, lag, width), F32),
            jax.ShapeDtypeStruct((2 * rows, width), F32),
        ),
        grid_spec=pltpu.PrefetchScalarGridSpec(
            num_scalar_prefetch=1,
            grid=(steps,),
            in_specs=[
                pl.BlockSpec((None, size, width), lambda j, c: (j ^ c[0], 0, 0)),
                whole(edge.shape),
                whole(gate.shape),
                whole(vec.shape),
            ],
            out_specs=[
                here,
                here,
                here,
                here,
                here,
                pl.BlockSpec((None, lag, width), lambda j, c: (j, 0, 0)),
                whole((2 * rows, width)),
            ],
            scratch_shapes=[
                pltpu.VMEM((size + lag, width), F32),
                pltpu.VMEM((2 * rows, width), F32),
            ],
        ),
        name="gates",
    )(ci, uy, edge, gate, vec)


def states_call(ci, a, e, uy, enter):
    steps, size, width = a.shape
    rows = enter.shape[0]
    here = pl.BlockSpec((None, size, width), lambda j, c: (j, 0, 0))
    whole = pl.BlockSpec((rows, width), lambda j, c: (0, 0))
    return pl.pallas_call(
        states_kernel,
        out_shape=(
            jax.ShapeDtypeStruct((steps, size, width), F32),
            jax.ShapeDtypeStruct((steps, size, width), BF),
            jax.ShapeDtypeStruct((steps, rows, width), F32),
            jax.ShapeDtypeStruct((rows, width), F32),
        ),
        grid_spec=pltpu.PrefetchScalarGridSpec(
            num_scalar_prefetch=1,
            grid=(steps,),
            in_specs=[
                here,
                here,
                pl.BlockSpec((None, size, width), lambda j, c: (j ^ c[0], 0, 1)),
                whole,
            ],
            out_specs=[
                here,
                pl.BlockSpec((None, size, width), lambda j, c: (j ^ c[0], 0, 0)),
                pl.BlockSpec((None, rows, width), lambda j, c: (j, 0, 0)),
                whole,
            ],
            scratch_shapes=[pltpu.VMEM((rows, width), F32)],
        ),
        name="states",
    )(ci, a, e, uy, enter)


def back_call(ci, dz, uy, h, a, rows):
    steps, size, width = a.shape
    last = steps - 1
    here = pl.BlockSpec((None, size, width), lambda j, c: (last - j, 0, 0))
    there = pl.BlockSpec((None, size, width), lambda j, c: ((last - j) ^ c[0], 0, 0))
    return pl.pallas_call(
        back_kernel,
        out_shape=(
            jax.ShapeDtypeStruct((steps, size, width), F32),
            jax.ShapeDtypeStruct((steps, size, width), BF),
            jax.ShapeDtypeStruct((rows, width), F32),
        ),
        grid_spec=pltpu.PrefetchScalarGridSpec(
            num_scalar_prefetch=1,
            grid=(steps,),
            in_specs=[
                there,
                pl.BlockSpec((None, size, width), lambda j, c: ((last - j) ^ c[0], 0, 1)),
                here,
                here,
            ],
            out_specs=[here, there, pl.BlockSpec((rows, width), lambda j, c: (0, 0))],
            scratch_shapes=[pltpu.VMEM((rows, width), F32)],
        ),
        name="back",
    )(ci, dz, uy, h, a)


def grads_call(ci, dh, a, ra, ri, v, h, h_before, uy, u_before, gate, vec, late):
    steps, size, width = a.shape
    rows = late.shape[0]
    lag = u_before.shape[1]
    last = steps - 1
    count = lag // rows + 5
    here = pl.BlockSpec((None, size, width), lambda j, c: (last - j, 0, 0))
    there = pl.BlockSpec((None, size, width), lambda j, c: ((last - j) ^ c[0], 0, 0))
    small = lambda size: pl.BlockSpec((None, size, width), lambda j, c: (last - j, 0, 0))
    whole = lambda shape: pl.BlockSpec(shape, lambda j, c: (0,) * len(shape))
    return pl.pallas_call(
        grads_kernel,
        out_shape=(
            jax.ShapeDtypeStruct((steps, size, 2 * width), BF),
            jax.ShapeDtypeStruct((steps, size, width), BF),
            jax.ShapeDtypeStruct((lag, width), F32),
            jax.ShapeDtypeStruct((lag, width), F32),
            jax.ShapeDtypeStruct((count * rows, width), F32),
            jax.ShapeDtypeStruct((rows, width), F32),
        ),
        grid_spec=pltpu.PrefetchScalarGridSpec(
            num_scalar_prefetch=1,
            grid=(steps,),
            in_specs=[
                here,
                here,
                here,
                here,
                here,
                here,
                small(rows),
                there,
                small(lag),
                whole(gate.shape),
                whole(vec.shape),
                whole(late.shape),
            ],
            out_specs=[
                pl.BlockSpec((None, size, 2 * width), lambda j, c: (last - j, 0, 0)),
                there,
                whole((lag, width)),
                whole((lag, width)),
                whole((count * rows, width)),
                whole((rows, width)),
            ],
            scratch_shapes=[
                pltpu.VMEM((rows, width), F32),
                pltpu.VMEM((size + lag, width), F32),
                pltpu.VMEM((size, width), F32),
                pltpu.VMEM((size + rows, width), F32),
                pltpu.VMEM((size + lag, width), F32),
            ],
        ),
        name="grads",
    )(ci, dh, a, ra, ri, v, h, h_before, uy, u_before, gate, vec, late)


def norm_back(grad_norm, normed, inv_root, gain):
    scaled = grad_norm * gain
    mean_term = jnp.mean(scaled * normed, axis=-1, keepdims=True)
    return inv_root * (scaled - normed * mean_term)


def inverse_rms(value):
    return lax.rsqrt(jnp.mean(value * value, axis=-1, keepdims=True) + 1e-06)


def shards(
    tokens,
    norm_gain,
    mlp_gain,
    recur_proj,
    branch_proj,
    out_proj,
    gate_proj,
    up_proj,
    down_proj,
    recur_gate,
    input_gate,
    recur_bias,
    input_bias,
    decay_param,
    conv_bias,
    conv_weight,
    init_state,
    init_tail,
    reset_flags,
    cotangent,
):
    nsx, nsc, nco = (lax.axis_size(name) for name in BLOCKS)
    nseq = nsx * nsc
    blocks = nseq * nco
    co = lax.axis_index("co")
    block = lax.axis_index(BLOCKS)
    first = block == 0
    ci = lax.axis_index(PEERS)
    order = ci.astype(jnp.int32).reshape(1)
    rows, share, model = tokens.shape
    own = rows * share
    taps = conv_weight.shape[0]
    lag = taps - 1
    part = conv_bias.shape[0]
    chunk = part * nseq
    width = chunk * nco
    keep = (1 - reset_flags).astype(F32)[:, None]

    def owned(value):
        return feature_order(jnp.swapaxes(value, 0, 1).reshape(own, model))

    gains = lax.all_gather(jnp.stack([norm_gain, mlp_gain]), EVERY, axis=0)
    gains = feature_order(jnp.swapaxes(gains, 0, 1).reshape(2, model).astype(F32))
    gain_one, gain_two = (gains[0:1], gains[1:2])
    vectors = jnp.concatenate(
        [
            conv_weight,
            conv_bias[None],
            recur_bias[None],
            input_bias[None],
            decay_param[None],
            init_state,
            jnp.swapaxes(init_tail, 0, 1).reshape(lag * rows, part),
        ],
        axis=0,
    )
    vectors = lax.all_gather(vectors, BLOCKS, axis=0)
    vectors = jnp.transpose(vectors.reshape(nseq, nco, -1, part), (2, 1, 0, 3))
    vectors = chunk_order(vectors, 1).reshape(-1, width).astype(F32)
    decay32 = vectors[taps + 3 : taps + 4]
    vec = jnp.concatenate([vectors[: taps + 3], jax.nn.softplus(-decay32)], axis=0)
    vec = jnp.pad(vec, ((0, -vec.shape[0] % 8), (0, 0)))
    state_start = vectors[taps + 4 : taps + 4 + rows] * keep
    tail_start = vectors[taps + 4 + rows :] * jnp.tile(keep, (lag, 1))
    both = jnp.stack([recur_gate, input_gate])
    heads, span = both.shape[1], both.shape[3]
    both = lax.all_gather(both, BLOCKS, axis=0).reshape(nseq, nco, 2, heads, -1, span)
    both = chunk_order(jnp.transpose(both, (2, 1, 3, 0, 4, 5)), 1)
    both = both.reshape(2, nco * heads, span, span)
    gate = jnp.concatenate(
        [
            jnp.concatenate(
                [
                    jnp.pad(both[g, h], ((0, 0), (span * h, width - span * (h + 1))))
                    for h in range(nco * heads)
                ],
                axis=0,
            )
            for g in range(2)
        ],
        axis=1,
    )

    def sides(items):
        half = items[0].shape[1] // 2
        return jnp.concatenate(
            [item[:, :half] for item in items] + [item[:, half:] for item in items], axis=1
        )

    def stacked(items):
        return jnp.concatenate(items, axis=0)

    mine = owned(tokens)
    group = collect(mine)
    full_in = jnp.concatenate(
        gather_weight(jnp.concatenate([recur_proj, branch_proj], axis=1), sides), axis=0
    )
    full_out = jnp.concatenate(gather_weight(out_proj, stacked), axis=1)
    mlp_parts = gather_weight(jnp.concatenate([gate_proj, up_proj], axis=1), sides)
    inner = mlp_parts[0].shape[1] // 2
    full_gate = jnp.concatenate([item[:, :inner] for item in mlp_parts], axis=0)
    full_up = jnp.concatenate([item[:, inner:] for item in mlp_parts], axis=0)
    full_down = jnp.concatenate(gather_weight(down_proj, stacked), axis=1)
    grad_mine = owned(cotangent)
    grad_full = jnp.concatenate(collect(grad_mine), axis=0)

    def normal(piece):
        value = piece.astype(F32)
        return (value * inverse_rms(value) * gain_one).astype(BF)

    normal_in = jnp.concatenate([normal(piece) for piece in group], axis=0)
    uy = matmul(normal_in, full_in).reshape(PEER, own, 2 * width)

    edge_at = (lax.bitwise_xor(jnp.int32(PEER - 1), ci.astype(jnp.int32)), own - lag * rows, 0)
    ends = lax.dynamic_slice(uy, edge_at, (1, lag * rows, width))[0].astype(BF)
    edge = jnp.where(first, tail_start.astype(BF), chunk_roll(block_shift(ends, 1), 1))
    v, ra, ri, decay, drive, u_before, summary = gates_call(order, uy, edge, gate, vec, rows)
    enter = state_start
    for k in reversed(range(1, blocks)):
        other = chunk_roll(block_shift(summary, k), k)
        enter = jnp.where(block >= k, other[:rows] * enter + other[rows:], enter)
    h, z, h_before, h_end = states_call(order, decay, drive, uy, enter)
    branch = matmul(z.reshape(PEER * own, width), full_out).reshape(PEER, own, model)
    resid = mine.astype(F32) + hand_back([branch[k] for k in range(PEER)])

    inv_two = inverse_rms(resid)
    normed_two = resid * inv_two
    normal_mine = (normed_two * gain_two).astype(BF)
    normal_mid = jnp.concatenate(collect(normal_mine), axis=0)
    gate_pre = matmul(normal_mid, full_gate)
    up_pre = matmul(normal_mid, full_up)
    gate_act, gate_slope = gelu_parts(gate_pre)
    hidden = (gate_act * up_pre).astype(BF)
    mlp = matmul(hidden, full_down).astype(BF).reshape(PEER, own, model)
    mlp_sum = hand_back([mlp[k].astype(F32) for k in range(PEER)])
    mixed = (resid + mlp_sum).astype(BF)

    grad_hidden = times_transpose(grad_full, full_down)
    grad_gate = (grad_hidden * up_pre * gate_slope).astype(BF)
    grad_up = (grad_hidden * gate_act).astype(BF)
    mid = times_transpose(grad_gate, full_gate) + times_transpose(grad_up, full_up)
    mid = mid.reshape(PEER, own, model)
    mid_sum = hand_back([mid[k] for k in range(PEER)])
    gain_two_part = jnp.sum(mid_sum * normed_two, axis=0)
    resid_grad = grad_mine.astype(F32) + norm_back(mid_sum, normed_two, inv_two, gain_two)
    resid_low = jnp.concatenate(collect(resid_grad.astype(BF)), axis=0)
    down_grad = over_tokens(hidden, grad_full).astype(BF)
    gate_grad = over_tokens(normal_mid, grad_gate).astype(BF)
    up_grad = over_tokens(normal_mid, grad_up).astype(BF)

    out_grad = over_tokens(z.reshape(PEER * own, width), resid_low).astype(BF)
    dz = times_transpose(resid_low, full_out).reshape(PEER, own, width)
    dh, grad_branch, local_end = back_call(order, dz, uy, h, decay, rows)
    message = jnp.concatenate([summary[:rows], local_end], axis=0)
    late = jnp.zeros((rows, width), F32)
    for k in reversed(range(1, blocks)):
        other = chunk_roll(block_shift(message, -k), -k)
        late = jnp.where(block + k < blocks, other[:rows] * late + other[rows:], late)
    gates_low, grad_u, edge_out, last, sums, start_grad = grads_call(
        order, dh, decay, ra, ri, v, h, h_before, uy, u_before, gate, vec, late
    )
    edge_in = chunk_roll(block_shift(edge_out, -1), -1)
    grad_u = lax.dynamic_update_slice(grad_u, (last + edge_in).astype(BF)[None], edge_at)
    grad_u = grad_u.reshape(PEER * own, width)
    grad_branch = grad_branch.reshape(PEER * own, width)
    recur_grad = over_tokens(normal_in, grad_u).astype(BF)
    branch_grad = over_tokens(normal_in, grad_branch).astype(BF)
    both_grad = over_tokens(v.reshape(PEER * own, width), gates_low.reshape(PEER * own, 2 * width))
    back_terms = times_transpose(grad_u, full_in[:, :width]) + times_transpose(
        grad_branch, full_in[:, width:]
    )
    back_terms = back_terms.reshape(PEER, own, model)
    back_sum = hand_back([back_terms[k] for k in range(PEER)])
    value = mine.astype(F32)
    inv_one = inverse_rms(value)
    normed_one = value * inv_one
    gain_one_part = jnp.sum(back_sum * normed_one, axis=0)
    tokens_grad = resid_grad + norm_back(back_sum, normed_one, inv_one, gain_one)

    def right(total):
        half = total.shape[1] // nco
        return [total[:, r * half : (r + 1) * half] for r in range(nco)]

    def low(total):
        half = total.shape[0] // nco
        return [total[r * half : (r + 1) * half] for r in range(nco)]

    recur_out = scatter_weight(recur_grad, right, 0)
    branch_out = scatter_weight(branch_grad, right, 0)
    out_out = scatter_weight(out_grad, low, 1)
    gate_out = scatter_weight(gate_grad, right, 0)
    up_out = scatter_weight(up_grad, right, 0)
    down_out = scatter_weight(down_grad, low, 1)

    pieces = jnp.stack(
        [
            both_grad[span * h : span * (h + 1), g * width + span * h : g * width + span * (h + 1)]
            for g in range(2)
            for h in range(nco * heads)
        ]
    )
    pieces = chunk_order(pieces.reshape(2, nco, heads, nseq, -1, span), 1)
    pieces = jnp.transpose(pieces, (3, 1, 0, 2, 4, 5)).reshape(blocks, 2, heads, -1, span)
    both_out = lax.psum_scatter(
        pieces.astype(BF), BLOCKS, scatter_dimension=0, tiled=True
    )[0].astype(F32)

    sums = jnp.sum(sums.reshape(-1, rows, width), axis=1)
    small = jnp.concatenate(
        [
            sums[0:2],
            sums[2:3] * 8.0 * jax.nn.sigmoid(-decay32),
            sums[3:],
            jnp.where(first, keep * start_grad, 0.0),
            jnp.where(first, jnp.tile(keep, (lag, 1)) * edge_out, 0.0),
        ],
        axis=0,
    )
    small = chunk_order(small.reshape(-1, nco, nseq, part), 1)
    small = jnp.transpose(small, (2, 1, 0, 3)).reshape(blocks, -1, part)
    small = lax.psum_scatter(small, BLOCKS, scatter_dimension=0, tiled=True)[0]

    gain_parts = feature_restore(jnp.stack([gain_one_part, gain_two_part]))
    gain_parts = jnp.swapaxes(gain_parts.reshape(2, -1, norm_gain.shape[0]), 0, 1)
    gain_out = lax.psum_scatter(gain_parts, EVERY, scatter_dimension=0, tiled=True)[0]

    finish = jnp.concatenate([h_end, ends.astype(F32)], axis=0)
    reach = jnp.where(co == nco - 1, finish[:, :chunk], 0.0)
    for k in range(1, nco):
        piece = finish[:, (nco - k) * chunk : (nco - k + 1) * chunk]
        reach = reach + lax.ppermute(piece, "co", [(nco - 1, k - 1)])
    group_states = reach[:rows][None]
    group_tails = jnp.swapaxes(reach[rows:].reshape(lag, rows, chunk), 0, 1).astype(BF)[None]

    def returned(value):
        return jnp.swapaxes(feature_restore(value).reshape(share, rows, model), 0, 1)

    return (
        returned(mixed),
        returned(tokens_grad),
        gain_out[0],
        gain_out[1],
        recur_out,
        branch_out,
        out_out,
        gate_out,
        up_out,
        down_out,
        both_out[0],
        both_out[1],
        small[0],
        small[1],
        small[2],
        small[3],
        small[4 : 4 + taps],
        small[4 + taps : 4 + taps + rows],
        jnp.swapaxes(small[4 + taps + rows :].reshape(lag, rows, part), 0, 1),
        group_states,
        group_tails,
    )


def solution(mesh):
    nseq, nchan = mesh.devices.shape
    fine = Mesh(
        mesh.devices.reshape(nseq // 2, 2, nchan // PEER, 2, 2), ("sx", "sc", "co", "ca", "cb")
    )
    seq = ("sx", "sc")
    chan = ("co", "ca", "cb")
    place = P(None, seq + chan, None)
    vector = P(chan + seq)
    in_specs = (
        place,
        vector,
        vector,
        P(seq, chan),
        P(seq, chan),
        P(chan, seq),
        P(seq, chan),
        P(seq, chan),
        P(chan, seq),
        P(chan, seq, None),
        P(chan, seq, None),
        vector,
        vector,
        vector,
        vector,
        P(None, chan + seq),
        P(None, chan + seq),
        P(None, None, chan + seq),
        P(),
        place,
    )
    out_specs = (
        place,
        place,
        vector,
        vector,
        P(seq, chan),
        P(seq, chan),
        P(chan, seq),
        P(seq, chan),
        P(seq, chan),
        P(chan, seq),
        P(chan, seq, None),
        P(chan, seq, None),
        vector,
        vector,
        vector,
        vector,
        P(None, chan + seq),
        P(None, chan + seq),
        P(None, None, chan + seq),
        P(seq, None, chan),
        P(seq, None, None, chan),
    )
    return jax.shard_map(shards, mesh=fine, in_specs=in_specs, out_specs=out_specs, check_vma=False)
```

time: 3000 us -> 1270 us (0.42); the launches traced: 2940 us -> 1260 us
  local copies, waits for them, and re-layouts: 937 us -> 80.6 us
  waiting for transfers between devices: 1390 us -> 538 us
  other arithmetic: 264 us -> 94.6 us
  blocking collectives: 120 us -> 219 us
  starting transfers between devices: 4.31 us -> 93.6 us
  Pallas kernels: 0 us -> 37.5 us
    psum x2 -> x0, waiting for transfers between devices: 933 us -> none  [the longest x1 486 us: shards(): resid = inputs32 + lax.psum(branch_terms, 'chan')]
    pad x56 -> x0, local copies, waits for them, and re-layouts: 821 us -> none  [the longest x28 438 us: shards(): lax.associative_scan(affine_pair, (next_decay, grad_states), axis=1, reve...]
    ppermute x2 -> x75, waiting for transfers between devices: 0.01 us -> 463 us  [the longest x34 221 us: shift(): lax.ppermute(value, axis, [(i, (i + step) % count) for i in range(count)])]
    all_gather x8 -> x0, waiting for transfers between devices: 247 us -> none  [the longest x1 127 us: shards(): grad_full = lax.all_gather(cotangent, 'chan', axis=1, tiled=True)]
    reduce_scatter x8 -> x1, waiting for transfers between devices: 209 us -> 32.2 us  [shards(): lax.psum_scatter(pieces.astype(BF), BLOCKS, scatter_dimension=0, tiled=True)]
    ppermute x2 -> x75, starting transfers between devices: 3.42 us -> 93.4 us  [the longest x34 34.3 us: shift(): lax.ppermute(value, axis, [(i, (i + step) % count) for i in range(count)])]
    add x49 -> x20, other arithmetic: 94.2 us -> 30.4 us  [the longest x6 17.5 us: scatter_weight(): mine + shift(lax.slice_in_dim(grad, half, 2 * half, axis=axis), 'sc', -1)...]
    all_gather x10 -> x3, blocking collectives: 86 us -> 146 us  [the longest x1 77.7 us: shards(): vectors = lax.all_gather(vectors, BLOCKS, axis=0)]
  transfers between devices with their start and end apart: 24 -> 77, of which waited for: 13 -> 34; matrix products, arithmetic and copies ran while one was open for 45% -> 22% of each run, Pallas kernels for 0% -> 3%
where the time goes in v1:
time: 1270 us; the launch traced here: 1260 us
  waiting for transfers between devices  538 us (42%)
  blocking collectives  219 us (17%)
  matrix products  179 us (14%)
  other arithmetic  94.6 us (7%)
  starting transfers between devices  93.6 us (7%)
  local copies, waits for them, and re-layouts  80.6 us (6%)
  Pallas kernels  37.5 us (3%)
  between operations  16.6 us (1%)
    ppermute x34, waiting for transfers between devices, shift(): lax.ppermute(value, axis, [(i, (i + step) % count) for i in range(count)])  221 us
    ppermute x24, waiting for transfers between devices, peer(): return lax.ppermute(value, PEERS, [(i, i ^ step) for i in range(PEER)])  182 us
    dot_general x6, matrix products, times_transpose(): lax.dot_general(left, right, (((1,), (1,)), ((), ())), preferred_element_...  79.8 us
    all_gather x1, blocking collectives, shards(): vectors = lax.all_gather(vectors, BLOCKS, axis=0)  77.7 us
    unnamed x1, blocking collectives  73.1 us
    ppermute x16, waiting for transfers between devices, block_shift(): return lax.ppermute(value, BLOCKS, route)  59.3 us
    dot_general x7, matrix products, over_tokens(): lax.dot_general(left, right, (((0,), (0,)), ((), ())), preferred_element_...  49.9 us
    dot_general x5, matrix products, matmul(): return jnp.dot(left, right, preferred_element_type=F32)  49.2 us
  transfers between devices with their start and end apart: 77, of which 34 were waited for; matrix products, arithmetic and copies ran while one was open for 22% of the time, Pallas kernels for 3%

profile of v1, /device:TPU:0, one launch (start us, length us, event | category | flops | bytes accessed | tf_op | source)
XLA Modules:
  0.0 1259.0 jit_solution(5896552461831913407)
XLA Ops:
  21.5 77.7 %all-gather.1 = bf16[320,80]{1,0:T(8,128)(2,1)S(1)} all-gather(bf16[40,80]{1,0:T(8,128)(2,1)} %concatenate.142), channel_id=3, replica_groups=mesh['sx'=2,'sc'=2,'co'=2,'ca'=2,'cb'=2] {'sx','sc','co'}, dimensions={0}, use_global_device_ids=true | all-gather | bytes 57600 | tf_op jit(solution)/shard_map/all_gather | solution.py:543
  103.6 39.4 %all-gather.3 = bf16[32,2,64]{2,1,0:T(2,128)(2,1)S(1)} all-gather(bf16[1,2,64]{2,1,0:T(2,128)(2,1)S(1)} %maximum_bitcast_fusion.4), channel_id=2, replica_groups=mesh['sx'=2,'sc'=2,'co'=2,'ca'=2,'cb'=2] {'co','ca','cb','sx','sc'}, dimensions={0}, use_global_device_ids=true | all-gather | bytes 8448 | tf_op jit(solution)/shard_map/all_gather | solution.py:528
  152.7 28.5 %all-gather.2 = bf16[16,2,40,160]{3,2,1,0:T(8,128)(2,1)S(1)} all-gather(bf16[2,2,40,160]{3,2,1,0:T(8,128)(2,1)S(1)} %pad_maximum_fusion.22), channel_id=4, replica_groups=mesh['sx'=2,'sc'=2,'co'=2,'ca'=2,'cb'=2] {'sx','sc','co'}, dimensions={0}, use_global_device_ids=true | all-gather | bytes 460800 | tf_op jit(solution)/shard_map/all_gather | solution.py:553
  212.7 16.2 %collective-permute-done.4 = bf16[512,1280]{0,1:T(8,128)(2,1)} collective-permute-done((bf16[512,1280]{0,1:T(8,128)(2,1)}, bf16[512,1280]{0,1:T(8,128)(2,1)}, u32[]{:S(2)}, u32[]{:S(2)}) %collective-permute-start.4) | collective-permute-done | bytes 1310752 | tf_op jit(solution)/shard_map/ppermute | solution.py:23
  234.6 38.9 %collective-permute-done.25 = bf16[512,1536]{1,0:T(8,128)(2,1)S(1)} collective-permute-done((bf16[512,1536]{1,0:T(8,128)(2,1)}, bf16[512,1536]{1,0:T(8,128)(2,1)S(1)}, u32[]{:S(2)}, u32[]{:S(2)}) %collective-permute-start.25) | collective-permute-done | bytes 1572896 | tf_op jit(solution)/shard_map/ppermute | solution.py:23
  273.7 12.0 pad_maximum_fusion.3
  329.4 41.2 %collective-permute-done.13 = f32[16,640]{1,0:T(8,128)S(1)} collective-permute-done((f32[16,640]{1,0:T(8,128)}, f32[16,640]{1,0:T(8,128)S(1)}, u32[]{:S(2)}, u32[]{:S(2)}) %collective-permute-start.13) | collective-permute-done | bytes 40992 | tf_op jit(solution)/shard_map/ppermute | solution.py:33
  395.6 19.9 %collective-permute-done.29 = bf16[768,512]{1,0:T(8,128)(2,1)} collective-permute-done((bf16[768,512]{1,0:T(8,128)(2,1)}, bf16[768,512]{1,0:T(8,128)(2,1)}, u32[]{:S(2)}, u32[]{:S(2)}) %collective-permute-start.29) | collective-permute-done | bytes 786464 | tf_op jit(solution)/shard_map/ppermute | solution.py:23
  423.7 18.0 %collective-permute-done.19 = bf16[256,2048]{1,0:T(8,128)(2,1)S(1)} collective-permute-done((bf16[256,2048]{1,0:T(8,128)(2,1)S(1)}, bf16[256,2048]{1,0:T(8,128)(2,1)S(1)}, u32[]{:S(2)}, u32[]{:S(2)}) %collective-permute-start.19) | collective-permute-done | bytes 1048608 | tf_op jit(solution)/shard_map/ppermute | solution.py:27
  443.0 19.9 %collective-permute-done.20 = bf16[256,2048]{1,0:T(8,128)(2,1)S(1)} collective-permute-done((bf16[256,2048]{1,0:T(8,128)(2,1)S(1)}, bf16[256,2048]{1,0:T(8,128)(2,1)S(1)}, u32[]{:S(2)}, u32[]{:S(2)}) %collective-permute-start.20) | collective-permute-done | bytes 1048608 | tf_op jit(solution)/shard_map/ppermute | solution.py:27
  479.2 11.9 collective-permute-done.24
  491.4 21.0 %collective-permute-done.23 = bf16[256,2048]{1,0:T(8,128)(2,1)S(1)} collective-permute-done((bf16[256,2048]{1,0:T(8,128)(2,1)S(1)}, bf16[256,2048]{1,0:T(8,128)(2,1)S(1)}, u32[]{:S(2)}, u32[]{:S(2)}) %collective-permute-start.23) | collective-permute-done | bytes 1048608 | tf_op jit(solution)/shard_map/ppermute | solution.py:27
  513.8 12.0 fusion.139
  525.8 12.0 fusion.137
  537.8 17.7 %collective-permute-done.38 = bf16[256,2048]{1,0:T(8,128)(2,1)} collective-permute-done((bf16[256,2048]{1,0:T(8,128)(2,1)}, bf16[256,2048]{1,0:T(8,128)(2,1)}, u32[]{:S(2)}, u32[]{:S(2)}) %collective-permute-start.38) | collective-permute-done | bytes 1048608 | tf_op jit(solution)/shard_map/ppermute | solution.py:27
  555.5 25.7 %multiply_convert_fusion.1 = (bf16[1024,1536]{1,0:T(8,128)(2,1)}, bf16[1024,1536]{1,0:T(8,128)(2,1)}, bf16[1024,1536]{1,0:T(8,128)(2,1)}) fusion(f32[1024,1536]{1,0:T(8,128)} %fusion.137, f32[1024,1536]{1,0:T(8,128)} %fusion.139, bf16[1536,512]{1,0:T(8,128)(2,1)} %collective-permute-done.32, bf16[1536,512]{1,0:T(8,128)(2,1)} %collective-permute-done.31, ...), kind=kOutput, calls=%fused_computation.10 | convolution fusion | flops 6534725632 | bytes 32505856 | tf_op jit(solution)/shard_map/dot_general | solution.py:115
  581.3 14.7 %fusion.138 = f32[1024,2048]{1,0:T(8,128)} fusion(bf16[1024,1536]{1,0:T(8,128)(2,1)} %get-tuple-element.78, bf16[512,1536]{1,0:T(8,128)(2,1)} %get-tuple-element.97, bf16[512,1536]{1,0:T(8,128)(2,1)} %copy-done.45, bf16[512,1536]{1,0:T(8,128)(2,1)} %copy-done.43, bf16[512,768]{1,0:T(8,128)(2,1)} %copy-done.18, bf16[512,768]{1,0:T(8,128)(2,1)S(1)} %copy-done.13), kind=kOutput, calls=%fused_computation.376 | convolution fusion | flops 6473908224 | bytes 17825792 | tf_op jit(solution)/shard_map/dot_general | solution.py:115
  595.9 18.1 %fusion.167 = (bf16[1024,2048]{1,0:T(8,128)(2,1)}, f32[1024,2048]{1,0:T(8,128)}) fusion(f32[1024,2048]{1,0:T(8,128)} %fusion.138, bf16[1024,1536]{1,0:T(8,128)(2,1)} %get-tuple-element.77, bf16[512,1536]{1,0:T(8,128)(2,1)} %get-tuple-element.96, bf16[512,1536]{1,0:T(8,128)(2,1)} %copy-done.44, bf16[512,1536]{1,0:T(8,128)(2,1)} %copy-done.42, ...), kind=kOutput, calls=%fused_computation.402 | convolution fusion | flops 6478102528 | bytes 30408704 | tf_op jit(solution)/shard_map/dot_general | solution.py:115
  642.4 39.1 %collective-permute-done.39 = bf16[256,2048]{1,0:T(8,128)(2,1)} collective-permute-done((bf16[256,2048]{1,0:T(8,128)(2,1)S(1)}, bf16[256,2048]{1,0:T(8,128)(2,1)}, u32[]{:S(2)}, u32[]{:S(2)}) %collective-permute-start.39) | collective-permute-done | bytes 1048608 | tf_op jit(solution)/shard_map/ppermute | solution.py:27
  714.5 14.6 %convolution_convert_fusion = bf16[1536,2048]{1,0:T(8,128)(2,1)S(1)} fusion(bf16[1024,1536]{1,0:T(8,128)(2,1)} %get-tuple-element.79, bf16[256,2048]{1,0:T(8,128)(2,1)} %collective-permute-done.38, bf16[256,2048]{1,0:T(8,128)(2,1)} %collective-permute-done.37, bf16[256,2048]{1,0:T(8,128)(2,1)} %collective-permute-done.36, bf16[256,512]{1,0:T(8,128)(2,1)S(1)} %copy-done.36, ...), kind=kOutput, calls=%fused_computation | convolution fusion | flops 6474956800 | bytes 13631488 | tf_op jit(solution)/shard_map/dot_general | solution.py:111
  738.8 16.2 %collective-permute-done.43 = bf16[256,2048]{1,0:T(8,128)(2,1)S(1)} collective-permute-done((bf16[256,2048]{1,0:T(8,128)(2,1)S(1)}, bf16[256,2048]{1,0:T(8,128)(2,1)S(1)}, u32[]{:S(2)}, u32[]{:S(2)}) %collective-permute-start.43) | collective-permute-done | bytes 1048608 | tf_op jit(solution)/shard_map/ppermute | solution.py:27
  817.1 14.0 %grads.1 = (bf16[4,256,1280]{2,1,0:T(8,128)(2,1)}, bf16[4,256,640]{2,1,0:T(8,128)(2,1)}, f32[24,640]{1,0:T(8,128)}, f32[24,640]{1,0:T(8,128)}, f32[64,640]{1,0:T(8,128)}, /*index=5*/f32[8,640]{1,0:T(8,128)}) custom-call(s32[1]{0:T(128)} %bitcast.2.ci, f32[4,256,640]{2,1,0:T(8,128)} %get-tuple-element.46.dh_ref, f32[4,256,640]{2,1,0:T(8,128)} %get-tuple-element.41.a_ref, ...), custom_call_target="tpu_custom_call" | custom-call | tf_op jit(solution)/shard_map/grads/pallas_call | solution.py:429
  857.7 43.5 %all-reduce.12.cloned.1.call-done = f32[8,40,80]{2,1,0:T(8,128)} async-done(((f32[8,40,80]{2,1,0:T(8,128)}), f32[8,40,80]{2,1,0:T(8,128)}) %all-reduce.12.cloned.1.call-update) | async-done | bytes 102416
  909.0 32.2 %reduce-scatter.2.cloned.1.call-done = bf16[1,2,2,40,160]{4,3,2,1,0:T(8,128)(2,1)} async-done(((bf16[8,2,2,40,160]{4,3,2,1,0:T(8,128)(2,1)}), bf16[1,2,2,40,160]{4,3,2,1,0:T(8,128)(2,1)}) %reduce-scatter.2.cloned.1.call-update) | async-done | bytes 51216 | tf_op jit(solution)/shard_map/reduce_scatter | solution.py:690
  971.5 19.4 %collective-permute-done.54 = bf16[256,2048]{1,0:T(8,128)(2,1)S(1)} collective-permute-done((bf16[256,2048]{1,0:T(8,128)(2,1)S(1)}, bf16[256,2048]{1,0:T(8,128)(2,1)S(1)}, u32[]{:S(2)}, u32[]{:S(2)}) %collective-permute-start.54) | collective-permute-done | bytes 1048608 | tf_op jit(solution)/shard_map/ppermute | solution.py:27
  998.3 73.1 %all-reduce.8 = f32[32,2,64]{2,1,0:T(2,128)S(1)} all-reduce(f32[32,2,64]{2,1,0:T(2,128)S(1)} %copy.90), channel_id=5, replica_groups=mesh['sx'=2,'sc'=2,'co'=2,'ca'=2,'cb'=2] {'co','ca','cb','sx','sc'}, use_global_device_ids=true, to_apply=%region_9.10.clone | all-reduce | flops 4096 | bytes 32768
  1108.9 13.1 %collective-permute-done.57 = bf16[512,640]{0,1:T(8,128)(2,1)S(1)} collective-permute-done((bf16[512,640]{0,1:T(8,128)(2,1)S(1)}, bf16[512,640]{0,1:T(8,128)(2,1)S(1)}, u32[]{:S(2)}, u32[]{:S(2)}) %collective-permute-start.57) | collective-permute-done | bytes 655392 | tf_op jit(solution)/shard_map/ppermute | solution.py:23
  1126.3 16.2 %collective-permute-done.61 = bf16[512,320]{0,1:T(8,128)(2,1)S(1)} collective-permute-done((bf16[512,320]{0,1:T(8,128)(2,1)S(1)}, bf16[512,320]{0,1:T(8,128)(2,1)S(1)}, u32[]{:S(2)}, u32[]{:S(2)}) %collective-permute-start.61) | collective-permute-done | bytes 327712 | tf_op jit(solution)/shard_map/ppermute | solution.py:23
  1155.0 45.0 %collective-permute-done.58 = bf16[512,320]{0,1:T(8,128)(2,1)S(1)} collective-permute-done((bf16[512,320]{0,1:T(8,128)(2,1)S(1)}, bf16[512,320]{0,1:T(8,128)(2,1)S(1)}, u32[]{:S(2)}, u32[]{:S(2)}) %collective-permute-start.58) | collective-permute-done | bytes 327712 | tf_op jit(solution)/shard_map/ppermute | solution.py:23
  1201.0 15.9 %collective-permute-done.67 = bf16[512,768]{1,0:T(8,128)(2,1)S(1)} collective-permute-done((bf16[512,768]{1,0:T(8,128)(2,1)S(1)}, bf16[512,768]{1,0:T(8,128)(2,1)S(1)}, u32[]{:S(2)}, u32[]{:S(2)}) %collective-permute-start.67) | collective-permute-done | bytes 786464 | tf_op jit(solution)/shard_map/ppermute | solution.py:23
  1218.2 15.5 %collective-permute-done.70 = bf16[512,768]{1,0:T(8,128)(2,1)S(1)} collective-permute-done((bf16[512,768]{1,0:T(8,128)(2,1)S(1)}, bf16[512,768]{1,0:T(8,128)(2,1)S(1)}, u32[]{:S(2)}, u32[]{:S(2)}) %collective-permute-start.70) | collective-permute-done | bytes 786464 | tf_op jit(solution)/shard_map/ppermute | solution.py:23
  1235.1 15.4 %collective-permute-done.73 = bf16[768,512]{1,0:T(8,128)(2,1)S(1)} collective-permute-done((bf16[768,512]{1,0:T(8,128)(2,1)S(1)}, bf16[768,512]{1,0:T(8,128)(2,1)S(1)}, u32[]{:S(2)}, u32[]{:S(2)}) %collective-permute-start.73) | collective-permute-done | bytes 786464 | tf_op jit(solution)/shard_map/ppermute | solution.py:23
  (560 shorter events, 424.1 us)
Async XLA Ops:
  7.2 894.0 %all-reduce.12.cloned.1.call-start = ((), (), s32[]{:S(2)}) async-start(), calls=%async_computation.2 | async-start | bytes 327680
  10.2 200.2 %collective-permute-start.2 = (bf16[256,2048]{1,0:T(8,128)(2,1)S(1)}, bf16[256,2048]{1,0:T(8,128)(2,1)S(1)}, u32[]{:S(2)}, u32[]{:S(2)}) collective-permute-start(bf16[256,2048]{1,0:T(8,128)(2,1)S(1)} %get-tuple-element.76), channel_id=1, source_target_pairs={{0,3},{1,2},{2,1},{3,0},{4,7},{5,6},{6,5},{7,4},{8,11},{9,10},{10,... | collective-permute-start | bytes 3145736 | tf_op jit(solution)/shard_map/ppermute | solution.py:27
  14.2 198.1 %collective-permute-start.1 = (bf16[256,2048]{1,0:T(8,128)(2,1)S(1)}, bf16[256,2048]{1,0:T(8,128)(2,1)S(1)}, u32[]{:S(2)}, u32[]{:S(2)}) collective-permute-start(bf16[256,2048]{1,0:T(8,128)(2,1)S(1)} %get-tuple-element.76), channel_id=1, source_target_pairs={{0,2},{1,3},{2,0},{3,1},{4,6},{5,7},{6,4},{7,5},{8,10},{9,11},{10,... | collective-permute-start | bytes 3145736 | tf_op jit(solution)/shard_map/ppermute | solution.py:27
  14.7 214.2 %collective-permute-start = (bf16[256,2048]{1,0:T(8,128)(2,1)S(1)}, bf16[256,2048]{1,0:T(8,128)(2,1)}, u32[]{:S(2)}, u32[]{:S(2)}) collective-permute-start(bf16[256,2048]{1,0:T(8,128)(2,1)S(1)} %get-tuple-element.76), channel_id=1, source_target_pairs={{0,1},{1,0},{2,3},{3,2},{4,5},{5,4},{6,7},{7,6},{8,9},{9,8},{10,11... | collective-permute-start | bytes 3145736 | tf_op jit(solution)/shard_map/ppermute | solution.py:27
  14.8 192.1 %collective-permute-start.15 = (bf16[320,512]{1,0:T(8,128)(2,1)}, bf16[320,512]{1,0:T(8,128)(2,1)}, u32[]{:S(2)}, u32[]{:S(2)}) collective-permute-start(bf16[320,512]{1,0:T(8,128)(2,1)} %param.25), channel_id=1, source_target_pairs={{0,4},{4,0},{1,5},{5,1},{2,6},{6,2},{3,7},{7,3},{8,12},{12,8},{9,1... | collective-permute-start | bytes 983048 | tf_op jit(solution)/shard_map/ppermute | solution.py:23
  19.6 174.9 %collective-permute-start.3 = (bf16[512,640]{0,1:T(8,128)(2,1)}, bf16[512,640]{0,1:T(8,128)(2,1)}, u32[]{:S(2)}, u32[]{:S(2)}) collective-permute-start(bf16[512,640]{0,1:T(8,128)(2,1)} %pad_maximum_fusion.18), channel_id=1, source_target_pairs={{0,4},{4,0},{1,5},{5,1},{2,6},{6,2},{3,7},{7,3},{8,12},{12,8},{9,1... | collective-permute-start | bytes 1966088 | tf_op jit(solution)/shard_map/ppermute | solution.py:23
  206.9 66.6 %collective-permute-start.25 = (bf16[512,1536]{1,0:T(8,128)(2,1)}, bf16[512,1536]{1,0:T(8,128)(2,1)S(1)}, u32[]{:S(2)}, u32[]{:S(2)}) collective-permute-start(bf16[512,1536]{1,0:T(8,128)(2,1)} %pad_maximum_fusion.10), channel_id=1, source_target_pairs={{0,4},{4,0},{1,5},{5,1},{2,6},{6,2},{3,7},{7,3},{8,12},{12,8},{9,1... | collective-permute-start | bytes 4718600 | tf_op jit(solution)/shard_map/ppermute | solution.py:23
  210.4 107.1 %collective-permute-start.16 = (bf16[640,512]{1,0:T(8,128)(2,1)}, bf16[640,512]{1,0:T(8,128)(2,1)}, u32[]{:S(2)}, u32[]{:S(2)}) collective-permute-start(bf16[640,512]{1,0:T(8,128)(2,1)} %constant_dynamic-update-slice_fusion), channel_id=1, source_target_pairs={{0,16},{16,0},{1,17},{17,1},{2,18},{18,2},{3,19},{19,3},{4,20},{20... | collective-permute-start | bytes 1966088 | tf_op jit(solution)/shard_map/ppermute | solution.py:23
  299.5 120.3 %collective-permute-start.26 = (bf16[512,3072]{1,0:T(8,128)(2,1)}, bf16[512,3072]{1,0:T(8,128)(2,1)}, u32[]{:S(2)}, u32[]{:S(2)}) collective-permute-start(bf16[512,3072]{1,0:T(8,128)(2,1)} %pad_maximum_fusion.8), channel_id=1, source_target_pairs={{0,16},{16,0},{1,17},{17,1},{2,18},{18,2},{3,19},{19,3},{4,20},{20... | collective-permute-start | bytes 9437192 | tf_op jit(solution)/shard_map/ppermute | solution.py:23
  317.5 69.0 %collective-permute-start.17 = (bf16[640,512]{1,0:T(8,128)(2,1)}, bf16[640,512]{1,0:T(8,128)(2,1)}, u32[]{:S(2)}, u32[]{:S(2)}) collective-permute-start(bf16[640,512]{1,0:T(8,128)(2,1)} %constant_dynamic-update-slice_fusion), channel_id=1, source_target_pairs={{0,8},{8,0},{1,9},{9,1},{2,10},{10,2},{3,11},{11,3},{4,12},{12,4},... | collective-permute-start | bytes 1966088 | tf_op jit(solution)/shard_map/ppermute | solution.py:23
  317.5 70.3 %collective-permute-start.18 = (bf16[640,512]{1,0:T(8,128)(2,1)}, bf16[640,512]{1,0:T(8,128)(2,1)}, u32[]{:S(2)}, u32[]{:S(2)}) collective-permute-start(bf16[640,512]{1,0:T(8,128)(2,1)} %collective-permute-done.16), channel_id=1, source_target_pairs={{0,8},{8,0},{1,9},{9,1},{2,10},{10,2},{3,11},{11,3},{4,12},{12,4},... | collective-permute-start | bytes 1966088 | tf_op jit(solution)/shard_map/ppermute | solution.py:23
  379.0 89.0 %collective-permute-start.27 = (bf16[512,3072]{1,0:T(8,128)(2,1)}, bf16[512,3072]{1,0:T(8,128)(2,1)}, u32[]{:S(2)}, u32[]{:S(2)}) collective-permute-start(bf16[512,3072]{1,0:T(8,128)(2,1)} %pad_maximum_fusion.8), channel_id=1, source_target_pairs={{0,8},{8,0},{1,9},{9,1},{2,10},{10,2},{3,11},{11,3},{4,12},{12,4},... | collective-permute-start | bytes 9437192 | tf_op jit(solution)/shard_map/ppermute | solution.py:23
  471.9 65.9 %collective-permute-start.37 = (bf16[256,2048]{1,0:T(8,128)(2,1)}, bf16[256,2048]{1,0:T(8,128)(2,1)}, u32[]{:S(2)}, u32[]{:S(2)}) collective-permute-start(bf16[256,2048]{1,0:T(8,128)(2,1)} %pad_maximum_fusion.15), channel_id=1, source_target_pairs={{0,2},{1,3},{2,0},{3,1},{4,6},{5,7},{6,4},{7,5},{8,10},{9,11},{10,... | collective-permute-start | bytes 3145736 | tf_op jit(solution)/shard_map/ppermute | solution.py:27
  491.2 64.3 %collective-permute-start.38 = (bf16[256,2048]{1,0:T(8,128)(2,1)}, bf16[256,2048]{1,0:T(8,128)(2,1)}, u32[]{:S(2)}, u32[]{:S(2)}) collective-permute-start(bf16[256,2048]{1,0:T(8,128)(2,1)} %pad_maximum_fusion.15), channel_id=1, source_target_pairs={{0,3},{1,2},{2,1},{3,0},{4,7},{5,6},{6,5},{7,4},{8,11},{9,10},{10,... | collective-permute-start | bytes 3145736 | tf_op jit(solution)/shard_map/ppermute | solution.py:27
  617.7 74.6 %collective-permute-start.41 = (bf16[256,2048]{1,0:T(8,128)(2,1)}, bf16[256,2048]{1,0:T(8,128)(2,1)}, u32[]{:S(2)}, u32[]{:S(2)}) collective-permute-start(bf16[256,2048]{1,0:T(8,128)(2,1)} %get-tuple-element.84), channel_id=1, source_target_pairs={{0,3},{1,2},{2,1},{3,0},{4,7},{5,6},{6,5},{7,4},{8,11},{9,10},{10,... | collective-permute-start | bytes 3145736 | tf_op jit(solution)/shard_map/ppermute | solution.py:27
  618.2 74.0 %collective-permute-start.40 = (bf16[256,2048]{1,0:T(8,128)(2,1)S(1)}, bf16[256,2048]{1,0:T(8,128)(2,1)}, u32[]{:S(2)}, u32[]{:S(2)}) collective-permute-start(bf16[256,2048]{1,0:T(8,128)(2,1)S(1)} %get-tuple-element.85), channel_id=1, source_target_pairs={{0,2},{1,3},{2,0},{3,1},{4,6},{5,7},{6,4},{7,5},{8,10},{9,11},{10,... | collective-permute-start | bytes 3145736 | tf_op jit(solution)/shard_map/ppermute | solution.py:27
  632.0 74.8 %collective-permute-start.33 = (bf16[256,2048]{1,0:T(8,128)(2,1)}, bf16[256,2048]{1,0:T(8,128)(2,1)S(1)}, u32[]{:S(2)}, u32[]{:S(2)}) collective-permute-start(bf16[256,2048]{1,0:T(8,128)(2,1)} %get-tuple-element.86), channel_id=1, source_target_pairs={{0,1},{1,0},{2,3},{3,2},{4,5},{5,4},{6,7},{7,6},{8,9},{9,8},{10,11... | collective-permute-start | bytes 3145736 | tf_op jit(solution)/shard_map/ppermute | solution.py:27
  632.3 74.4 %collective-permute-start.35 = (bf16[256,2048]{1,0:T(8,128)(2,1)}, bf16[256,2048]{1,0:T(8,128)(2,1)S(1)}, u32[]{:S(2)}, u32[]{:S(2)}) collective-permute-start(bf16[256,2048]{1,0:T(8,128)(2,1)} %get-tuple-element.87), channel_id=1, source_target_pairs={{0,3},{1,2},{2,1},{3,0},{4,7},{5,6},{6,5},{7,4},{8,11},{9,10},{10,... | collective-permute-start | bytes 3145736 | tf_op jit(solution)/shard_map/ppermute | solution.py:27
  736.5 206.3 %collective-permute-start.65 = (bf16[1024,1536]{1,0:T(8,128)(2,1)}, bf16[1024,1536]{1,0:T(8,128)(2,1)}, u32[]{:S(2)}, u32[]{:S(2)}) collective-permute-start(bf16[1024,1536]{1,0:T(8,128)(2,1)} %slice.790), channel_id=1, source_target_pairs={{0,8},{8,0},{1,9},{9,1},{2,10},{10,2},{3,11},{11,3},{4,12},{12,4},... | collective-permute-start | bytes 9437192 | tf_op jit(solution)/shard_map/ppermute | solution.py:23
  736.5 212.6 %collective-permute-start.68 = (bf16[1024,1536]{1,0:T(8,128)(2,1)}, bf16[1024,1536]{1,0:T(8,128)(2,1)}, u32[]{:S(2)}, u32[]{:S(2)}) collective-permute-start(bf16[1024,1536]{1,0:T(8,128)(2,1)} %slice.796), channel_id=1, source_target_pairs={{0,8},{8,0},{1,9},{9,1},{2,10},{10,2},{3,11},{11,3},{4,12},{12,4},... | collective-permute-start | bytes 9437192 | tf_op jit(solution)/shard_map/ppermute | solution.py:23
  814.7 143.5 %collective-permute-start.71 = (bf16[1536,1024]{1,0:T(8,128)(2,1)}, bf16[1536,1024]{1,0:T(8,128)(2,1)}, u32[]{:S(2)}, u32[]{:S(2)}) collective-permute-start(bf16[1536,1024]{1,0:T(8,128)(2,1)} %slice.802), channel_id=1, source_target_pairs={{0,8},{8,0},{1,9},{9,1},{2,10},{10,2},{3,11},{11,3},{4,12},{12,4},... | collective-permute-start | bytes 9437192 | tf_op jit(solution)/shard_map/ppermute | solution.py:23
  815.8 256.7 %collective-permute-start.62 = (bf16[640,1024]{1,0:T(8,128)(2,1)}, bf16[640,1024]{1,0:T(8,128)(2,1)}, u32[]{:S(2)}, u32[]{:S(2)}) collective-permute-start(bf16[640,1024]{1,0:T(8,128)(2,1)} %slice.784), channel_id=1, source_target_pairs={{0,8},{8,0},{1,9},{9,1},{2,10},{10,2},{3,11},{11,3},{4,12},{12,4},... | collective-permute-start | bytes 3932168 | tf_op jit(solution)/shard_map/ppermute | solution.py:23
  836.2 105.0 %reduce-scatter.2.cloned.1.call-start = ((), (), s32[]{:S(2)}) async-start(), calls=%async_computation.1 | async-start | bytes 737280 | tf_op jit(solution)/shard_map/reduce_scatter | solution.py:690
  857.4 105.6 %collective-permute-start.53 = (bf16[256,2048]{1,0:T(8,128)(2,1)}, bf16[256,2048]{1,0:T(8,128)(2,1)S(1)}, u32[]{:S(2)}, u32[]{:S(2)}) collective-permute-start(bf16[256,2048]{1,0:T(8,128)(2,1)} %get-tuple-element.80), channel_id=1, source_target_pairs={{0,1},{1,0},{2,3},{3,2},{4,5},{5,4},{6,7},{7,6},{8,9},{9,8},{10,11... | collective-permute-start | bytes 3145736 | tf_op jit(solution)/shard_map/ppermute | solution.py:27
  958.2 120.2 %collective-permute-start.59 = (bf16[1024,640]{0,1:T(8,128)(2,1)}, bf16[1024,640]{0,1:T(8,128)(2,1)}, u32[]{:S(2)}, u32[]{:S(2)}) collective-permute-start(bf16[1024,640]{0,1:T(8,128)(2,1)} %slice.778), channel_id=1, source_target_pairs={{0,8},{8,0},{1,9},{9,1},{2,10},{10,2},{3,11},{11,3},{4,12},{12,4},... | collective-permute-start | bytes 3932168 | tf_op jit(solution)/shard_map/ppermute | solution.py:23
  963.0 117.6 %collective-permute-start.56 = (bf16[1024,640]{0,1:T(8,128)(2,1)}, bf16[1024,640]{0,1:T(8,128)(2,1)}, u32[]{:S(2)}, u32[]{:S(2)}) collective-permute-start(bf16[1024,640]{0,1:T(8,128)(2,1)} %slice.772), channel_id=1, source_target_pairs={{0,8},{8,0},{1,9},{9,1},{2,10},{10,2},{3,11},{11,3},{4,12},{12,4},... | collective-permute-start | bytes 3932168 | tf_op jit(solution)/shard_map/ppermute | solution.py:23
  970.1 173.3 %collective-permute-start.66 = (bf16[512,1536]{1,0:T(8,128)(2,1)}, bf16[512,1536]{1,0:T(8,128)(2,1)}, u32[]{:S(2)}, u32[]{:S(2)}) collective-permute-start(bf16[512,1536]{1,0:T(8,128)(2,1)} %slice.1147), channel_id=1, source_target_pairs={{0,16},{16,0},{1,17},{17,1},{2,18},{18,2},{3,19},{19,3},{4,20},{20... | collective-permute-start | bytes 4718600 | tf_op jit(solution)/shard_map/ppermute | solution.py:23
  990.9 154.8 %collective-permute-start.69 = (bf16[512,1536]{1,0:T(8,128)(2,1)}, bf16[512,1536]{1,0:T(8,128)(2,1)}, u32[]{:S(2)}, u32[]{:S(2)}) collective-permute-start(bf16[512,1536]{1,0:T(8,128)(2,1)} %slice.1146), channel_id=1, source_target_pairs={{0,16},{16,0},{1,17},{17,1},{2,18},{18,2},{3,19},{19,3},{4,20},{20... | collective-permute-start | bytes 4718600 | tf_op jit(solution)/shard_map/ppermute | solution.py:23
  1123.0 77.0 %collective-permute-start.58 = (bf16[512,320]{0,1:T(8,128)(2,1)S(1)}, bf16[512,320]{0,1:T(8,128)(2,1)S(1)}, u32[]{:S(2)}, u32[]{:S(2)}) collective-permute-start(bf16[512,320]{0,1:T(8,128)(2,1)S(1)} %slice.1156), channel_id=1, source_target_pairs={{0,4},{4,0},{1,5},{5,1},{2,6},{6,2},{3,7},{7,3},{8,12},{12,8},{9,1... | collective-permute-start | bytes 983048 | tf_op jit(solution)/shard_map/ppermute | solution.py:23
  1145.6 71.3 %collective-permute-start.67 = (bf16[512,768]{1,0:T(8,128)(2,1)S(1)}, bf16[512,768]{1,0:T(8,128)(2,1)S(1)}, u32[]{:S(2)}, u32[]{:S(2)}) collective-permute-start(bf16[512,768]{1,0:T(8,128)(2,1)S(1)} %slice.1150), channel_id=1, source_target_pairs={{0,4},{4,0},{1,5},{5,1},{2,6},{6,2},{3,7},{7,3},{8,12},{12,8},{9,1... | collective-permute-start | bytes 2359304 | tf_op jit(solution)/shard_map/ppermute | solution.py:23
  1147.9 85.8 %collective-permute-start.70 = (bf16[512,768]{1,0:T(8,128)(2,1)S(1)}, bf16[512,768]{1,0:T(8,128)(2,1)S(1)}, u32[]{:S(2)}, u32[]{:S(2)}) collective-permute-start(bf16[512,768]{1,0:T(8,128)(2,1)S(1)} %slice.1149), channel_id=1, source_target_pairs={{0,4},{4,0},{1,5},{5,1},{2,6},{6,2},{3,7},{7,3},{8,12},{12,8},{9,1... | collective-permute-start | bytes 2359304 | tf_op jit(solution)/shard_map/ppermute | solution.py:23
  1154.3 96.2 %collective-permute-start.73 = (bf16[768,512]{1,0:T(8,128)(2,1)S(1)}, bf16[768,512]{1,0:T(8,128)(2,1)S(1)}, u32[]{:S(2)}, u32[]{:S(2)}) collective-permute-start(bf16[768,512]{1,0:T(8,128)(2,1)S(1)} %slice.1148), channel_id=1, source_target_pairs={{0,4},{4,0},{1,5},{5,1},{2,6},{6,2},{3,7},{7,3},{8,12},{12,8},{9,1... | collective-permute-start | bytes 2359304 | tf_op jit(solution)/shard_map/ppermute | solution.py:23
  (161 other events, 3751.2 us)
Sparse Core Ops, SparseCore 0:
  836.3 64.8 all-reduce.11
  905.2 35.9 reduce-scatter.1

commit v2 on v1

--- a/solution.py
+++ b/solution.py
@@ -12,7 +12,6 @@
 F32 = jnp.float32
 BLOCKS = ("sx", "sc", "co")
 PEERS = ("ca", "cb")
-EVERY = ("co", "ca", "cb", "sx", "sc")
 PEER = 4
 GELU_C = 0.7978845608028654
 GELU_K = 0.044715
@@ -69,38 +68,92 @@
     return jnp.concatenate(parts, axis=-1)
 
 
-def chunk_order(value, axis):
-    count, mine = lax.axis_size("co"), lax.axis_index("co")
-    return jnp.concatenate(
-        [
-            lax.dynamic_slice_in_dim(value, lax.rem(mine - r + count, count), 1, axis)
-            for r in range(count)
-        ],
-        axis=axis,
-    )
-
-
-def gather_weight(shard, join):
-    held = join([shard] + [shift(shard, "co", r) for r in range(1, lax.axis_size("co"))])
-    rows = [held] + [shift(held, "sx", r) for r in range(1, lax.axis_size("sx"))]
-    return rows + [shift(item, "sc", 1) for item in rows]
-
-
-def scatter_weight(grad, cut, axis):
-    nsx = lax.axis_size("sx")
-    half = grad.shape[axis] // 2
-    mine = lax.slice_in_dim(grad, 0, half, axis=axis).astype(F32)
-    mine = mine + shift(lax.slice_in_dim(grad, half, 2 * half, axis=axis), "sc", -1).astype(F32)
-    width = half // nsx
-    total = lax.slice_in_dim(mine, 0, width, axis=axis)
-    for r in range(1, nsx):
-        part = lax.slice_in_dim(mine, r * width, (r + 1) * width, axis=axis).astype(BF)
-        total = total + shift(part, "sx", -r).astype(F32)
-    parts = cut(total)
-    total = parts[0]
+def after(value, *done):
+    return lax.optimization_barrier((value, *done))[0]
+
+
+def around(value, axis):
+    return [value] + [shift(value, axis, r) for r in range(1, lax.axis_size(axis))]
+
+
+def sum_around(parts, axis):
+    total = parts[0].astype(F32)
     for r in range(1, len(parts)):
-        total = total + shift(parts[r].astype(BF), "co", -r).astype(F32)
+        total = total + shift(parts[r].astype(BF), axis, -r).astype(F32)
     return total
+
+
+def cut(value, count, axis):
+    size = value.shape[axis] // count
+    return [lax.slice_in_dim(value, r * size, (r + 1) * size, axis=axis) for r in range(count)]
+
+
+def over_cores(grad, axis):
+    return sum_around(cut(grad, lax.axis_size("sc"), axis), "sc")
+
+
+def over_chips(grad, axis):
+    return sum_around(cut(grad, lax.axis_size("sx"), axis), "sx")
+
+
+def over_chunks(grad, axis):
+    return sum_around(cut(grad, lax.axis_size("co"), axis), "co")
+
+
+def join_kernel(groups, *refs):
+    out = refs[-1]
+    width = refs[0].shape[1] // groups
+    at = 0
+    for g in range(groups):
+        for ref in refs[:-1]:
+            out[:, at : at + width] = ref[:, g * width : (g + 1) * width]
+            at += width
+
+
+def join_columns(items, groups):
+    rows, width = items[0].shape
+    block = rows // 4
+    return pl.pallas_call(
+        functools.partial(join_kernel, groups),
+        out_shape=jax.ShapeDtypeStruct((rows, width * len(items)), items[0].dtype),
+        grid=(4,),
+        in_specs=[pl.BlockSpec((block, width), lambda i: (i, 0))] * len(items),
+        out_specs=pl.BlockSpec((block, width * len(items)), lambda i: (i, 0)),
+        name="join",
+    )(*items)
+
+
+def compose(earlier, later, rows):
+    decay, state = later[:rows], later[rows:]
+    return jnp.concatenate([earlier[:rows] * decay, decay * earlier[rows:] + state], axis=0)
+
+
+def other_blocks(summary, rows, backward):
+    width = summary.shape[-1]
+    empty = jnp.concatenate([jnp.ones((rows, width), F32), jnp.zeros((rows, width), F32)], axis=0)
+    outer = empty
+    for axis in ("co", "sc", "sx"):
+        count, mine = lax.axis_size(axis), lax.axis_index(axis)
+        items = around(summary, axis)
+        if axis == "co":
+            items = [chunk_roll(item, r) for r, item in enumerate(items)]
+        if count == 2:
+            mate = items[1]
+            ahead = (mine == 0) if backward else (mine == 1)
+            joined = compose(mate, summary, rows)
+            outer = jnp.where(ahead, compose(mate, outer, rows), outer)
+            summary = jnp.where(ahead, joined, compose(summary, mate, rows))
+        else:
+            table = jnp.stack(items)
+            total, inner = empty, empty
+            for place in reversed(range(count)) if backward else range(count):
+                item = table[lax.rem(mine - place + count, count)]
+                total = compose(total, item, rows)
+                ahead = (place > mine) if backward else (place < mine)
+                inner = jnp.where(ahead, compose(inner, item, rows), inner)
+            outer = compose(inner, outer, rows)
+            summary = total
+    return outer
 
 
 def matmul(left, right):
@@ -309,6 +362,24 @@
         edge_ref[t * rows : (t + 1) * rows, :] = row
 
 
+def gate_matrix_kernel(blocks_ref, out_ref):
+    kinds, heads, span, _ = blocks_ref.shape
+    out_ref[...] = jnp.zeros(out_ref.shape, BF)
+    for g in range(kinds):
+        for h in range(heads):
+            at = (g * heads + h) * span
+            out_ref[h * span : (h + 1) * span, at : at + span] = blocks_ref[g, h]
+
+
+def gate_matrix(blocks):
+    kinds, heads, span, _ = blocks.shape
+    return pl.pallas_call(
+        gate_matrix_kernel,
+        out_shape=jax.ShapeDtypeStruct((heads * span, kinds * heads * span), BF),
+        name="gate_matrix",
+    )(blocks)
+
+
 def gates_call(ci, uy, edge, gate, vec, rows):
     steps, size, wide = uy.shape
     width = wide // 2
@@ -507,10 +578,8 @@
 ):
     nsx, nsc, nco = (lax.axis_size(name) for name in BLOCKS)
     nseq = nsx * nsc
-    blocks = nseq * nco
     co = lax.axis_index("co")
-    block = lax.axis_index(BLOCKS)
-    first = block == 0
+    first = lax.axis_index(BLOCKS) == 0
     ci = lax.axis_index(PEERS)
     order = ci.astype(jnp.int32).reshape(1)
     rows, share, model = tokens.shape
@@ -525,9 +594,6 @@
     def owned(value):
         return feature_order(jnp.swapaxes(value, 0, 1).reshape(own, model))
 
-    gains = lax.all_gather(jnp.stack([norm_gain, mlp_gain]), EVERY, axis=0)
-    gains = feature_order(jnp.swapaxes(gains, 0, 1).reshape(2, model).astype(F32))
-    gain_one, gain_two = (gains[0:1], gains[1:2])
     vectors = jnp.concatenate(
         [
             conv_weight,
@@ -540,73 +606,117 @@
         ],
         axis=0,
     )
-    vectors = lax.all_gather(vectors, BLOCKS, axis=0)
-    vectors = jnp.transpose(vectors.reshape(nseq, nco, -1, part), (2, 1, 0, 3))
-    vectors = chunk_order(vectors, 1).reshape(-1, width).astype(F32)
+    heads, span = recur_gate.shape[0], recur_gate.shape[2]
+    both = jnp.stack([recur_gate, input_gate]).reshape(-1, span)
+    gains = jnp.stack([norm_gain, mlp_gain])
+    unit = norm_gain.shape[0]
+
+    def gather_small(value):
+        items = around(value, "co")
+        mark = items[-1]
+        items = [other for item in items for other in around(item, "sx")]
+        return [other for item in items for other in around(item, "sc")], mark
+
+    gains, mark_gains = gather_small(gains)
+    vectors, mark_vectors = gather_small(vectors)
+    both, mark_both = gather_small(both)
+
+    def owned(value):
+        return feature_order(jnp.swapaxes(value, 0, 1).reshape(own, model))
+
+    mine = owned(tokens)
+    group = collect(mine)
+    in_shard = after(
+        jnp.concatenate([recur_proj, branch_proj], axis=1), mark_gains, mark_vectors, mark_both
+    )
+    in_chunks = around(in_shard, "co")
+    in_rows = around(join_columns(in_chunks, 2), "sx")
+    full_in = jnp.concatenate(in_rows + [shift(item, "sc", 1) for item in in_rows], axis=0)
+    out_chunks = around(after(out_proj, in_chunks[-1]), "co")
+    out_columns = around(after(jnp.concatenate(out_chunks, axis=0), in_rows[-1]), "sx")
+    full_out = jnp.concatenate(
+        out_columns + [shift(item, "sc", 1) for item in out_columns], axis=1
+    )
+    grad_mine = owned(cotangent)
+    grad_group = collect(after(grad_mine, *group[1:]))
+    grad_full = jnp.concatenate(grad_group, axis=0)
+
+    gains = jnp.stack(gains).reshape(-1, 2 * unit)
+    gains = jnp.concatenate(collect(gains), axis=0)
+    place = jnp.arange(model // unit)
+    rel = place // (model // unit // nseq)
+    sx, sc = lax.axis_index("sx"), lax.axis_index("sc")
+    here_seq = ((sx - rel % nsx) % nsx) * nsc + (sc - rel // nsx) % nsc
+    whole_unit = here_seq * (model // unit // nseq) + place % (model // unit // nseq)
+    from_chan, from_seq = whole_unit // nseq, whole_unit % nseq
+    source = (from_chan % PEER) ^ ci
+    source = source * nco + (co - from_chan // PEER) % nco
+    source = source * nsx + (sx - from_seq // nsc) % nsx
+    source = source * nsc + (sc - from_seq % nsc) % nsc
+    pick = (source[:, None] == jnp.arange(model // unit)[None, :]).astype(F32)
+    gains = jnp.dot(pick, gains.astype(F32), precision=lax.Precision.HIGHEST)
+    gain_one = gains[:, :unit].reshape(1, model)
+    gain_two = gains[:, unit:].reshape(1, model)
+
+    def blocks_in_order(items):
+        table = jnp.stack(items).reshape(nco, nsx, nsc, *items[0].shape)
+        table = jnp.moveaxis(table, 0, 2).reshape(nseq, nco, *items[0].shape)
+        return jnp.concatenate(
+            [
+                lax.dynamic_slice_in_dim(
+                    table, ((sx - s // nsc) % nsx) * nsc + (sc - s % nsc) % nsc, 1, 0
+                )
+                for s in range(nseq)
+            ],
+            axis=0,
+        )
+
+    vectors = jnp.transpose(blocks_in_order(vectors), (2, 1, 0, 3)).reshape(-1, width)
+    vectors = vectors.astype(F32)
     decay32 = vectors[taps + 3 : taps + 4]
     vec = jnp.concatenate([vectors[: taps + 3], jax.nn.softplus(-decay32)], axis=0)
     vec = jnp.pad(vec, ((0, -vec.shape[0] % 8), (0, 0)))
     state_start = vectors[taps + 4 : taps + 4 + rows] * keep
     tail_start = vectors[taps + 4 + rows :] * jnp.tile(keep, (lag, 1))
-    both = jnp.stack([recur_gate, input_gate])
-    heads, span = both.shape[1], both.shape[3]
-    both = lax.all_gather(both, BLOCKS, axis=0).reshape(nseq, nco, 2, heads, -1, span)
-    both = chunk_order(jnp.transpose(both, (2, 1, 3, 0, 4, 5)), 1)
-    both = both.reshape(2, nco * heads, span, span)
-    gate = jnp.concatenate(
-        [
-            jnp.concatenate(
-                [
-                    jnp.pad(both[g, h], ((0, 0), (span * h, width - span * (h + 1))))
-                    for h in range(nco * heads)
-                ],
-                axis=0,
-            )
-            for g in range(2)
-        ],
-        axis=1,
-    )
-
-    def sides(items):
-        half = items[0].shape[1] // 2
-        return jnp.concatenate(
-            [item[:, :half] for item in items] + [item[:, half:] for item in items], axis=1
-        )
-
-    def stacked(items):
-        return jnp.concatenate(items, axis=0)
-
-    mine = owned(tokens)
-    group = collect(mine)
-    full_in = jnp.concatenate(
-        gather_weight(jnp.concatenate([recur_proj, branch_proj], axis=1), sides), axis=0
-    )
-    full_out = jnp.concatenate(gather_weight(out_proj, stacked), axis=1)
-    mlp_parts = gather_weight(jnp.concatenate([gate_proj, up_proj], axis=1), sides)
-    inner = mlp_parts[0].shape[1] // 2
-    full_gate = jnp.concatenate([item[:, :inner] for item in mlp_parts], axis=0)
-    full_up = jnp.concatenate([item[:, inner:] for item in mlp_parts], axis=0)
-    full_down = jnp.concatenate(gather_weight(down_proj, stacked), axis=1)
-    grad_mine = owned(cotangent)
-    grad_full = jnp.concatenate(collect(grad_mine), axis=0)
+    both = blocks_in_order(both).reshape(nseq, nco, 2, heads, -1, span)
+    both = jnp.transpose(both, (2, 1, 3, 0, 4, 5)).reshape(2, nco * heads, span, span)
+    gate = gate_matrix(both)
+
+    def normed(piece):
+        value = piece.astype(F32)
+        return value * inverse_rms(value)
 
     def normal(piece):
-        value = piece.astype(F32)
-        return (value * inverse_rms(value) * gain_one).astype(BF)
+        return (normed(piece) * gain_one).astype(BF)
 
     normal_in = jnp.concatenate([normal(piece) for piece in group], axis=0)
-    uy = matmul(normal_in, full_in).reshape(PEER, own, 2 * width)
-
-    edge_at = (lax.bitwise_xor(jnp.int32(PEER - 1), ci.astype(jnp.int32)), own - lag * rows, 0)
-    ends = lax.dynamic_slice(uy, edge_at, (1, lag * rows, width))[0].astype(BF)
+    final = lax.bitwise_xor(jnp.int32(PEER - 1), ci.astype(jnp.int32))
+    tail_at = final * own + own - lag * rows
+    ends = matmul(lax.dynamic_slice_in_dim(normal_in, tail_at, lag * rows, 0), full_in)
+    ends = ends[:, :width].astype(BF)
     edge = jnp.where(first, tail_start.astype(BF), chunk_roll(block_shift(ends, 1), 1))
+    uy = matmul(after(normal_in, ends), full_in).reshape(PEER, own, 2 * width)
+
+    edge_at = (final, own - lag * rows, 0)
     v, ra, ri, decay, drive, u_before, summary = gates_call(order, uy, edge, gate, vec, rows)
-    enter = state_start
-    for k in reversed(range(1, blocks)):
-        other = chunk_roll(block_shift(summary, k), k)
-        enter = jnp.where(block >= k, other[:rows] * enter + other[rows:], enter)
+    outer = other_blocks(summary, rows, False)
+    enter = outer[:rows] * state_start + outer[rows:]
+
+    gate_shard = after(gate_proj, enter)
+    gate_chunks = around(gate_shard, "co")
+    gate_rows = around(join_columns(gate_chunks, 1), "sx")
+    full_gate = jnp.concatenate(gate_rows + [shift(item, "sc", 1) for item in gate_rows], axis=0)
+    up_chunks = around(after(up_proj, gate_chunks[-1]), "co")
+    up_rows = around(after(join_columns(up_chunks, 1), gate_rows[-1]), "sx")
+    full_up = jnp.concatenate(up_rows + [shift(item, "sc", 1) for item in up_rows], axis=0)
+    down_chunks = around(after(down_proj, up_chunks[-1]), "co")
+    down_columns = around(after(jnp.concatenate(down_chunks, axis=0), up_rows[-1]), "sx")
+    full_down = jnp.concatenate(
+        down_columns + [shift(item, "sc", 1) for item in down_columns], axis=1
+    )
     h, z, h_before, h_end = states_call(order, decay, drive, uy, enter)
-    branch = matmul(z.reshape(PEER * own, width), full_out).reshape(PEER, own, model)
+    z_low = after(z, grad_full)
+    branch = matmul(z_low.reshape(PEER * own, width), full_out).reshape(PEER, own, model)
     resid = mine.astype(F32) + hand_back([branch[k] for k in range(PEER)])
 
     inv_two = inverse_rms(resid)
@@ -618,8 +728,6 @@
     gate_act, gate_slope = gelu_parts(gate_pre)
     hidden = (gate_act * up_pre).astype(BF)
     mlp = matmul(hidden, full_down).astype(BF).reshape(PEER, own, model)
-    mlp_sum = hand_back([mlp[k].astype(F32) for k in range(PEER)])
-    mixed = (resid + mlp_sum).astype(BF)
 
     grad_hidden = times_transpose(grad_full, full_down)
     grad_gate = (grad_hidden * up_pre * gate_slope).astype(BF)
@@ -627,21 +735,24 @@
     mid = times_transpose(grad_gate, full_gate) + times_transpose(grad_up, full_up)
     mid = mid.reshape(PEER, own, model)
     mid_sum = hand_back([mid[k] for k in range(PEER)])
-    gain_two_part = jnp.sum(mid_sum * normed_two, axis=0)
+    gain_two_part = jnp.sum(mid_sum * normed_two, axis=0, keepdims=True)
     resid_grad = grad_mine.astype(F32) + norm_back(mid_sum, normed_two, inv_two, gain_two)
-    resid_low = jnp.concatenate(collect(resid_grad.astype(BF)), axis=0)
-    down_grad = over_tokens(hidden, grad_full).astype(BF)
-    gate_grad = over_tokens(normal_mid, grad_gate).astype(BF)
-    up_grad = over_tokens(normal_mid, grad_up).astype(BF)
-
-    out_grad = over_tokens(z.reshape(PEER * own, width), resid_low).astype(BF)
+    resid_group = collect(resid_grad.astype(BF))
+    resid_low = jnp.concatenate(resid_group, axis=0)
+    down_grad = over_cores(over_tokens(hidden, grad_full).astype(BF), 1)
+    gate_grad = over_cores(over_tokens(normal_mid, grad_gate).astype(BF), 0)
+    up_grad = over_cores(over_tokens(normal_mid, grad_up).astype(BF), 0)
+    down_grad = over_chips(down_grad, 1)
+
+    resid_low = after(resid_low, down_grad, gate_grad, up_grad)
     dz = times_transpose(resid_low, full_out).reshape(PEER, own, width)
     dh, grad_branch, local_end = back_call(order, dz, uy, h, decay, rows)
-    message = jnp.concatenate([summary[:rows], local_end], axis=0)
-    late = jnp.zeros((rows, width), F32)
-    for k in reversed(range(1, blocks)):
-        other = chunk_roll(block_shift(message, -k), -k)
-        late = jnp.where(block + k < blocks, other[:rows] * late + other[rows:], late)
+    mlp_low, local_end = lax.optimization_barrier((mlp, local_end))
+    mlp_sum = hand_back([mlp_low[k].astype(F32) for k in range(PEER)])
+    mixed = (resid + mlp_sum).astype(BF)
+    late = other_blocks(jnp.concatenate([summary[:rows], local_end], axis=0), rows, True)[rows:]
+    gate_grad = over_chips(after(gate_grad, late), 0)
+    down_grad = over_chunks(after(down_grad, late), 0)
     gates_low, grad_u, edge_out, last, sums, start_grad = grads_call(
         order, dh, decay, ra, ri, v, h, h_before, uy, u_before, gate, vec, late
     )
@@ -649,34 +760,52 @@
     grad_u = lax.dynamic_update_slice(grad_u, (last + edge_in).astype(BF)[None], edge_at)
     grad_u = grad_u.reshape(PEER * own, width)
     grad_branch = grad_branch.reshape(PEER * own, width)
-    recur_grad = over_tokens(normal_in, grad_u).astype(BF)
-    branch_grad = over_tokens(normal_in, grad_branch).astype(BF)
+    out_grad = over_tokens(z.reshape(PEER * own, width), resid_low).astype(BF)
+    out_grad = over_cores(out_grad, 1)
+    branch_grad = over_cores(over_tokens(normal_in, grad_branch).astype(BF), 0)
     both_grad = over_tokens(v.reshape(PEER * own, width), gates_low.reshape(PEER * own, 2 * width))
     back_terms = times_transpose(grad_u, full_in[:, :width]) + times_transpose(
         grad_branch, full_in[:, width:]
     )
     back_terms = back_terms.reshape(PEER, own, model)
-    back_sum = hand_back([back_terms[k] for k in range(PEER)])
+    back_low = back_terms[1:].astype(BF)
+    gain_one_part = sum(
+        jnp.sum(back_terms[k] * normed(group[k]), axis=0, keepdims=True) for k in range(PEER)
+    )
+    back_sum = back_terms[0]
+    for k in range(1, PEER):
+        back_sum = back_sum + peer(back_low[k - 1], k).astype(F32)
+    recur_grad = over_cores(over_tokens(normal_in, grad_u).astype(BF), 0)
     value = mine.astype(F32)
     inv_one = inverse_rms(value)
-    normed_one = value * inv_one
-    gain_one_part = jnp.sum(back_sum * normed_one, axis=0)
-    tokens_grad = resid_grad + norm_back(back_sum, normed_one, inv_one, gain_one)
-
-    def right(total):
-        half = total.shape[1] // nco
-        return [total[:, r * half : (r + 1) * half] for r in range(nco)]
-
-    def low(total):
-        half = total.shape[0] // nco
-        return [total[r * half : (r + 1) * half] for r in range(nco)]
-
-    recur_out = scatter_weight(recur_grad, right, 0)
-    branch_out = scatter_weight(branch_grad, right, 0)
-    out_out = scatter_weight(out_grad, low, 1)
-    gate_out = scatter_weight(gate_grad, right, 0)
-    up_out = scatter_weight(up_grad, right, 0)
-    down_out = scatter_weight(down_grad, low, 1)
+    tokens_grad = resid_grad + norm_back(back_sum, value * inv_one, inv_one, gain_one)
+
+    up_grad = over_chips(after(up_grad, gate_grad), 0)
+    gate_out = over_chunks(after(gate_grad, down_grad), 1)
+    out_grad = over_chips(after(out_grad, up_grad), 1)
+    up_out = over_chunks(after(up_grad, gate_out), 1)
+    branch_grad = over_chips(after(branch_grad, out_grad), 0)
+    out_out = over_chunks(after(out_grad, up_out), 0)
+    recur_grad = over_chips(after(recur_grad, branch_grad), 0)
+    branch_out = over_chunks(after(branch_grad, out_out), 1)
+    recur_out = over_chunks(after(recur_grad, branch_out), 1)
+    down_out = down_grad
+
+    def blocks_apart(value):
+        return jnp.concatenate(
+            [
+                lax.dynamic_slice_in_dim(
+                    value, ((sx - rx) % nsx) * nsc + (sc - rc) % nsc, 1, 0
+                )
+                for rc in range(nsc)
+                for rx in range(nsx)
+            ],
+            axis=0,
+        )
+
+    def scatter_small(value):
+        value = blocks_apart(value).astype(BF)
+        return over_chunks(over_chips(over_cores(value, 0), 0)[0], 0)[0]
 
     pieces = jnp.stack(
         [
@@ -685,11 +814,9 @@
             for h in range(nco * heads)
         ]
     )
-    pieces = chunk_order(pieces.reshape(2, nco, heads, nseq, -1, span), 1)
-    pieces = jnp.transpose(pieces, (3, 1, 0, 2, 4, 5)).reshape(blocks, 2, heads, -1, span)
-    both_out = lax.psum_scatter(
-        pieces.astype(BF), BLOCKS, scatter_dimension=0, tiled=True
-    )[0].astype(F32)
+    pieces = pieces.reshape(2, nco, heads, nseq, -1, span)
+    pieces = jnp.transpose(pieces, (3, 1, 0, 2, 4, 5)).reshape(nseq, nco, -1, span)
+    both_out = scatter_small(pieces).reshape(2, heads, -1, span)
 
     sums = jnp.sum(sums.reshape(-1, rows, width), axis=1)
     small = jnp.concatenate(
@@ -702,13 +829,15 @@
         ],
         axis=0,
     )
-    small = chunk_order(small.reshape(-1, nco, nseq, part), 1)
-    small = jnp.transpose(small, (2, 1, 0, 3)).reshape(blocks, -1, part)
-    small = lax.psum_scatter(small, BLOCKS, scatter_dimension=0, tiled=True)[0]
-
-    gain_parts = feature_restore(jnp.stack([gain_one_part, gain_two_part]))
-    gain_parts = jnp.swapaxes(gain_parts.reshape(2, -1, norm_gain.shape[0]), 0, 1)
-    gain_out = lax.psum_scatter(gain_parts, EVERY, scatter_dimension=0, tiled=True)[0]
+    small = jnp.transpose(small.reshape(-1, nco, nseq, part), (2, 1, 0, 3))
+    small = scatter_small(small)
+
+    total = feature_restore(jnp.concatenate([gain_one_part, gain_two_part], axis=0))
+    for axis in ("sc", "sx", "co"):
+        total = sum(around(total, axis)[1:], total)
+    total = sum(collect(total)[1:], total)
+    place = (lax.axis_index(("co", "ca", "cb")) * nseq + sx * nsc + sc) * unit
+    gain_out = lax.dynamic_slice_in_dim(total, place, unit, 1)
 
     finish = jnp.concatenate([h_end, ends.astype(F32)], axis=0)
     reach = jnp.where(co == nco - 1, finish[:, :chunk], 0.0)

time: 1270 us -> 948 us (0.75)
  blocking collectives: 219 us -> 0 us
  waiting for transfers between devices: 538 us -> 481 us
  other arithmetic: 94.6 us -> 70.7 us
  matrix products: 179 us -> 160 us
  between operations: 16.6 us -> 3.15 us
  Pallas kernels: 37.5 us -> 50.5 us
    all_gather x3 -> x0, blocking collectives: 146 us -> none  [the longest x1 77.7 us: shards(): vectors = lax.all_gather(vectors, BLOCKS, axis=0)]
    ppermute x34 -> x74, waiting for transfers between devices: 221 us -> 307 us  [shift(): lax.ppermute(value, axis, [(i, (i + step) % count) for i in range(count)])]
    unnamed x1 -> x0, blocking collectives: 73.1 us -> none
    ppermute x16 -> x2, waiting for transfers between devices: 59.3 us -> 9.93 us  [block_shift(): return lax.ppermute(value, BLOCKS, route)]
    unnamed x3 -> x0, waiting for transfers between devices: 43.6 us -> none
    reduce_scatter x1 -> x0, waiting for transfers between devices: 32.2 us -> none  [shards(): lax.psum_scatter(pieces.astype(BF), BLOCKS, scatter_dimension=0, tiled=True)]
    ppermute x16 -> x2, starting transfers between devices: 30 us -> 3.81 us  [block_shift(): return lax.ppermute(value, BLOCKS, route)]
    dot_general x6, matrix products: 79.8 us -> 55.1 us  [times_transpose(): lax.dot_general(left, right, (((1,), (1,)), ((), ())), preferred_element_...]
  transfers between devices with their start and end apart: 77 -> 107, of which waited for: 34 -> 45; matrix products, arithmetic and copies ran while one was open for 22% -> 24% of each run, Pallas kernels for 3% -> 5%
where the time goes in v2:
time: 948 us; the launch traced here: 938 us
  waiting for transfers between devices  481 us (51%)
  matrix products  160 us (17%)
  starting transfers between devices  92.6 us (10%)
  local copies, waits for them, and re-layouts  79.3 us (8%)
  other arithmetic  70.7 us (7%)
  Pallas kernels  50.5 us (5%)
    ppermute x74, waiting for transfers between devices, shift(): lax.ppermute(value, axis, [(i, (i + step) % count) for i in range(count)])  307 us
    ppermute x30, waiting for transfers between devices, peer(): return lax.ppermute(value, PEERS, [(i, i ^ step) for i in range(PEER)])  160 us
    dot_general x6, matrix products, matmul(): return jnp.dot(left, right, preferred_element_type=F32)  57.2 us
    dot_general x6, matrix products, times_transpose(): lax.dot_general(left, right, (((1,), (1,)), ((), ())), preferred_element_...  55.1 us
    ppermute x74, starting transfers between devices, shift(): lax.ppermute(value, axis, [(i, (i + step) % count) for i in range(count)])  51 us
    dot_general x7, matrix products, over_tokens(): lax.dot_general(left, right, (((0,), (0,)), ((), ())), preferred_element_...  48 us
    ppermute x30, starting transfers between devices, peer(): return lax.ppermute(value, PEERS, [(i, i ^ step) for i in range(PEER)])  36.6 us
    unnamed x226, local copies, waits for them, and re-layouts  32.9 us
  transfers between devices with their start and end apart: 107, of which 45 were waited for; matrix products, arithmetic and copies ran while one was open for 24% of the time, Pallas kernels for 5%

profile of v2, /device:TPU:0, one launch (start us, length us, event | category | flops | bytes accessed | tf_op | source)
XLA Modules:
  0.0 938.1 jit_solution(5507212490727172559)
XLA Ops:
  57.2 43.3 %collective-permute-done.15.refs_1_ = bf16[512,640]{1,0:T(8,128)(2,1)} collective-permute-done((bf16[512,640]{1,0:T(8,128)(2,1)}, bf16[512,640]{1,0:T(8,128)(2,1)}, u32[]{:S(2)}, u32[]{:S(2)}) %collective-permute-start.15) | collective-permute-done | bytes 655392 | tf_op jit(solution)/shard_map/ppermute | solution.py:22
  124.8 12.9 %collective-permute-done.16 = bf16[512,1280]{1,0:T(8,128)(2,1)} collective-permute-done((bf16[512,1280]{1,0:T(8,128)(2,1)}, bf16[512,1280]{1,0:T(8,128)(2,1)}, u32[]{:S(2)}, u32[]{:S(2)}) %collective-permute-start.16) | collective-permute-done | bytes 1310752 | tf_op jit(solution)/shard_map/ppermute | solution.py:22
  156.0 9.9 %collective-permute-done.25 = bf16[24,640]{1,0:T(8,128)(2,1)S(1)} collective-permute-done((bf16[24,640]{1,0:T(8,128)(2,1)S(1)}, bf16[24,640]{1,0:T(8,128)(2,1)S(1)}, u32[]{:S(2)}, u32[]{:S(2)}) %collective-permute-start.25) | collective-permute-done | bytes 30752 | tf_op jit(solution)/shard_map/ppermute | solution.py:32
  166.7 9.1 gates.1
  195.1 9.1 collective-permute-done.39
  210.9 15.2 %collective-permute-done.48.refs_1_ = bf16[512,768]{1,0:T(8,128)(2,1)S(1)} collective-permute-done((bf16[512,768]{1,0:T(8,128)(2,1)S(1)}, bf16[512,768]{1,0:T(8,128)(2,1)S(1)}, u32[]{:S(2)}, u32[]{:S(2)}) %collective-permute-start.48) | collective-permute-done | bytes 786464 | tf_op jit(solution)/shard_map/ppermute | solution.py:22
  240.7 8.9 fusion.120
  254.9 20.1 %collective-permute-done.52.refs_1_ = bf16[512,768]{1,0:T(8,128)(2,1)} collective-permute-done((bf16[512,768]{1,0:T(8,128)(2,1)}, bf16[512,768]{1,0:T(8,128)(2,1)}, u32[]{:S(2)}, u32[]{:S(2)}) %collective-permute-start.52) | collective-permute-done | bytes 786464 | tf_op jit(solution)/shard_map/ppermute | solution.py:22
  293.3 19.3 %collective-permute-done.44 = bf16[256,2048]{1,0:T(8,128)(2,1)S(1)} collective-permute-done((bf16[256,2048]{1,0:T(8,128)(2,1)}, bf16[256,2048]{1,0:T(8,128)(2,1)S(1)}, u32[]{:S(2)}, u32[]{:S(2)}) %collective-permute-start.44) | collective-permute-done | bytes 1048608 | tf_op jit(solution)/shard_map/ppermute | solution.py:26
  312.5 21.4 %collective-permute-done.43 = bf16[256,2048]{1,0:T(8,128)(2,1)} collective-permute-done((bf16[256,2048]{1,0:T(8,128)(2,1)}, bf16[256,2048]{1,0:T(8,128)(2,1)}, u32[]{:S(2)}, u32[]{:S(2)}) %collective-permute-start.43) | collective-permute-done | bytes 1048608 | tf_op jit(solution)/shard_map/ppermute | solution.py:26
  343.2 31.2 %collective-permute-done.57 = bf16[1536,512]{1,0:T(8,128)(2,1)S(1)} collective-permute-done((bf16[1536,512]{1,0:T(8,128)(2,1)S(1)}, bf16[1536,512]{1,0:T(8,128)(2,1)S(1)}, u32[]{:S(2)}, u32[]{:S(2)}) %collective-permute-start.57) | collective-permute-done | bytes 1572896 | tf_op jit(solution)/shard_map/ppermute | solution.py:22
  377.2 9.9 %collective-permute-done.46 = bf16[256,2048]{1,0:T(8,128)(2,1)S(1)} collective-permute-done((bf16[256,2048]{1,0:T(8,128)(2,1)S(1)}, bf16[256,2048]{1,0:T(8,128)(2,1)S(1)}, u32[]{:S(2)}, u32[]{:S(2)}) %collective-permute-start.46) | collective-permute-done | bytes 1048608 | tf_op jit(solution)/shard_map/ppermute | solution.py:26
  388.0 11.3 %collective-permute-done.45 = bf16[256,2048]{1,0:T(8,128)(2,1)} collective-permute-done((bf16[256,2048]{1,0:T(8,128)(2,1)S(1)}, bf16[256,2048]{1,0:T(8,128)(2,1)}, u32[]{:S(2)}, u32[]{:S(2)}) %collective-permute-start.45) | collective-permute-done | bytes 1048608 | tf_op jit(solution)/shard_map/ppermute | solution.py:26
  399.3 11.5 %fusion.107 = f32[1024,1536]{1,0:T(8,128)} fusion(bf16[2048,1536]{1,0:T(8,128)(2,1)S(1)} %constant_dynamic-update-slice_fusion.24, bf16[256,2048]{1,0:T(8,128)(2,1)} %collective-permute-done.47, bf16[256,2048]{1,0:T(8,128)(2,1)} %copy-done.80, bf16[256,2048]{1,0:T(8,128)(2,1)} %collective-permute-done.45, bf16[256,2048]{1,0:T(8,128)(2,1)S(1)} %multiply_convert_fusion.3), kind=kOutput, calls=%fused_computation.414 | convolution fusion | flops 6459228160 | bytes 16777216 | tf_op jit(solution)/shard_map/dot_general | solution.py:160
  420.9 17.5 %multiply_convert_fusion.1 = (bf16[1024,1536]{1,0:T(8,128)(2,1)}, bf16[1024,1536]{1,0:T(8,128)(2,1)}, bf16[1024,1536]{1,0:T(8,128)(2,1)}) fusion(f32[1024,1536]{1,0:T(8,128)} %fusion.124, f32[1024,1536]{1,0:T(8,128)} %fusion.107, bf16[512,1536]{1,0:T(8,128)(2,1)} %collective-permute-done.51, bf16[512,1536]{1,0:T(8,128)(2,1)} %copy-done.78, ...), kind=kOutput, calls=%fused_computation.8 | convolution fusion | flops 6522142720 | bytes 32505856 | tf_op jit(solution)/shard_map/dot_general | solution.py:160
  438.4 11.7 %convolution_convert_fusion.2 = bf16[1536,2048]{1,0:T(8,128)(2,1)} fusion(bf16[1024,1536]{1,0:T(8,128)(2,1)} %get-tuple-element.192, bf16[1024,2048]{1,0:T(8,128)(2,1)} %constant_dynamic-update-slice_fusion.16), kind=kOutput, calls=%fused_computation.2 | convolution fusion | flops 6445596672 | bytes 13631488 | tf_op jit(solution)/shard_map/dot_general | solution.py:164
  450.1 10.8 %fusion.125 = f32[1024,2048]{1,0:T(8,128)} fusion(bf16[1024,1536]{1,0:T(8,128)(2,1)S(1)} %copy-done.83, bf16[2048,1536]{1,0:T(8,128)(2,1)} %copy-done.49), kind=kOutput, calls=%fused_computation.431 | convolution fusion | flops 6442450944 | bytes 17825792 | tf_op jit(solution)/shard_map/dot_general | solution.py:168
  461.0 13.6 %fusion.121 = (bf16[1024,2048]{1,0:T(8,128)(2,1)S(1)}, f32[1024,2048]{1,0:T(8,128)}) fusion(f32[1024,2048]{1,0:T(8,128)} %fusion.125, bf16[1024,1536]{1,0:T(8,128)(2,1)} %get-tuple-element.190, bf16[512,1536]{1,0:T(8,128)(2,1)} %collective-permute-done.51, bf16[512,1536]{1,0:T(8,128)(2,1)} %copy-done.78, bf16[512,1536]{1,0:T(8,128)(2,1)} %collective-permute-done.49, ...), kind=kOutput, calls=%fused_computation.427 | convolution fusion | flops 6471811072 | bytes 30408704 | tf_op jit(solution)/shard_map/dot_general | solution.py:168
  488.9 32.4 %collective-permute-done.60 = bf16[256,2048]{1,0:T(8,128)(2,1)S(1)} collective-permute-done((bf16[256,2048]{1,0:T(8,128)(2,1)S(1)}, bf16[256,2048]{1,0:T(8,128)(2,1)S(1)}, u32[]{:S(2)}, u32[]{:S(2)}) %collective-permute-start.60) | collective-permute-done | bytes 1048608 | tf_op jit(solution)/shard_map/ppermute | solution.py:26
  527.7 9.2 convolution_convert_fusion
  543.7 10.7 %collective-permute-done.65 = bf16[256,2048]{1,0:T(8,128)(2,1)S(1)} collective-permute-done((bf16[256,2048]{1,0:T(8,128)(2,1)S(1)}, bf16[256,2048]{1,0:T(8,128)(2,1)S(1)}, u32[]{:S(2)}, u32[]{:S(2)}) %collective-permute-start.65) | collective-permute-done | bytes 1048608 | tf_op jit(solution)/shard_map/ppermute | solution.py:26
  555.7 11.1 %convolution_convert_fusion.3 = bf16[1024,2048]{1,0:T(8,128)(2,1)} fusion(bf16[1024,1536]{1,0:T(8,128)(2,1)S(1)} %copy-done.84, bf16[1536,2048]{1,0:T(8,128)(2,1)} %copy-done.48), kind=kOutput, calls=%fused_computation.20 | convolution fusion | flops 6444548096 | bytes 13631488 | tf_op jit(solution)/shard_map/dot_general | solution.py:160
  593.5 19.9 %collective-permute-done.67 = bf16[1536,512]{1,0:T(8,128)(2,1)S(1)} collective-permute-done((bf16[1536,512]{1,0:T(8,128)(2,1)S(1)}, bf16[1536,512]{1,0:T(8,128)(2,1)S(1)}, u32[]{:S(2)}, u32[]{:S(2)}) %collective-permute-start.67) | collective-permute-done | bytes 1572896 | tf_op jit(solution)/shard_map/ppermute | solution.py:22
  662.7 13.9 %grads.1 = (bf16[4,256,1280]{2,1,0:T(8,128)(2,1)}, bf16[4,256,640]{2,1,0:T(8,128)(2,1)}, f32[24,640]{1,0:T(8,128)}, f32[24,640]{1,0:T(8,128)}, f32[64,640]{1,0:T(8,128)}, /*index=5*/f32[8,640]{1,0:T(8,128)}) custom-call(s32[1]{0:T(128)} %bitcast.2.ci, f32[4,256,640]{2,1,0:T(8,128)} %get-tuple-element.85.dh_ref, f32[4,256,640]{2,1,0:T(8,128)} %get-tuple-element.68.a_ref, ...), custom_call_target="tpu_custom_call" | custom-call | tf_op jit(solution)/shard_map/grads/pallas_call | solution.py:500
  720.4 21.9 %collective-permute-done.102 = bf16[1,160,160]{2,1,0:T(8,128)(2,1)S(1)} collective-permute-done((bf16[1,160,160]{2,1,0:T(8,128)(2,1)S(1)}, bf16[1,160,160]{2,1,0:T(8,128)(2,1)S(1)}, u32[]{:S(2)}, u32[]{:S(2)}) %collective-permute-start.102) | collective-permute-done | bytes 51232 | tf_op jit(solution)/shard_map/ppermute | solution.py:22
  754.3 35.3 %collective-permute-done.77 = bf16[256,2048]{1,0:T(8,128)(2,1)S(1)} collective-permute-done((bf16[256,2048]{1,0:T(8,128)(2,1)S(1)}, bf16[256,2048]{1,0:T(8,128)(2,1)S(1)}, u32[]{:S(2)}, u32[]{:S(2)}) %collective-permute-start.77) | collective-permute-done | bytes 1048608 | tf_op jit(solution)/shard_map/ppermute | solution.py:26
  801.4 32.4 %collective-permute-done.95 = bf16[512,768]{1,0:T(8,128)(2,1)S(1)} collective-permute-done((bf16[512,768]{1,0:T(8,128)(2,1)S(1)}, bf16[512,768]{1,0:T(8,128)(2,1)S(1)}, u32[]{:S(2)}, u32[]{:S(2)}) %collective-permute-start.95) | collective-permute-done | bytes 786464 | tf_op jit(solution)/shard_map/ppermute | solution.py:22
  838.4 14.3 %collective-permute-done.91 = bf16[640,512]{1,0:T(8,128)(2,1)S(1)} collective-permute-done((bf16[640,512]{1,0:T(8,128)(2,1)S(1)}, bf16[640,512]{1,0:T(8,128)(2,1)S(1)}, u32[]{:S(2)}, u32[]{:S(2)}) %collective-permute-start.91) | collective-permute-done | bytes 655392 | tf_op jit(solution)/shard_map/ppermute | solution.py:22
  853.9 19.4 %collective-permute-done.96 = bf16[512,768]{1,0:T(8,128)(2,1)S(1)} collective-permute-done((bf16[512,768]{1,0:T(8,128)(2,1)S(1)}, bf16[512,768]{1,0:T(8,128)(2,1)S(1)}, u32[]{:S(2)}, u32[]{:S(2)}) %collective-permute-start.96) | collective-permute-done | bytes 786464 | tf_op jit(solution)/shard_map/ppermute | solution.py:22
  875.0 16.3 %collective-permute-done.97 = bf16[320,512]{1,0:T(8,128)(2,1)S(1)} collective-permute-done((bf16[320,512]{1,0:T(8,128)(2,1)S(1)}, bf16[320,512]{1,0:T(8,128)(2,1)S(1)}, u32[]{:S(2)}, u32[]{:S(2)}) %collective-permute-start.97) | collective-permute-done | bytes 327712 | tf_op jit(solution)/shard_map/ppermute | solution.py:22
  900.0 13.3 %collective-permute-done.82 = f32[2,2048]{1,0:T(2,128)S(1)} collective-permute-done((f32[2,2048]{1,0:T(2,128)S(1)}, f32[2,2048]{1,0:T(2,128)S(1)}, u32[]{:S(2)}, u32[]{:S(2)}) %collective-permute-start.82) | collective-permute-done | bytes 16416 | tf_op jit(solution)/shard_map/ppermute | solution.py:22
  921.3 15.3 %collective-permute-done.99 = bf16[512,320]{1,0:T(8,128)(2,1)S(1)} collective-permute-done((bf16[512,320]{1,0:T(8,128)(2,1)S(1)}, bf16[512,320]{1,0:T(8,128)(2,1)S(1)}, u32[]{:S(2)}, u32[]{:S(2)}) %collective-permute-start.99) | collective-permute-done | bytes 327712 | tf_op jit(solution)/shard_map/ppermute | solution.py:22
  (622 shorter events, 382.7 us)
Async XLA Ops:
  39.2 79.8 %collective-permute-start.12 = (bf16[256,2048]{1,0:T(8,128)(2,1)S(1)}, bf16[256,2048]{1,0:T(8,128)(2,1)S(1)}, u32[]{:S(2)}, u32[]{:S(2)}) collective-permute-start(bf16[256,2048]{1,0:T(8,128)(2,1)S(1)} %get-tuple-element.189), channel_id=1, source_target_pairs={{0,3},{1,2},{2,1},{3,0},{4,7},{5,6},{6,5},{7,4},{8,11},{9,10},{10,... | collective-permute-start | bytes 3145736 | tf_op jit(solution)/shard_map/ppermute | solution.py:26
  43.0 76.1 %collective-permute-start.11 = (bf16[256,2048]{1,0:T(8,128)(2,1)S(1)}, bf16[256,2048]{1,0:T(8,128)(2,1)S(1)}, u32[]{:S(2)}, u32[]{:S(2)}) collective-permute-start(bf16[256,2048]{1,0:T(8,128)(2,1)S(1)} %get-tuple-element.189), channel_id=1, source_target_pairs={{0,2},{1,3},{2,0},{3,1},{4,6},{5,7},{6,4},{7,5},{8,10},{9,11},{10,... | collective-permute-start | bytes 3145736 | tf_op jit(solution)/shard_map/ppermute | solution.py:26
  47.5 53.0 %collective-permute-start.15 = (bf16[512,640]{1,0:T(8,128)(2,1)}, bf16[512,640]{1,0:T(8,128)(2,1)}, u32[]{:S(2)}, u32[]{:S(2)}) collective-permute-start(bf16[512,640]{1,0:T(8,128)(2,1)} %pad_maximum_fusion.10.refs_0_), channel_id=1, source_target_pairs={{0,4},{4,0},{1,5},{5,1},{2,6},{6,2},{3,7},{7,3},{8,12},{12,8},{9,1... | collective-permute-start | bytes 1966088 | tf_op jit(solution)/shard_map/ppermute | solution.py:22
  54.4 64.6 %collective-permute-start.10 = (bf16[256,2048]{1,0:T(8,128)(2,1)S(1)}, bf16[256,2048]{1,0:T(8,128)(2,1)}, u32[]{:S(2)}, u32[]{:S(2)}) collective-permute-start(bf16[256,2048]{1,0:T(8,128)(2,1)S(1)} %get-tuple-element.189), channel_id=1, source_target_pairs={{0,1},{1,0},{2,3},{3,2},{4,5},{5,4},{6,7},{7,6},{8,9},{9,8},{10,11... | collective-permute-start | bytes 3145736 | tf_op jit(solution)/shard_map/ppermute | solution.py:26
  56.0 48.1 %collective-permute-start.31 = (bf16[160,160]{1,0:T(8,128)(2,1)S(1)}, bf16[160,160]{1,0:T(8,128)(2,1)S(1)}, u32[]{:S(2)}, u32[]{:S(2)}) collective-permute-start(bf16[160,160]{1,0:T(8,128)(2,1)S(1)} %collective-permute-done.30), channel_id=1, source_target_pairs={{0,8},{8,0},{1,9},{9,1},{2,10},{10,2},{3,11},{11,3},{4,12},{12,4},... | collective-permute-start | bytes 153608 | tf_op jit(solution)/shard_map/ppermute | solution.py:22
  119.1 87.5 %collective-permute-start.37 = (bf16[256,2048]{1,0:T(8,128)(2,1)}, bf16[256,2048]{1,0:T(8,128)(2,1)}, u32[]{:S(2)}, u32[]{:S(2)}) collective-permute-start(bf16[256,2048]{1,0:T(8,128)(2,1)} %pad_maximum_fusion.9), channel_id=1, source_target_pairs={{0,3},{1,2},{2,1},{3,0},{4,7},{5,6},{6,5},{7,4},{8,11},{9,10},{10,... | collective-permute-start | bytes 3145736 | tf_op jit(solution)/shard_map/ppermute | solution.py:26
  119.2 85.0 %collective-permute-start.36 = (bf16[256,2048]{1,0:T(8,128)(2,1)}, bf16[256,2048]{1,0:T(8,128)(2,1)}, u32[]{:S(2)}, u32[]{:S(2)}) collective-permute-start(bf16[256,2048]{1,0:T(8,128)(2,1)} %pad_maximum_fusion.9), channel_id=1, source_target_pairs={{0,2},{1,3},{2,0},{3,1},{4,6},{5,7},{6,4},{7,5},{8,10},{9,11},{10,... | collective-permute-start | bytes 3145736 | tf_op jit(solution)/shard_map/ppermute | solution.py:26
  121.7 68.4 %collective-permute-start.35 = (bf16[256,2048]{1,0:T(8,128)(2,1)}, bf16[256,2048]{1,0:T(8,128)(2,1)}, u32[]{:S(2)}, u32[]{:S(2)}) collective-permute-start(bf16[256,2048]{1,0:T(8,128)(2,1)} %pad_maximum_fusion.9), channel_id=1, source_target_pairs={{0,1},{1,0},{2,3},{3,2},{4,5},{5,4},{6,7},{7,6},{8,9},{9,8},{10,11... | collective-permute-start | bytes 3145736 | tf_op jit(solution)/shard_map/ppermute | solution.py:26
  143.2 88.5 %collective-permute-start.40 = (bf16[640,512]{1,0:T(8,128)(2,1)}, bf16[640,512]{1,0:T(8,128)(2,1)S(1)}, u32[]{:S(2)}, u32[]{:S(2)}) collective-permute-start(bf16[640,512]{1,0:T(8,128)(2,1)} %pad_maximum_fusion.12), channel_id=1, source_target_pairs={{0,8},{8,0},{1,9},{9,1},{2,10},{10,2},{3,11},{11,3},{4,12},{12,4},... | collective-permute-start | bytes 1966088 | tf_op jit(solution)/shard_map/ppermute | solution.py:22
  230.6 48.0 %collective-permute-start.49 = (bf16[512,1536]{1,0:T(8,128)(2,1)}, bf16[512,1536]{1,0:T(8,128)(2,1)}, u32[]{:S(2)}, u32[]{:S(2)}) collective-permute-start(bf16[512,1536]{1,0:T(8,128)(2,1)} %join.4), channel_id=1, source_target_pairs={{0,16},{16,0},{1,17},{17,1},{2,18},{18,2},{3,19},{19,3},{4,20},{20... | collective-permute-start | bytes 4718600 | tf_op jit(solution)/shard_map/ppermute | solution.py:22
  252.5 60.1 %collective-permute-start.44 = (bf16[256,2048]{1,0:T(8,128)(2,1)}, bf16[256,2048]{1,0:T(8,128)(2,1)S(1)}, u32[]{:S(2)}, u32[]{:S(2)}) collective-permute-start(bf16[256,2048]{1,0:T(8,128)(2,1)} %get-tuple-element.203), channel_id=1, source_target_pairs={{0,3},{1,2},{2,1},{3,0},{4,7},{5,6},{6,5},{7,4},{8,11},{9,10},{10,... | collective-permute-start | bytes 3145736 | tf_op jit(solution)/shard_map/ppermute | solution.py:26
  254.7 79.2 %collective-permute-start.43 = (bf16[256,2048]{1,0:T(8,128)(2,1)}, bf16[256,2048]{1,0:T(8,128)(2,1)}, u32[]{:S(2)}, u32[]{:S(2)}) collective-permute-start(bf16[256,2048]{1,0:T(8,128)(2,1)} %get-tuple-element.204), channel_id=1, source_target_pairs={{0,2},{1,3},{2,0},{3,1},{4,6},{5,7},{6,4},{7,5},{8,10},{9,11},{10,... | collective-permute-start | bytes 3145736 | tf_op jit(solution)/shard_map/ppermute | solution.py:26
  278.6 59.0 %collective-permute-start.53 = (bf16[512,1536]{1,0:T(8,128)(2,1)}, bf16[512,1536]{1,0:T(8,128)(2,1)}, u32[]{:S(2)}, u32[]{:S(2)}) collective-permute-start(bf16[512,1536]{1,0:T(8,128)(2,1)} %join.5), channel_id=1, source_target_pairs={{0,16},{16,0},{1,17},{17,1},{2,18},{18,2},{3,19},{19,3},{4,20},{20... | collective-permute-start | bytes 4718600 | tf_op jit(solution)/shard_map/ppermute | solution.py:22
  287.4 50.0 %collective-permute-start.56 = (bf16[768,512]{1,0:T(8,128)(2,1)}, bf16[768,512]{1,0:T(8,128)(2,1)S(1)}, u32[]{:S(2)}, u32[]{:S(2)}) collective-permute-start(bf16[768,512]{1,0:T(8,128)(2,1)} %param.28), channel_id=1, source_target_pairs={{0,4},{4,0},{1,5},{5,1},{2,6},{6,2},{3,7},{7,3},{8,12},{12,8},{9,1... | collective-permute-start | bytes 2359304 | tf_op jit(solution)/shard_map/ppermute | solution.py:22
  341.1 46.0 %collective-permute-start.46 = (bf16[256,2048]{1,0:T(8,128)(2,1)S(1)}, bf16[256,2048]{1,0:T(8,128)(2,1)S(1)}, u32[]{:S(2)}, u32[]{:S(2)}) collective-permute-start(bf16[256,2048]{1,0:T(8,128)(2,1)S(1)} %multiply_convert_fusion.3), channel_id=1, source_target_pairs={{0,2},{1,3},{2,0},{3,1},{4,6},{5,7},{6,4},{7,5},{8,10},{9,11},{10,... | collective-permute-start | bytes 3145736 | tf_op jit(solution)/shard_map/ppermute | solution.py:26
  376.4 44.5 %collective-permute-start.51 = (bf16[512,1536]{1,0:T(8,128)(2,1)}, bf16[512,1536]{1,0:T(8,128)(2,1)}, u32[]{:S(2)}, u32[]{:S(2)}) collective-permute-start(bf16[512,1536]{1,0:T(8,128)(2,1)} %collective-permute-done.49), channel_id=1, source_target_pairs={{0,8},{8,0},{1,9},{9,1},{2,10},{10,2},{3,11},{11,3},{4,12},{12,4},... | collective-permute-start | bytes 4718600 | tf_op jit(solution)/shard_map/ppermute | solution.py:22
  474.9 46.4 %collective-permute-start.60 = (bf16[256,2048]{1,0:T(8,128)(2,1)S(1)}, bf16[256,2048]{1,0:T(8,128)(2,1)S(1)}, u32[]{:S(2)}, u32[]{:S(2)}) collective-permute-start(bf16[256,2048]{1,0:T(8,128)(2,1)S(1)} %get-tuple-element.199), channel_id=1, source_target_pairs={{0,1},{1,0},{2,3},{3,2},{4,5},{5,4},{6,7},{7,6},{8,9},{9,8},{10,11... | collective-permute-start | bytes 3145736 | tf_op jit(solution)/shard_map/ppermute | solution.py:26
  476.2 45.1 %collective-permute-start.62 = (bf16[256,2048]{1,0:T(8,128)(2,1)S(1)}, bf16[256,2048]{1,0:T(8,128)(2,1)S(1)}, u32[]{:S(2)}, u32[]{:S(2)}) collective-permute-start(bf16[256,2048]{1,0:T(8,128)(2,1)S(1)} %get-tuple-element.200), channel_id=1, source_target_pairs={{0,3},{1,2},{2,1},{3,0},{4,7},{5,6},{6,5},{7,4},{8,11},{9,10},{10,... | collective-permute-start | bytes 3145736 | tf_op jit(solution)/shard_map/ppermute | solution.py:26
  476.2 46.3 %collective-permute-start.61 = (bf16[256,2048]{1,0:T(8,128)(2,1)S(1)}, bf16[256,2048]{1,0:T(8,128)(2,1)S(1)}, u32[]{:S(2)}, u32[]{:S(2)}) collective-permute-start(bf16[256,2048]{1,0:T(8,128)(2,1)S(1)} %get-tuple-element.201), channel_id=1, source_target_pairs={{0,2},{1,3},{2,0},{3,1},{4,6},{5,7},{6,4},{7,5},{8,10},{9,11},{10,... | collective-permute-start | bytes 3145736 | tf_op jit(solution)/shard_map/ppermute | solution.py:26
  480.5 96.3 %collective-permute-start.66 = (bf16[1536,1024]{1,0:T(8,128)(2,1)}, bf16[1536,1024]{1,0:T(8,128)(2,1)}, u32[]{:S(2)}, u32[]{:S(2)}) collective-permute-start(bf16[1536,1024]{1,0:T(8,128)(2,1)} %slice.693), channel_id=1, source_target_pairs={{0,8},{8,0},{1,9},{9,1},{2,10},{10,2},{3,11},{11,3},{4,12},{12,4},... | collective-permute-start | bytes 9437192 | tf_op jit(solution)/shard_map/ppermute | solution.py:22
  540.8 47.3 %collective-permute-start.69 = (bf16[1024,1536]{1,0:T(8,128)(2,1)}, bf16[1024,1536]{1,0:T(8,128)(2,1)}, u32[]{:S(2)}, u32[]{:S(2)}) collective-permute-start(bf16[1024,1536]{1,0:T(8,128)(2,1)} %slice.699), channel_id=1, source_target_pairs={{0,8},{8,0},{1,9},{9,1},{2,10},{10,2},{3,11},{11,3},{4,12},{12,4},... | collective-permute-start | bytes 9437192 | tf_op jit(solution)/shard_map/ppermute | solution.py:22
  653.0 90.8 %collective-permute-start.70 = (bf16[256,2048]{1,0:T(8,128)(2,1)}, bf16[256,2048]{1,0:T(8,128)(2,1)}, u32[]{:S(2)}, u32[]{:S(2)}) collective-permute-start(bf16[256,2048]{1,0:T(8,128)(2,1)} %get-tuple-element.196), channel_id=1, source_target_pairs={{0,1},{1,0},{2,3},{3,2},{4,5},{5,4},{6,7},{7,6},{8,9},{9,8},{10,11... | collective-permute-start | bytes 3145736 | tf_op jit(solution)/shard_map/ppermute | solution.py:26
  653.7 95.3 %collective-permute-start.72 = (bf16[256,2048]{1,0:T(8,128)(2,1)}, bf16[256,2048]{1,0:T(8,128)(2,1)}, u32[]{:S(2)}, u32[]{:S(2)}) collective-permute-start(bf16[256,2048]{1,0:T(8,128)(2,1)} %get-tuple-element.197), channel_id=1, source_target_pairs={{0,3},{1,2},{2,1},{3,0},{4,7},{5,6},{6,5},{7,4},{8,11},{9,10},{10,... | collective-permute-start | bytes 3145736 | tf_op jit(solution)/shard_map/ppermute | solution.py:26
  654.4 94.6 %collective-permute-start.71 = (bf16[256,2048]{1,0:T(8,128)(2,1)}, bf16[256,2048]{1,0:T(8,128)(2,1)}, u32[]{:S(2)}, u32[]{:S(2)}) collective-permute-start(bf16[256,2048]{1,0:T(8,128)(2,1)} %get-tuple-element.198), channel_id=1, source_target_pairs={{0,2},{1,3},{2,0},{3,1},{4,6},{5,7},{6,4},{7,5},{8,10},{9,11},{10,... | collective-permute-start | bytes 3145736 | tf_op jit(solution)/shard_map/ppermute | solution.py:26
  742.3 47.3 %collective-permute-start.77 = (bf16[256,2048]{1,0:T(8,128)(2,1)S(1)}, bf16[256,2048]{1,0:T(8,128)(2,1)S(1)}, u32[]{:S(2)}, u32[]{:S(2)}) collective-permute-start(bf16[256,2048]{1,0:T(8,128)(2,1)S(1)} %get-tuple-element.193), channel_id=1, source_target_pairs={{0,1},{1,0},{2,3},{3,2},{4,5},{5,4},{6,7},{7,6},{8,9},{9,8},{10,11... | collective-permute-start | bytes 3145736 | tf_op jit(solution)/shard_map/ppermute | solution.py:26
  743.8 45.8 %collective-permute-start.79 = (bf16[256,2048]{1,0:T(8,128)(2,1)S(1)}, bf16[256,2048]{1,0:T(8,128)(2,1)S(1)}, u32[]{:S(2)}, u32[]{:S(2)}) collective-permute-start(bf16[256,2048]{1,0:T(8,128)(2,1)S(1)} %get-tuple-element.194), channel_id=1, source_target_pairs={{0,3},{1,2},{2,1},{3,0},{4,7},{5,6},{6,5},{7,4},{8,11},{9,10},{10,... | collective-permute-start | bytes 3145736 | tf_op jit(solution)/shard_map/ppermute | solution.py:26
  743.8 47.7 %collective-permute-start.78 = (bf16[256,2048]{1,0:T(8,128)(2,1)S(1)}, bf16[256,2048]{1,0:T(8,128)(2,1)S(1)}, u32[]{:S(2)}, u32[]{:S(2)}) collective-permute-start(bf16[256,2048]{1,0:T(8,128)(2,1)S(1)} %get-tuple-element.195), channel_id=1, source_target_pairs={{0,2},{1,3},{2,0},{3,1},{4,6},{5,7},{6,4},{7,5},{8,10},{9,11},{10,... | collective-permute-start | bytes 3145736 | tf_op jit(solution)/shard_map/ppermute | solution.py:26
  749.0 50.5 %collective-permute-start.88 = (bf16[640,1024]{1,0:T(8,128)(2,1)}, bf16[640,1024]{1,0:T(8,128)(2,1)}, u32[]{:S(2)}, u32[]{:S(2)}) collective-permute-start(bf16[640,1024]{1,0:T(8,128)(2,1)} %slice.733), channel_id=1, source_target_pairs={{0,8},{8,0},{1,9},{9,1},{2,10},{10,2},{3,11},{11,3},{4,12},{12,4},... | collective-permute-start | bytes 3932168 | tf_op jit(solution)/shard_map/ppermute | solution.py:22
  749.0 46.2 %collective-permute-start.89 = (bf16[512,1536]{1,0:T(8,128)(2,1)S(1)}, bf16[512,1536]{1,0:T(8,128)(2,1)S(1)}, u32[]{:S(2)}, u32[]{:S(2)}) collective-permute-start(bf16[512,1536]{1,0:T(8,128)(2,1)S(1)} %copy-done.37), channel_id=1, source_target_pairs={{0,16},{16,0},{1,17},{17,1},{2,18},{18,2},{3,19},{19,3},{4,20},{20... | collective-permute-start | bytes 4718600 | tf_op jit(solution)/shard_map/ppermute | solution.py:22
  789.5 48.6 %collective-permute-start.87 = (bf16[1024,640]{1,0:T(8,128)(2,1)}, bf16[1024,640]{1,0:T(8,128)(2,1)S(1)}, u32[]{:S(2)}, u32[]{:S(2)}) collective-permute-start(bf16[1024,640]{1,0:T(8,128)(2,1)} %slice.731), channel_id=1, source_target_pairs={{0,8},{8,0},{1,9},{9,1},{2,10},{10,2},{3,11},{11,3},{4,12},{12,4},... | collective-permute-start | bytes 3932168 | tf_op jit(solution)/shard_map/ppermute | solution.py:22
  789.6 85.2 %collective-permute-start.86 = (bf16[1024,640]{1,0:T(8,128)(2,1)}, bf16[1024,640]{1,0:T(8,128)(2,1)S(1)}, u32[]{:S(2)}, u32[]{:S(2)}) collective-permute-start(bf16[1024,640]{1,0:T(8,128)(2,1)} %slice.729), channel_id=1, source_target_pairs={{0,8},{8,0},{1,9},{9,1},{2,10},{10,2},{3,11},{11,3},{4,12},{12,4},... | collective-permute-start | bytes 3932168 | tf_op jit(solution)/shard_map/ppermute | solution.py:22
  836.9 57.4 %collective-permute-start.81 = (f32[2,2048]{1,0:T(2,128)S(1)}, f32[2,2048]{1,0:T(2,128)S(1)}, u32[]{:S(2)}, u32[]{:S(2)}) collective-permute-start(f32[2,2048]{1,0:T(2,128)S(1)} %fusion.155), channel_id=1, source_target_pairs={{0,16},{16,0},{1,17},{17,1},{2,18},{18,2},{3,19},{19,3},{4,20},{20... | collective-permute-start | bytes 49160 | tf_op jit(solution)/shard_map/ppermute | solution.py:22
  (167 other events, 3161.8 us)

commit v3 on v2

v3 whole, which is shorter than its diff:
```python
import functools

import jax
import jax.numpy as jnp
from jax import lax
from jax.experimental import pallas as pl
from jax.experimental.pallas import tpu as pltpu
from jax.sharding import Mesh
from jax.sharding import PartitionSpec as P

BF = jnp.bfloat16
F32 = jnp.float32
BLOCKS = ("sx", "sc", "co")
PEERS = ("ca", "cb")
PEER = 4
GELU_C = 0.7978845608028654
GELU_K = 0.044715


def shift(value, axis, step):
    count = lax.axis_size(axis)
    return lax.ppermute(value, axis, [(i, (i + step) % count) for i in range(count)])


def block_shift(value, step):
    count = lax.axis_size(BLOCKS)
    route = [(i, i + step) for i in range(count) if 0 <= i + step < count]
    return lax.ppermute(value, BLOCKS, route)


def peer(value, step):
    return lax.ppermute(value, PEERS, [(i, i ^ step) for i in range(PEER)])


def before_last(value):
    count = lax.axis_size(BLOCKS)
    return sum(
        lax.ppermute(
            value,
            BLOCKS + PEERS,
            [((b - 1) * PEER + PEER - 1, b * PEER + k) for b in range(1, count)],
        )
        for k in range(PEER)
    )


def peer_rows(value, hold=()):
    near = peer(value, 1)
    far = peer(after(value, *hold), 2)
    return [value, near, far, peer(after(far, near), 1)]


def peer_sum(terms, hold=()):
    mine, near, far, across = terms
    across = peer(across, 1)
    near = peer(after(near, across), 1)
    relay = (far.astype(F32) + across.astype(F32)).astype(BF)
    far = peer(after(relay, *hold), 2)
    return mine.astype(F32) + near.astype(F32) + far.astype(F32)


def after(value, *done):
    return lax.optimization_barrier((value, *done))[0]


def around(value, axis):
    return [value] + [shift(value, axis, r) for r in range(1, lax.axis_size(axis))]


def over_die(items):
    return items + [shift(item, "sc", r) for r in range(1, lax.axis_size("sc")) for item in items]


def cut(value, count, axis):
    size = value.shape[axis] // count
    return [lax.slice_in_dim(value, r * size, (r + 1) * size, axis=axis) for r in range(count)]


def around_back(parts, axis):
    return parts[:1] + [shift(part, axis, -1 - r) for r, part in enumerate(parts[1:])]


def sum_around(parts, axis, hold=()):
    total = parts[0].astype(F32)
    for r in range(1, len(parts)):
        term = shift(parts[r].astype(BF), axis, -r)
        total = total + after(term, *hold).astype(F32)
    return total


def chunk_roll(value, step):
    count = lax.axis_size("co")
    step = step % count
    if step == 0:
        return value
    width = value.shape[-1] // count
    cut = width * (count - step)
    return jnp.concatenate([value[..., cut:], value[..., :cut]], axis=-1)


def feature_order(value):
    nsx, nsc = lax.axis_size("sx"), lax.axis_size("sc")
    sx, sc = lax.axis_index("sx"), lax.axis_index("sc")
    width = value.shape[-1] // (nsx * nsc)
    parts = []
    for rc in range(nsc):
        for rx in range(nsx):
            owner = lax.rem(sx - rx + nsx, nsx) * nsc + lax.rem(sc - rc + nsc, nsc)
            parts.append(lax.dynamic_slice_in_dim(value, owner * width, width, value.ndim - 1))
    return jnp.concatenate(parts, axis=-1)


def feature_restore(value):
    nsx, nsc = lax.axis_size("sx"), lax.axis_size("sc")
    sx, sc = lax.axis_index("sx"), lax.axis_index("sc")
    width = value.shape[-1] // (nsx * nsc)
    parts = []
    for owner in range(nsx * nsc):
        rx = lax.rem(sx - owner // nsc + nsx, nsx)
        rc = lax.rem(sc - owner % nsc + nsc, nsc)
        parts.append(
            lax.dynamic_slice_in_dim(value, (rc * nsx + rx) * width, width, value.ndim - 1)
        )
    return jnp.concatenate(parts, axis=-1)


def join_kernel(groups, *refs):
    out = refs[-1]
    width = refs[0].shape[1] // groups
    at = 0
    for g in range(groups):
        for ref in refs[:-1]:
            out[:, at : at + width] = ref[:, g * width : (g + 1) * width]
            at += width


def join_columns(items, groups):
    rows, width = items[0].shape
    block = rows // 2
    return pl.pallas_call(
        functools.partial(join_kernel, groups),
        out_shape=jax.ShapeDtypeStruct((rows, width * len(items)), items[0].dtype),
        grid=(2,),
        in_specs=[pl.BlockSpec((block, width), lambda i: (i, 0))] * len(items),
        out_specs=pl.BlockSpec((block, width * len(items)), lambda i: (i, 0)),
        name="join",
    )(*items)


def compose(earlier, later, rows):
    decay, state = later[:rows], later[rows:]
    return jnp.concatenate([earlier[:rows] * decay, decay * earlier[rows:] + state], axis=0)


def other_blocks(summary, rows, backward):
    width = summary.shape[-1]
    empty = jnp.concatenate([jnp.ones((rows, width), F32), jnp.zeros((rows, width), F32)], axis=0)
    outer = empty
    for axis in ("co", "sc", "sx"):
        count, mine = lax.axis_size(axis), lax.axis_index(axis)
        items = around(summary, axis)
        if axis == "co":
            items = [chunk_roll(item, r) for r, item in enumerate(items)]
        if count == 2:
            mate = items[1]
            ahead = (mine == 0) if backward else (mine == 1)
            joined = compose(mate, summary, rows)
            outer = jnp.where(ahead, compose(mate, outer, rows), outer)
            summary = jnp.where(ahead, joined, compose(summary, mate, rows))
        else:
            table = jnp.stack(items)
            total, inner = empty, empty
            for place in reversed(range(count)) if backward else range(count):
                item = table[lax.rem(mine - place + count, count)]
                total = compose(total, item, rows)
                ahead = (place > mine) if backward else (place < mine)
                inner = jnp.where(ahead, compose(inner, item, rows), inner)
            outer = compose(inner, outer, rows)
            summary = total
    return outer


def matmul(left, right):
    return jnp.dot(left, right, preferred_element_type=F32)


def over_tokens(left, right):
    return lax.dot_general(left, right, (((0,), (0,)), ((), ())), preferred_element_type=F32)


def times_transpose(left, right):
    return lax.dot_general(left, right, (((1,), (1,)), ((), ())), preferred_element_type=F32)


def weight_grad(left, right, halved):
    if halved == 0:
        halves = [over_tokens(half, right).astype(BF) for half in cut(left, 2, 1)]
    else:
        halves = [over_tokens(left, half).astype(BF) for half in cut(right, 2, 1)]
    return [lax.optimization_barrier(half) for half in halves]


def gelu_parts(value):
    square = value * value
    wave = jnp.tanh(GELU_C * (value + GELU_K * value * square))
    half = 0.5 * (1.0 + wave)
    slope = half + 0.5 * value * (1.0 - wave * wave) * (GELU_C * (1.0 + 3.0 * GELU_K * square))
    return value * half, slope


def minus_expm1(value):
    series = 1.0 + value * (1.0 / 7.0)
    for order in (6.0, 5.0, 4.0, 3.0, 2.0):
        series = 1.0 + value * (1.0 / order) * series
    return -jnp.where(value > -0.3, value * series, jnp.exp(value) - 1.0)


def decay_terms(rate, soft):
    log_decay = -8.0 * rate * soft
    return jnp.exp(log_decay), jnp.sqrt(minus_expm1(2.0 * log_decay))


def rows_times(values, pieces, columns=slice(None)):
    total = None
    size = pieces[0].shape[0]
    for i, piece in enumerate(pieces):
        term = matmul(values[:, i * size : (i + 1) * size], piece[:, columns])
        total = term if total is None else total + term
    return total


def columns_times(values, pieces):
    total = None
    size = pieces[0].shape[1]
    for i, piece in enumerate(pieces):
        term = times_transpose(values[:, i * size : (i + 1) * size], piece[...])
        total = term if total is None else total + term
    return total


def gates_kernel(
    count, here, x_ref, border_ref, gain_ref, tail_ref, gate_ref, vec_ref, *refs
):
    pieces, refs = refs[:count], refs[count:]
    n_ref, u_ref, v_ref, ra_ref, ri_ref, a_ref, e_ref, before_ref, end_ref, pad, held = refs
    step = pl.program_id(0)
    rows = held.shape[0] // 2
    size, width = u_ref.shape
    lag = tail_ref.shape[0]

    def normal(value):
        value = value.astype(F32)
        root = lax.rsqrt(jnp.mean(value * value, axis=-1, keepdims=True) + 1e-06)
        return (value * root * gain_ref[...]).astype(BF)

    @pl.when(step == 0)
    def _():
        edge = rows_times(normal(border_ref[...]), pieces).astype(BF).astype(F32)
        pad[0:lag, :] = jnp.where(here[1] == 1, tail_ref[...].astype(BF).astype(F32), edge)
        held[0:rows, :] = jnp.ones((rows, width), F32)
        held[rows:, :] = jnp.zeros((rows, width), F32)

    @pl.when(step > 0)
    def _():
        pad[0:lag, :] = pad[size : size + lag, :]

    low = normal(x_ref[...])
    n_ref[...] = low
    conv_in = rows_times(low, pieces).astype(BF)
    u_ref[...] = conv_in
    pad[lag:, :] = conv_in.astype(F32)
    before_ref[...] = pad[0:lag, :]
    taps = lag // rows + 1
    conv = vec_ref[taps : taps + 1, :] + vec_ref[0:1, :] * pad[lag : lag + size, :]
    for k in range(1, taps):
        conv = conv + vec_ref[k : k + 1, :] * pad[lag - rows * k : lag - rows * k + size, :]
    low = conv.astype(BF)
    v_ref[...] = low
    pre = jnp.dot(low, gate_ref[...], preferred_element_type=F32)
    ra = jax.nn.sigmoid(pre[:, :width] + vec_ref[taps + 1 : taps + 2, :])
    ri = jax.nn.sigmoid(pre[:, width:] + vec_ref[taps + 2 : taps + 3, :])
    decay, root = decay_terms(ra, vec_ref[taps + 3 : taps + 4, :])
    ra_ref[...] = ra
    ri_ref[...] = ri
    a_ref[...] = decay
    e_ref[...] = low.astype(F32) * ri * root
    prod = held[0:rows, :]
    state = held[rows:, :]
    for t in range(size // rows):
        now = a_ref[t * rows : (t + 1) * rows, :]
        state = now * state + e_ref[t * rows : (t + 1) * rows, :]
        prod = prod * now
    held[0:rows, :] = prod
    held[rows:, :] = state
    end_ref[0:rows, :] = prod
    end_ref[rows:, :] = state


def branch_kernel(count, n_ref, *refs):
    refs[count][...] = rows_times(n_ref[...], refs[:count])


def states_kernel(place, a_ref, e_ref, yp_ref, enter_ref, h_ref, z_ref, before_ref, end_ref, held):
    step = pl.program_id(0)
    rows = held.shape[0]

    @pl.when(step == 0)
    def _():
        held[...] = enter_ref[...]

    state = held[...]
    before_ref[...] = state
    for t in range(a_ref.shape[0] // rows):
        at = slice(t * rows, (t + 1) * rows)
        state = a_ref[at, :] * state + e_ref[at, :]
        h_ref[at, :] = state
    held[...] = state
    end_ref[...] = state
    act, _ = gelu_parts(yp_ref[...])
    z_ref[...] = (h_ref[...] * act).astype(BF)


def back_kernel(count, place, g_ref, yp_ref, h_ref, a_ref, *refs):
    pieces = refs[:count]
    dh_ref, dyp_ref, end_ref, held = refs[count:]
    step = pl.program_id(0)
    rows = held.shape[0]

    @pl.when(step == 0)
    def _():
        held[...] = jnp.zeros(held.shape, F32)

    act, slope = gelu_parts(yp_ref[...])
    dz = columns_times(g_ref[...], pieces)
    dh_ref[...] = dz * act
    dyp_ref[...] = (dz * h_ref[...] * slope).astype(BF)
    carry = held[...]
    for t in reversed(range(a_ref.shape[0] // rows)):
        at = slice(t * rows, (t + 1) * rows)
        carry = a_ref[at, :] * (dh_ref[at, :] + carry)
    held[...] = carry
    end_ref[...] = carry


def mlp_kernel(count, n_ref, dy_ref, *refs):
    gates, ups, downs = refs[:count], refs[count : 2 * count], refs[2 * count : 3 * count]
    m_ref, dg_ref, du_ref = refs[3 * count :]
    gate = rows_times(n_ref[...], gates)
    up = rows_times(n_ref[...], ups)
    grad = columns_times(dy_ref[...], downs)
    act, slope = gelu_parts(gate)
    m_ref[...] = (act * up).astype(BF)
    dg_ref[...] = (grad * up * slope).astype(BF)
    du_ref[...] = (grad * act).astype(BF)


def product_kernel(count, per, x_ref, *refs):
    out_ref = refs[count]
    step = pl.program_id(0)
    for i in range(count):

        @pl.when(step // per == i)
        def _():
            out_ref[...] = matmul(x_ref[...], refs[i][...]).astype(BF)


def transposed_kernel(count, per, x_ref, y_ref, *refs):
    out_ref = refs[2 * count]
    step = pl.program_id(0)
    for i in range(count):

        @pl.when(step // per == i)
        def _():
            out_ref[...] = (
                times_transpose(x_ref[...], refs[i][...])
                + times_transpose(y_ref[...], refs[count + i][...])
            ).astype(BF)


def grads_kernel(
    place, dh_ref, a_ref, ra_ref, ri_ref, v_ref, h_ref, hb_ref, u_ref, ub_ref, gate_ref, vec_ref,
    late_ref, gates_ref, du_ref, edge_ref, last_ref, sums_ref, end_ref, held, pad, spad, hpad, upad,
):
    step = pl.program_id(0)
    rows = held.shape[0]
    size = dh_ref.shape[0]
    width = dh_ref.shape[1]
    lag = ub_ref.shape[0]
    taps = lag // rows + 1

    @pl.when(step == 0)
    def _():
        held[...] = late_ref[...]
        pad[size:, :] = jnp.zeros((lag, width), F32)
        sums_ref[...] = jnp.zeros(sums_ref.shape, F32)

    @pl.when(step > 0)
    def _():
        pad[size:, :] = pad[0:lag, :]

    carry = held[...]
    for t in reversed(range(size // rows)):
        at = slice(t * rows, (t + 1) * rows)
        now = dh_ref[at, :] + carry
        spad[at, :] = now
        carry = a_ref[at, :] * now
    held[...] = carry
    end_ref[...] = carry
    hpad[0:rows, :] = hb_ref[...]
    hpad[rows:, :] = h_ref[...]
    upad[0:lag, :] = ub_ref[...]
    upad[lag:, :] = u_ref[...].astype(F32)
    s = spad[...]
    ra = ra_ref[...]
    ri = ri_ref[...]
    soft = vec_ref[taps + 3 : taps + 4, :]
    decay, root = decay_terms(ra, soft)
    v = v_ref[...].astype(F32)
    sv = s * v
    grad_log = decay * (s * hpad[0:size, :] - sv * ri * decay / root)
    rated = grad_log * ra
    dap = (-8.0 * soft * rated * (1.0 - ra)).astype(BF)
    dip = (sv * root * ri * (1.0 - ri)).astype(BF)
    gates_ref[:, :width] = dap
    gates_ref[:, width:] = dip
    dv = s * ri * root + lax.dot_general(
        gates_ref[...], gate_ref[...], (((1,), (1,)), ((), ())), preferred_element_type=F32
    )
    pad[0:size, :] = dv

    def fold(value):
        return jnp.sum(value.reshape(size // rows, rows, width), axis=0)

    terms = [dap.astype(F32), dip.astype(F32), rated, dv]
    terms = terms + [dv * upad[lag - rows * k : lag - rows * k + size, :] for k in range(taps)]
    for i, term in enumerate(terms):
        sums_ref[i * rows : (i + 1) * rows, :] += fold(term)
    du = vec_ref[0:1, :] * dv
    for k in range(1, taps):
        du = du + vec_ref[k : k + 1, :] * pad[rows * k : rows * k + size, :]
    du_ref[...] = du.astype(BF)

    @pl.when(step == 0)
    def _():
        last_ref[...] = du[size - lag :, :]

    for t in range(taps - 1):
        row = jnp.zeros((rows, width), F32)
        for k in range(taps - 1 - t, taps):
            at = (t + k - (taps - 1)) * rows
            row = row + vec_ref[k : k + 1, :] * pad[at : at + rows, :]
        edge_ref[t * rows : (t + 1) * rows, :] = row


def gate_matrix_kernel(blocks_ref, out_ref):
    kinds, heads, span, _ = blocks_ref.shape
    out_ref[...] = jnp.zeros(out_ref.shape, BF)
    for g in range(kinds):
        for h in range(heads):
            at = (g * heads + h) * span
            out_ref[h * span : (h + 1) * span, at : at + span] = blocks_ref[g, h]


def gate_matrix(blocks):
    kinds, heads, span, _ = blocks.shape
    return pl.pallas_call(
        gate_matrix_kernel,
        out_shape=jax.ShapeDtypeStruct((heads * span, kinds * heads * span), BF),
        name="gate_matrix",
    )(blocks)


def whole(shape):
    return pl.BlockSpec(shape, lambda *_: (0,) * len(shape))


def gates_call(place, x, border, gain, tail, gate, vec, pieces, rows):
    steps, size, model = x.shape
    lag, width = tail.shape
    wide = pieces[0].shape[0]
    here = pl.BlockSpec((None, size, width), lambda j, c: (j, 0, 0))
    full = jax.ShapeDtypeStruct((steps, size, width), F32)
    low = jax.ShapeDtypeStruct((steps, size, width), BF)
    rowed = pl.BlockSpec((None, size, model), lambda j, c: (j ^ c[0], 0, 0))
    return pl.pallas_call(
        functools.partial(gates_kernel, len(pieces)),
        out_shape=(
            jax.ShapeDtypeStruct(x.shape, BF),
            low,
            low,
            full,
            full,
            full,
            full,
            jax.ShapeDtypeStruct((steps, lag, width), F32),
            jax.ShapeDtypeStruct((2 * rows, width), F32),
        ),
        grid_spec=pltpu.PrefetchScalarGridSpec(
            num_scalar_prefetch=1,
            grid=(steps,),
            in_specs=[
                rowed,
                whole(border.shape),
                whole(gain.shape),
                whole(tail.shape),
                whole(gate.shape),
                whole(vec.shape),
            ]
            + [pl.BlockSpec((wide, width), lambda j, c: (0, 0))] * len(pieces),
            out_specs=[
                rowed,
                here,
                here,
                here,
                here,
                here,
                here,
                pl.BlockSpec((None, lag, width), lambda j, c: (j, 0, 0)),
                whole((2 * rows, width)),
            ],
            scratch_shapes=[
                pltpu.VMEM((size + lag, width), F32),
                pltpu.VMEM((2 * rows, width), F32),
            ],
        ),
        name="gates",
    )(place, x, border, gain, tail, gate, vec, *pieces)


def branch_call(n, pieces):
    steps, size, model = n.shape
    wide, width = pieces[0].shape
    return pl.pallas_call(
        functools.partial(branch_kernel, len(pieces)),
        out_shape=jax.ShapeDtypeStruct((steps, size, width), F32),
        grid=(steps,),
        in_specs=[pl.BlockSpec((None, size, model), lambda j: (j, 0, 0))]
        + [whole((wide, width))] * len(pieces),
        out_specs=pl.BlockSpec((None, size, width), lambda j: (j, 0, 0)),
        name="branch",
    )(n, *pieces)


def states_call(place, a, e, yp, enter):
    steps, size, width = a.shape
    rows = enter.shape[0]
    here = pl.BlockSpec((None, size, width), lambda j, c: (j, 0, 0))
    there = pl.BlockSpec((None, size, width), lambda j, c: (j ^ c[0], 0, 0))
    return pl.pallas_call(
        states_kernel,
        out_shape=(
            jax.ShapeDtypeStruct((steps, size, width), F32),
            jax.ShapeDtypeStruct((steps, size, width), BF),
            jax.ShapeDtypeStruct((steps, rows, width), F32),
            jax.ShapeDtypeStruct((rows, width), F32),
        ),
        grid_spec=pltpu.PrefetchScalarGridSpec(
            num_scalar_prefetch=1,
            grid=(steps,),
            in_specs=[here, here, there, whole((rows, width))],
            out_specs=[
                here,
                there,
                pl.BlockSpec((None, rows, width), lambda j, c: (j, 0, 0)),
                whole((rows, width)),
            ],
            scratch_shapes=[pltpu.VMEM((rows, width), F32)],
        ),
        name="states",
    )(place, a, e, yp, enter)


def back_call(place, g, yp, h, a, pieces, rows):
    steps, size, width = a.shape
    last = steps - 1
    here = pl.BlockSpec((None, size, width), lambda j, c: (last - j, 0, 0))
    there = pl.BlockSpec((None, size, width), lambda j, c: ((last - j) ^ c[0], 0, 0))
    return pl.pallas_call(
        functools.partial(back_kernel, len(pieces)),
        out_shape=(
            jax.ShapeDtypeStruct((steps, size, width), F32),
            jax.ShapeDtypeStruct((steps, size, width), BF),
            jax.ShapeDtypeStruct((rows, width), F32),
        ),
        grid_spec=pltpu.PrefetchScalarGridSpec(
            num_scalar_prefetch=1,
            grid=(steps,),
            in_specs=[
                pl.BlockSpec((None, size, g.shape[2]), lambda j, c: ((last - j) ^ c[0], 0, 0)),
                there,
                here,
                here,
            ]
            + [whole(pieces[0].shape)] * len(pieces),
            out_specs=[here, there, whole((rows, width))],
            scratch_shapes=[pltpu.VMEM((rows, width), F32)],
        ),
        name="back",
    )(place, g, yp, h, a, *pieces)


def grads_call(place, dh, a, ra, ri, v, h, h_before, u, u_before, gate, vec, late):
    steps, size, width = a.shape
    rows = late.shape[0]
    lag = u_before.shape[1]
    last = steps - 1
    count = lag // rows + 5
    here = pl.BlockSpec((None, size, width), lambda j, c: (last - j, 0, 0))
    there = pl.BlockSpec((None, size, width), lambda j, c: ((last - j) ^ c[0], 0, 0))
    small = lambda size: pl.BlockSpec((None, size, width), lambda j, c: (last - j, 0, 0))
    return pl.pallas_call(
        grads_kernel,
        out_shape=(
            jax.ShapeDtypeStruct((steps, size, 2 * width), BF),
            jax.ShapeDtypeStruct((steps, size, width), BF),
            jax.ShapeDtypeStruct((lag, width), F32),
            jax.ShapeDtypeStruct((lag, width), F32),
            jax.ShapeDtypeStruct((count * rows, width), F32),
            jax.ShapeDtypeStruct((rows, width), F32),
        ),
        grid_spec=pltpu.PrefetchScalarGridSpec(
            num_scalar_prefetch=1,
            grid=(steps,),
            in_specs=[
            here,
            here,
            here,
            here,
            here,
            here,
            small(rows),
            here,
            small(lag),
            whole(gate.shape),
            whole(vec.shape),
            whole(late.shape),
        ],
        out_specs=[
            pl.BlockSpec((None, size, 2 * width), lambda j, c: (last - j, 0, 0)),
            there,
            whole((lag, width)),
            whole((lag, width)),
            whole((count * rows, width)),
            whole((rows, width)),
        ],
        scratch_shapes=[
            pltpu.VMEM((rows, width), F32),
            pltpu.VMEM((size + lag, width), F32),
            pltpu.VMEM((size, width), F32),
            pltpu.VMEM((size + rows, width), F32),
            pltpu.VMEM((size + lag, width), F32),
        ],
        ),
        name="grads",
    )(place, dh, a, ra, ri, v, h, h_before, u, u_before, gate, vec, late)


def tile_of(size, most):
    return max(t for t in range(128, most + 1, 128) if size % t == 0)


def mlp_call(n, dy, gates, ups, downs):
    tokens, model = n.shape
    wide, units = gates[0].shape
    tile = tile_of(units, 256)
    count = len(gates)
    out = pl.BlockSpec((tokens, tile), lambda j: (0, j))
    return pl.pallas_call(
        functools.partial(mlp_kernel, count),
        out_shape=[jax.ShapeDtypeStruct((tokens, units), BF)] * 3,
        grid=(units // tile,),
        in_specs=[whole((tokens, model))] * 2
        + [pl.BlockSpec((wide, tile), lambda j: (0, j))] * (2 * count)
        + [pl.BlockSpec((tile, wide), lambda j: (j, 0))] * count,
        out_specs=[out] * 3,
        name="mlp",
    )(n, dy, *gates, *ups, *downs)


def clipped(step, per, i):
    return jnp.clip(step - i * per, 0, per - 1)


def product_call(x, pieces):
    tokens, depth = x.shape
    wide = pieces[0].shape[1]
    tile = tile_of(wide, 512)
    per, count = wide // tile, len(pieces)
    return pl.pallas_call(
        functools.partial(product_kernel, count, per),
        out_shape=jax.ShapeDtypeStruct((tokens, wide * count), BF),
        grid=(per * count,),
        in_specs=[whole(x.shape)]
        + [
            pl.BlockSpec((depth, tile), lambda s, i=i: (0, clipped(s, per, i)))
            for i in range(count)
        ],
        out_specs=pl.BlockSpec((tokens, tile), lambda s: (0, s)),
        name="product",
    )(x, *pieces)


def transposed_call(x, y, first, second):
    tokens, depth = x.shape
    wide = first[0].shape[0]
    tile = tile_of(wide, 256)
    per, count = wide // tile, len(first)
    return pl.pallas_call(
        functools.partial(transposed_kernel, count, per),
        out_shape=jax.ShapeDtypeStruct((tokens, wide * count), BF),
        grid=(per * count,),
        in_specs=[whole(x.shape), whole(y.shape)]
        + [
            pl.BlockSpec((tile, depth), lambda s, i=i: (clipped(s, per, i), 0))
            for i in range(count)
        ]
        * 2,
        out_specs=pl.BlockSpec((tokens, tile), lambda s: (0, s)),
        name="transposed",
    )(x, y, *first, *second)


def norm_back(grad_norm, normed, inv_root, gain):
    scaled = grad_norm * gain
    mean_term = jnp.mean(scaled * normed, axis=-1, keepdims=True)
    return inv_root * (scaled - normed * mean_term)


def inverse_rms(value):
    return lax.rsqrt(jnp.mean(value * value, axis=-1, keepdims=True) + 1e-06)


def shards(
    tokens,
    norm_gain,
    mlp_gain,
    recur_proj,
    branch_proj,
    out_proj,
    gate_proj,
    up_proj,
    down_proj,
    recur_gate,
    input_gate,
    recur_bias,
    input_bias,
    decay_param,
    conv_bias,
    conv_weight,
    init_state,
    init_tail,
    reset_flags,
    cotangent,
):
    nsx, nsc, nco = (lax.axis_size(name) for name in BLOCKS)
    nseq = nsx * nsc
    co = lax.axis_index("co")
    first = lax.axis_index(BLOCKS) == 0
    ci = lax.axis_index(PEERS)
    place = jnp.stack([ci, first]).astype(jnp.int32)
    rows, share, model = tokens.shape
    own = rows * share
    group = PEER * own
    taps = conv_weight.shape[0]
    lag = taps - 1
    part = conv_bias.shape[0]
    chunk = part * nseq
    width = chunk * nco
    keep = (1 - reset_flags).astype(F32)[:, None]
    heads, span = recur_gate.shape[0], recur_gate.shape[2]
    unit = norm_gain.shape[0]
    sx, sc = lax.axis_index("sx"), lax.axis_index("sc")

    def owned(value):
        return feature_order(jnp.swapaxes(value, 0, 1).reshape(own, model))

    mine = owned(tokens)
    border = jnp.swapaxes(tokens[:, share - lag :], 0, 1).reshape(lag * rows, model)
    border = feature_order(before_last(border))

    vectors = jnp.concatenate(
        [
            conv_weight,
            conv_bias[None],
            recur_bias[None],
            input_bias[None],
            decay_param[None],
            init_state,
            jnp.swapaxes(init_tail, 0, 1).reshape(lag * rows, part),
        ],
        axis=0,
    )
    both = jnp.stack([recur_gate, input_gate]).reshape(-1, span)
    lines, lists = both.shape[0], vectors.shape[0]
    gains = jnp.stack([norm_gain, mlp_gain])
    packed = jnp.concatenate(
        [
            both,
            jnp.pad(vectors, ((0, 0), (0, span - part))),
            jnp.pad(
                jnp.concatenate([gains] + [peer(gains, k) for k in range(1, PEER)], axis=0),
                ((0, 0), (0, span - unit)),
            ),
        ],
        axis=0,
    )
    table = around(after(packed, border)[None], "co")
    ready = table[1:]
    table = jnp.concatenate(table, axis=0)
    for axis in ("sx", "sc"):
        table = jnp.concatenate(around(table, axis), axis=0)

    links = {"co": ready, "sx": ready}

    def travel(value, axis):
        items = around(after(value, *links[axis]), axis)
        links[axis] = items[1:]
        return items

    def gather(shard):
        return over_die(travel(join_columns(travel(shard, "co"), 1), "sx"))

    recur_chunks = travel(recur_proj, "co")
    x_group = peer_rows(mine, (border,))
    x_all = jnp.stack(x_group)
    recur_pieces = over_die(travel(join_columns(recur_chunks, 1), "sx"))
    branch_chunks = travel(after(branch_proj, x_group[2]), "co")
    out_chunks = travel(out_proj, "co")
    grad_mine = owned(cotangent)
    grad_near = peer(after(grad_mine, x_group[1]), 1)
    grad_far = peer(after(grad_mine, *out_chunks[1:]), 2)
    grad_group = [grad_mine, grad_near, grad_far, peer(grad_far, 1)]
    grad_full = jnp.concatenate(grad_group, axis=0)

    gains = table[:, lines + lists :, :unit].reshape(-1, PEER, 2 * unit)
    gains = jnp.swapaxes(gains, 0, 1).reshape(-1, 2 * unit)
    lot = jnp.arange(model // unit)
    rel = lot // (model // unit // nseq)
    here_seq = ((sx - rel % nsx) % nsx) * nsc + (sc - rel // nsx) % nsc
    whole_unit = here_seq * (model // unit // nseq) + lot % (model // unit // nseq)
    from_chan, from_seq = whole_unit // nseq, whole_unit % nseq
    source = ((from_chan % PEER) ^ lax.axis_index(PEERS)) * nsc + (sc - from_seq % nsc) % nsc
    source = source * nsx + (sx - from_seq // nsc) % nsx
    source = source * nco + (co - from_chan // PEER) % nco
    pick = (source[:, None] == jnp.arange(model // unit)[None, :]).astype(F32)
    gains = jnp.dot(pick, gains.astype(F32), precision=lax.Precision.HIGHEST)
    gain_one = gains[:, :unit].reshape(1, model)
    gain_two = gains[:, unit:].reshape(1, model)

    table = table[:, : lines + lists].reshape(nseq, nco, lines + lists, span)
    table = jnp.concatenate(
        [
            lax.dynamic_slice_in_dim(
                table, ((sc - s % nsc) % nsc) * nsx + (sx - s // nsc) % nsx, 1, 0
            )
            for s in range(nseq)
        ],
        axis=0,
    )
    vectors = table[:, :, lines:, :part]
    vectors = jnp.transpose(vectors, (2, 1, 0, 3)).reshape(-1, width).astype(F32)
    decay32 = vectors[taps + 3 : taps + 4]
    vec = jnp.concatenate([vectors[: taps + 3], jax.nn.softplus(-decay32)], axis=0)
    vec = jnp.pad(vec, ((0, -vec.shape[0] % 8), (0, 0)))
    state_start = vectors[taps + 4 : taps + 4 + rows] * keep
    tail_start = vectors[taps + 4 + rows :] * jnp.tile(keep, (lag, 1))
    both = table[:, :, :lines].reshape(nseq, nco, 2, heads, -1, span)
    both = jnp.transpose(both, (2, 1, 3, 0, 4, 5)).reshape(2, nco * heads, span, span)
    gate = gate_matrix(both)

    normal_in, u, v, ra, ri, decay, drive, u_before, summary = gates_call(
        place, x_all, border, gain_one, tail_start, gate, vec, recur_pieces, rows
    )
    branch_chunks = [branch_chunks[0]] + [after(item, recur_pieces[-1]) for item in branch_chunks[1:]]
    branch_pieces = over_die(travel(join_columns(branch_chunks, 1), "sx"))
    yp = branch_call(normal_in, branch_pieces)
    ends = u[PEER - 1, own - lag * rows :]
    outer = other_blocks(summary, rows, False)
    enter = outer[:rows] * state_start + outer[rows:]
    enter = after(enter, grad_near, grad_far)

    out_chunks = [out_chunks[0]] + [after(item, enter) for item in out_chunks[1:]]
    out_pieces = over_die(travel(jnp.concatenate(out_chunks, axis=0), "sx"))
    gate_chunks, up_chunks, down_chunks = (
        around(after(shard, enter), "co") for shard in (gate_proj, up_proj, down_proj)
    )

    h, z, h_before, h_end = states_call(place, decay, drive, yp, enter)
    z_rows = z.reshape(group, width)
    branch = product_call(z_rows, out_pieces)
    terms = cut(branch, PEER, 0)
    cross = peer(terms[3], 1)
    near = peer(after(terms[1], cross), 1)
    far = peer((terms[2].astype(F32) + cross.astype(F32)).astype(BF), 2)
    gate_chunks[1:] = [after(item, branch) for item in gate_chunks[1:]]
    gate_pieces = over_die(travel(join_columns(gate_chunks, 1), "sx"))
    resid = mine.astype(F32) + terms[0].astype(F32) + near.astype(F32) + far.astype(F32)
    resid = after(resid, grad_full)
    up_chunks[1:] = [after(item, resid) for item in up_chunks[1:]]
    up_pieces = over_die(travel(join_columns(up_chunks, 1), "sx"))

    inv_two = inverse_rms(resid)
    normed_two = resid * inv_two
    normal_group = peer_rows((normed_two * gain_two).astype(BF))
    normal_mid = jnp.concatenate(normal_group, axis=0)
    down_chunks[1:] = [after(item, normal_group[2]) for item in down_chunks[1:]]
    down_pieces = over_die(travel(jnp.concatenate(down_chunks, axis=0), "sx"))
    hidden, grad_gate, grad_up = mlp_call(
        normal_mid, grad_full, gate_pieces, up_pieces, down_pieces
    )
    def over_cores(halves):
        return sum_around(halves, "sc").astype(BF)

    def over_chips(grad, axis):
        return sum_around(cut(grad, nsx, axis), "sx").astype(BF)

    def over_chunks(grad, axis, *hold):
        return sum_around(cut(grad, nco, axis), "co", hold)

    down_grad = weight_grad(hidden, grad_full, 1)
    grad_gate, grad_up, down_sent = lax.optimization_barrier((grad_gate, grad_up, down_grad[1]))
    down_grad = over_cores([down_grad[0], down_sent])
    mid = transposed_call(grad_gate, grad_up, gate_pieces, up_pieces)
    mid_sum = peer_sum(cut(mid, PEER, 0))

    up_grad = over_cores(weight_grad(normal_mid, grad_up, 0))
    gate_grad = over_cores(weight_grad(normal_mid, grad_gate, 0))
    mlp = product_call(after(hidden, mid_sum), down_pieces)
    down_grad = over_chips(down_grad, 1)
    mid_sum = after(mid_sum, up_grad)
    gain_two_part = jnp.sum(mid_sum * normed_two, axis=0, keepdims=True)
    resid_grad = grad_mine.astype(F32) + norm_back(mid_sum, normed_two, inv_two, gain_two)
    resid_group = peer_rows(resid_grad.astype(BF))
    resid_all = jnp.stack(resid_group)
    up_grad = over_chips(after(up_grad, down_grad), 0)
    down_out = over_chunks(after(down_grad, resid_group[2]), 0)
    resid_all = after(resid_all, up_grad, down_out, gate_grad)

    dh, grad_branch, local_end = back_call(place, resid_all, yp, h, decay, out_pieces, rows)
    mlp_terms = cut(after(mlp, resid_all), PEER, 0)
    mlp_cross = peer(mlp_terms[3], 1)
    mlp_near = peer(after(mlp_terms[1], mlp_cross), 1)
    local_end = after(local_end, mlp_cross)
    late = other_blocks(jnp.concatenate([summary[:rows], local_end], axis=0), rows, True)[rows:]
    gate_grad = over_chips(after(gate_grad, late), 0)
    relay = (mlp_terms[2].astype(F32) + mlp_cross.astype(F32)).astype(BF)
    mlp_far = peer(after(relay, late), 2)
    mlp_sum = mlp_terms[0].astype(F32) + mlp_near.astype(F32) + mlp_far.astype(F32)
    mixed = (resid + mlp_sum).astype(BF)
    gates_low, grad_u, edge_out, last, sums, start_grad = grads_call(
        place, dh, decay, ra, ri, v, h, h_before, u, u_before, gate, vec, late
    )
    edge_in = chunk_roll(block_shift(edge_out, -1), -1)
    grad_branch, resid_late = lax.optimization_barrier(
        (grad_branch, resid_all, edge_out, mlp_cross)
    )[:2]
    grad_branch = grad_branch.reshape(group, width)
    normal_rows = normal_in.reshape(group, model)
    out_grad = over_cores(weight_grad(z_rows, resid_late.reshape(group, model), 1))
    branch_grad = over_cores(weight_grad(normal_rows, grad_branch, 0))
    fixed = (last + edge_in).astype(BF)[None]
    grad_u = lax.dynamic_update_slice(
        grad_u, fixed, (lax.bitwise_xor(ci, PEER - 1), own - lag * rows, 0)
    )
    grad_u = grad_u.reshape(group, width)
    back = transposed_call(grad_u, grad_branch, recur_pieces, branch_pieces)
    up_last = around_back(cut(after(up_grad, late), nco, 1), "co")
    gate_last = around_back(cut(after(gate_grad, late), nco, 1), "co")
    terms = cut(after(back, mlp_near, mlp_far, *up_last[1:]), PEER, 0)
    cross = peer(terms[3], 1)
    near = peer(after(terms[1], cross), 1)
    relay = (terms[2].astype(F32) + cross.astype(F32)).astype(BF)
    far = peer(after(relay, *gate_last[1:]), 2)
    back_sum = terms[0].astype(F32) + near.astype(F32) + far.astype(F32)
    both_grad = over_tokens(v.reshape(group, width), gates_low.reshape(group, 2 * width))
    recur_grad = over_cores(weight_grad(normal_rows, grad_u, 0))
    value = mine.astype(F32)
    inv_one = inverse_rms(value)
    normed_one = value * inv_one
    x_value = after(x_all, late).astype(F32)
    gain_one_part = jnp.sum(
        back.reshape(PEER, own, model).astype(F32) * (x_value * inverse_rms(x_value)), axis=(0, 1)
    )[None]
    tokens_grad = resid_grad + norm_back(back_sum, normed_one, inv_one, gain_one)

    up_out = sum(item.astype(F32) for item in up_last)
    gate_out = sum(item.astype(F32) for item in gate_last)
    out_grad = over_chips(out_grad, 1)
    branch_grad = over_chips(after(branch_grad, out_grad), 0)
    out_out = over_chunks(out_grad, 0, back_sum)
    recur_grad = over_chips(after(recur_grad, branch_grad), 0)
    branch_out = over_chunks(branch_grad, 1, back_sum)
    recur_out = over_chunks(recur_grad, 1)

    pieces = jnp.stack(
        [
            both_grad[span * h : span * (h + 1), g * width + span * h : g * width + span * (h + 1)]
            for g in range(2)
            for h in range(nco * heads)
        ]
    )
    pieces = pieces.reshape(2, nco, heads, nseq, -1, span)
    pieces = jnp.transpose(pieces, (3, 1, 0, 2, 4, 5)).reshape(nseq, nco, -1, span)
    sums = jnp.sum(sums.reshape(-1, rows, width), axis=1)
    small = jnp.concatenate(
        [
            sums[0:2],
            sums[2:3] * 8.0 * jax.nn.sigmoid(-decay32),
            sums[3:],
            jnp.where(first, keep * start_grad, 0.0),
            jnp.where(first, jnp.tile(keep, (lag, 1)) * edge_out, 0.0),
        ],
        axis=0,
    )
    small = jnp.transpose(small.reshape(-1, nco, nseq, part), (2, 1, 0, 3))
    small = jnp.pad(small, ((0, 0), (0, 0), (0, 0), (0, span - part)))
    packed = jnp.concatenate([pieces, small], axis=2)
    packed = jnp.concatenate(
        [
            lax.dynamic_slice_in_dim(packed, ((sx - rx) % nsx) * nsc + (sc - rc) % nsc, 1, 0)
            for rc in range(nsc)
            for rx in range(nsx)
        ],
        axis=0,
    ).astype(BF)
    packed = over_chips(over_cores(cut(packed, nsc, 0)), 0)[0]
    packed = over_chunks(after(packed, back_sum), 0)[0]
    both_out = packed[:lines].reshape(2, heads, -1, span)
    small = packed[lines:, :part]

    total = feature_restore(jnp.concatenate([gain_one_part, gain_two_part], axis=0))
    for axis in ("sc", "sx", "cb", "ca", "co"):
        if axis == "cb":
            total = after(total, back_sum)
        total = sum(around(total, axis)[1:], total)
    start = (lax.axis_index(("co", "ca", "cb")) * nseq + sx * nsc + sc) * unit
    gain_out = lax.dynamic_slice_in_dim(total, start, unit, 1)

    finish = after(jnp.concatenate([h_end, ends.astype(F32)], axis=0), hidden)
    reach = jnp.where(co == nco - 1, finish[:, :chunk], 0.0)
    for k in range(1, nco):
        piece = finish[:, (nco - k) * chunk : (nco - k + 1) * chunk]
        reach = reach + lax.ppermute(piece, "co", [(nco - 1, k - 1)])
    group_states = reach[:rows][None]
    group_tails = jnp.swapaxes(reach[rows:].reshape(lag, rows, chunk), 0, 1).astype(BF)[None]

    def returned(value):
        return jnp.swapaxes(feature_restore(value).reshape(share, rows, model), 0, 1)

    return (
        returned(mixed),
        returned(tokens_grad),
        gain_out[0],
        gain_out[1],
        recur_out,
        branch_out,
        out_out,
        gate_out,
        up_out,
        down_out,
        both_out[0],
        both_out[1],
        small[0],
        small[1],
        small[2],
        small[3],
        small[4 : 4 + taps],
        small[4 + taps : 4 + taps + rows],
        jnp.swapaxes(small[4 + taps + rows :].reshape(lag, rows, part), 0, 1),
        group_states,
        group_tails,
    )


def solution(mesh):
    nseq, nchan = mesh.devices.shape
    fine = Mesh(
        mesh.devices.reshape(nseq // 2, 2, nchan // PEER, 2, 2), ("sx", "sc", "co", "ca", "cb")
    )
    seq = ("sx", "sc")
    chan = ("co", "ca", "cb")
    place = P(None, seq + chan, None)
    vector = P(chan + seq)
    in_specs = (
        place,
        vector,
        vector,
        P(seq, chan),
        P(seq, chan),
        P(chan, seq),
        P(seq, chan),
        P(seq, chan),
        P(chan, seq),
        P(chan, seq, None),
        P(chan, seq, None),
        vector,
        vector,
        vector,
        vector,
        P(None, chan + seq),
        P(None, chan + seq),
        P(None, None, chan + seq),
        P(),
        place,
    )
    out_specs = (
        place,
        place,
        vector,
        vector,
        P(seq, chan),
        P(seq, chan),
        P(chan, seq),
        P(seq, chan),
        P(seq, chan),
        P(chan, seq),
        P(chan, seq, None),
        P(chan, seq, None),
        vector,
        vector,
        vector,
        vector,
        P(None, chan + seq),
        P(None, chan + seq),
        P(None, None, chan + seq),
        P(seq, None, chan),
        P(seq, None, None, chan),
    )
    return jax.shard_map(shards, mesh=fine, in_specs=in_specs, out_specs=out_specs, check_vma=False)
```

time: 948 us -> 839 us (0.89)
  matrix products: 160 us -> 56.5 us
  Pallas kernels: 50.5 us -> 147 us
  waiting for transfers between devices: 481 us -> 400 us
  local copies, waits for them, and re-layouts: 79.3 us -> 48.6 us
  other arithmetic: 70.7 us -> 83.9 us
    dot_general x12 -> x0, matrix products: 112 us -> none  [the longest x6 57.2 us: matmul(): return jnp.dot(left, right, preferred_element_type=F32)]
    pallas_call x2 -> x8, Pallas kernels: 17 us -> 114 us  [the longest x2 33.7 us: transposed_call(): pl.pallas_call(functools.partial(transposed_kernel, count, per), out_shap...]
    ppermute x74 -> x59, waiting for transfers between devices: 307 us -> 240 us  [shift(): lax.ppermute(value, axis, [(i, (i + step) % count) for i in range(count)])]
    unnamed x226 -> x175, local copies, waits for them, and re-layouts: 32.9 us -> 12.4 us
    add x28 -> x11, other arithmetic: 30.5 us -> 9.96 us  [the longest x1 2.54 us: shards(): mine.astype(F32) + terms[0].astype(F32) + near.astype(F32) + far.astype(F32)]
    convert_element_type x5 -> x21, other arithmetic: 4.7 us -> 24.5 us  [the longest x7 10.2 us: over_cores(): return sum_around(halves, 'sc').astype(BF)]
    ppermute x74 -> x59, starting transfers between devices: 51 us -> 61.4 us  [shift(): lax.ppermute(value, axis, [(i, (i + step) % count) for i in range(count)])]
    ppermute x2 -> x1, waiting for transfers between devices: 9.93 us -> 0.01 us  [block_shift(): return lax.ppermute(value, BLOCKS, route)]
  transfers between devices with their start and end apart: 107 -> 92, of which waited for: 45 -> 42; matrix products, arithmetic and copies ran while one was open for 24% -> 19% of each run, Pallas kernels for 5% -> 11%
where the time goes in v3:
time: 839 us; the launch traced here: 834 us
  waiting for transfers between devices  400 us (48%)
  Pallas kernels  147 us (18%)
  starting transfers between devices  95.2 us (11%)
  other arithmetic  83.9 us (10%)
  matrix products  56.5 us (7%)
  local copies, waits for them, and re-layouts  48.6 us (6%)
    ppermute x59, waiting for transfers between devices, shift(): lax.ppermute(value, axis, [(i, (i + step) % count) for i in range(count)])  240 us
    ppermute x27, waiting for transfers between devices, peer(): return lax.ppermute(value, PEERS, [(i, i ^ step) for i in range(PEER)])  156 us
    ppermute x59, starting transfers between devices, shift(): lax.ppermute(value, axis, [(i, (i + step) % count) for i in range(count)])  61.4 us
    dot_general x13, matrix products, over_tokens(): lax.dot_general(left, right, (((0,), (0,)), ((), ())), preferred_element_...  56.3 us
    pallas_call x2, Pallas kernels, transposed_call(): pl.pallas_call(functools.partial(transposed_kernel, count, per), out_shap...  33.7 us
    ppermute x27, starting transfers between devices, peer(): return lax.ppermute(value, PEERS, [(i, i ^ step) for i in range(PEER)])  28.3 us
    pallas_call x1, Pallas kernels, mlp_call(): pl.pallas_call(functools.partial(mlp_kernel, count), out_shape=[jax.Shape...  27.1 us
    pallas_call x2, Pallas kernels, product_call(): pl.pallas_call(functools.partial(product_kernel, count, per), out_shape=j...  19.6 us
  transfers between devices with their start and end apart: 92, of which 42 were waited for; matrix products, arithmetic and copies ran while one was open for 19% of the time, Pallas kernels for 11%

profile of v3, /device:TPU:0, one launch (start us, length us, event | category | flops | bytes accessed | tf_op | source)
XLA Modules:
  0.0 834.0 jit_solution(5115446985430224052)
XLA Ops:
  14.6 12.0 %collective-permute-start.10 = (bf16[1,208,160]{2,1,0:T(8,128)(2,1)S(1)}, bf16[1,208,160]{2,1,0:T(8,128)(2,1)S(1)}, u32[]{:S(2)}, u32[]{:S(2)}) collective-permute-start(bf16[1,208,160]{2,1,0:T(8,128)(2,1)S(1)} %bitcast.176), channel_id=1, source_target_pairs={{0,4},{4,0},{1,5},{5,1},{2,6},{6,2},{3,7},{7,3},{8,12},{12,8},{9,1... | collective-permute-start | bytes 199688 | tf_op jit(solution)/shard_map/ppermute | solution.py:22
  39.7 24.3 %collective-permute-done.13.refs_1_ = bf16[512,320]{1,0:T(8,128)(2,1)} collective-permute-done((bf16[512,320]{1,0:T(8,128)(2,1)S(1)}, bf16[512,320]{1,0:T(8,128)(2,1)}, u32[]{:S(2)}, u32[]{:S(2)}) %collective-permute-start.13) | collective-permute-done | bytes 327712 | tf_op jit(solution)/shard_map/ppermute | solution.py:22
  91.5 7.8 collective-permute-done.17.refs_1_
  104.7 16.0 %gates.1 = (bf16[4,256,2048]{2,1,0:T(8,128)(2,1)}, bf16[4,256,640]{2,1,0:T(8,128)(2,1)}, bf16[4,256,640]{2,1,0:T(8,128)(2,1)}, f32[4,256,640]{2,1,0:T(8,128)}, f...) custom-call(s32[2]{0:T(128)} %pad_add_fusion.here.place, ...), custom_call_target="tpu_custom_call" | custom-call | tf_op jit(solution)/shard_map/gates/pallas_call | solution.py:485
  132.3 12.7 %collective-permute-done.23 = f32[16,640]{1,0:T(8,128)S(1)} collective-permute-done((f32[16,640]{1,0:T(8,128)S(1)}, f32[16,640]{1,0:T(8,128)S(1)}, u32[]{:S(2)}, u32[]{:S(2)}) %collective-permute-start.23) | collective-permute-done | bytes 40992 | tf_op jit(solution)/shard_map/ppermute | solution.py:22
  152.5 13.6 %collective-permute-done.27.refs_1_ = bf16[640,512]{1,0:T(8,128)(2,1)} collective-permute-done((bf16[640,512]{1,0:T(8,128)(2,1)S(1)}, bf16[640,512]{1,0:T(8,128)(2,1)}, u32[]{:S(2)}, u32[]{:S(2)}) %collective-permute-start.27) | collective-permute-done | bytes 655392 | tf_op jit(solution)/shard_map/ppermute | solution.py:22
  167.8 7.4 branch.1.yp_ref
  181.9 7.4 product.2
  194.8 23.1 %collective-permute-done.30 = bf16[256,2048]{1,0:T(8,128)(2,1)S(1)} collective-permute-done((bf16[256,2048]{1,0:T(8,128)(2,1)S(1)}, bf16[256,2048]{1,0:T(8,128)(2,1)S(1)}, u32[]{:S(2)}, u32[]{:S(2)}) %collective-permute-start.30) | collective-permute-done | bytes 1048608 | tf_op jit(solution)/shard_map/ppermute | solution.py:32
  223.1 8.9 %collective-permute-done.37.refs_1_ = bf16[512,768]{1,0:T(8,128)(2,1)} collective-permute-done((bf16[512,768]{1,0:T(8,128)(2,1)}, bf16[512,768]{1,0:T(8,128)(2,1)}, u32[]{:S(2)}, u32[]{:S(2)}) %collective-permute-start.37) | collective-permute-done | bytes 786464 | tf_op jit(solution)/shard_map/ppermute | solution.py:22
  240.5 8.6 %pad_maximum_fusion.1.dy_ref = bf16[1024,2048]{1,0:T(8,128)(2,1)} fusion(bf16[256,2048]{1,0:T(8,128)(2,1)} %collective-permute-done.33, bf16[256,2048]{1,0:T(8,128)(2,1)} %collective-permute-done.26, bf16[256,2048]{1,0:T(8,128)(2,1)} %collective-permute-done.24, bf16[256,512]{1,0:T(8,128)(2,1)S(1)} %get-tuple-element.294, ...), kind=kLoop, calls=%fused_computation.9 | loop fusion | flops 29360128 | bytes 8388608 | tf_op jit(solution)/shard_map/concatenate | solution.py:833
  249.1 21.7 %collective-permute-done.32 = bf16[256,2048]{1,0:T(8,128)(2,1)} collective-permute-done((bf16[256,2048]{1,0:T(8,128)(2,1)S(1)}, bf16[256,2048]{1,0:T(8,128)(2,1)}, u32[]{:S(2)}, u32[]{:S(2)}) %collective-permute-start.32) | collective-permute-done | bytes 1048608 | tf_op jit(solution)/shard_map/ppermute | solution.py:32
  281.1 36.0 %collective-permute-done.45 = bf16[768,512]{1,0:T(8,128)(2,1)S(1)} collective-permute-done((bf16[768,512]{1,0:T(8,128)(2,1)S(1)}, bf16[768,512]{1,0:T(8,128)(2,1)S(1)}, u32[]{:S(2)}, u32[]{:S(2)}) %collective-permute-start.45) | collective-permute-done | bytes 786464 | tf_op jit(solution)/shard_map/ppermute | solution.py:22
  323.3 21.7 %collective-permute-done.36 = bf16[256,2048]{1,0:T(8,128)(2,1)S(1)} collective-permute-done((bf16[256,2048]{1,0:T(8,128)(2,1)S(1)}, bf16[256,2048]{1,0:T(8,128)(2,1)S(1)}, u32[]{:S(2)}, u32[]{:S(2)}) %collective-permute-start.36) | collective-permute-done | bytes 1048608 | tf_op jit(solution)/shard_map/ppermute | solution.py:32
  345.0 9.8 %collective-permute-done.46.refs_9_.refs_1_ = bf16[1536,512]{1,0:T(8,128)(2,1)S(1)} collective-permute-done((bf16[1536,512]{1,0:T(8,128)(2,1)S(1)}, bf16[1536,512]{1,0:T(8,128)(2,1)S(1)}, u32[]{:S(2)}, u32[]{:S(2)}) %collective-permute-start.46) | collective-permute-done | bytes 1572896 | tf_op jit(solution)/shard_map/ppermute | solution.py:22
  360.7 27.1 %mlp.1 = (bf16[1024,1536]{1,0:T(8,128)(2,1)}, bf16[1024,1536]{1,0:T(8,128)(2,1)}, bf16[1024,1536]{1,0:T(8,128)(2,1)}) custom-call(bf16[1024,2048]{1,0:T(8,128)(2,1)} %pad_maximum_fusion.2.n_ref, bf16[1024,2048]{1,0:T(8,128)(2,1)} %pad_maximum_fusion.1.dy_ref, bf16[512,1536]{1,0:T(8,128)(2,1)} %join.6.refs_0_, ...), custom_call_target="tpu_custom_call" | custom-call | tf_op jit(solution)/shard_map/mlp/pallas_call | solution.py:668
  387.8 7.7 convolution_convert_fusion.5
  395.4 21.0 %transposed.2 = bf16[1024,2048]{1,0:T(8,128)(2,1)} custom-call(bf16[1024,1536]{1,0:T(8,128)(2,1)} %get-tuple-element.138.x_ref, bf16[1024,1536]{1,0:T(8,128)(2,1)} %get-tuple-element.139.y_ref, bf16[512,1536]{1,0:T(8,128)(2,1)} %join.6.refs_0_, bf16[512,1536]{1,0:T(8,128)(2,1)} %collective-permute-done.38.refs_1_, bf16[512,1536]{1,0:T(8,128)(2,1)} %copy-done.19, ...), custom_call_target="tpu_custom_call" | custom-call | tf_op jit(solution)/shard_map/transposed/pallas_call | solution.py:708
  419.8 7.3 convolution_convert_fusion.3
  431.4 12.4 %collective-permute-done.49 = bf16[256,2048]{1,0:T(8,128)(2,1)S(1)} collective-permute-done((bf16[256,2048]{1,0:T(8,128)(2,1)S(1)}, bf16[256,2048]{1,0:T(8,128)(2,1)S(1)}, u32[]{:S(2)}, u32[]{:S(2)}) %collective-permute-start.49) | collective-permute-done | bytes 1048608 | tf_op jit(solution)/shard_map/ppermute | solution.py:32
  455.2 13.6 %collective-permute-done.51 = bf16[256,2048]{1,0:T(8,128)(2,1)S(1)} collective-permute-done((bf16[256,2048]{1,0:T(8,128)(2,1)S(1)}, bf16[256,2048]{1,0:T(8,128)(2,1)S(1)}, u32[]{:S(2)}, u32[]{:S(2)}) %collective-permute-start.51) | collective-permute-done | bytes 1048608 | tf_op jit(solution)/shard_map/ppermute | solution.py:32
  480.7 20.3 %collective-permute-done.54 = bf16[256,2048]{1,0:T(8,128)(2,1)} collective-permute-done((bf16[256,2048]{1,0:T(8,128)(2,1)S(1)}, bf16[256,2048]{1,0:T(8,128)(2,1)}, u32[]{:S(2)}, u32[]{:S(2)}) %collective-permute-start.54) | collective-permute-done | bytes 1048608 | tf_op jit(solution)/shard_map/ppermute | solution.py:32
  518.2 12.2 %product.3 = bf16[1024,2048]{1,0:T(8,128)(2,1)} custom-call(bf16[1024,1536]{1,0:T(8,128)(2,1)} %get-tuple-element.141.x_ref, bf16[1536,512]{1,0:T(8,128)(2,1)} %copy-done.9, bf16[1536,512]{1,0:T(8,128)(2,1)} %copy-done.23, bf16[1536,512]{1,0:T(8,128)(2,1)} %copy-done.24, bf16[1536,512]{1,0:T(8,128)(2,1)} %collective-permute-done.48.refs_11_.refs_3_), custom_call_target="tpu_custom_call" | custom-call | tf_op jit(solution)/shard_map/product/pallas_call | solution.py:689
  541.9 24.3 %collective-permute-done.59 = bf16[768,512]{1,0:T(8,128)(2,1)S(1)} collective-permute-done((bf16[768,512]{1,0:T(8,128)(2,1)S(1)}, bf16[768,512]{1,0:T(8,128)(2,1)S(1)}, u32[]{:S(2)}, u32[]{:S(2)}) %collective-permute-start.59) | collective-permute-done | bytes 786464 | tf_op jit(solution)/shard_map/ppermute | solution.py:22
  582.6 10.6 %back.1 = (f32[4,256,640]{2,1,0:T(8,128)}, bf16[4,256,640]{2,1,0:T(8,128)(2,1)}, f32[8,640]{1,0:T(8,128)}) custom-call(s32[2]{0:T(128)} %pad_add_fusion.here.place, bf16[4,256,2048]{2,1,0:T(8,128)(2,1)} %pad_maximum_fusion.3.g_ref, f32[4,256,640]{2,1,0:T(8,128)} %branch.1.yp_ref, f32[4,256,640]{2,1,0:T(8,128)} %get-tuple-element.150.h_ref, ...), custom_call_target="tpu_custom_call" | custom-call | tf_op jit(solution)/shard_map/back/pallas_call | solution.py:578
  608.9 14.2 %grads.1 = (bf16[4,256,1280]{2,1,0:T(8,128)(2,1)}, bf16[4,256,640]{2,1,0:T(8,128)(2,1)}, f32[24,640]{1,0:T(8,128)}, f32[24,640]{1,0:T(8,128)}, f32[64,640]{1,0:T(8,128)}, /*index=5*/f32[8,640]{1,0:T(8,128)}) custom-call(s32[2]{0:T(128)} %pad_add_fusion.here.place, f32[4,256,640]{2,1,0:T(8,128)} %get-tuple-element.154.dh_ref, ...), custom_call_target="tpu_custom_call" | custom-call | tf_op jit(solution)/shard_map/grads/pallas_call | solution.py:611
  657.9 12.7 %transposed.3 = bf16[1024,2048]{1,0:T(8,128)(2,1)} custom-call(bf16[1024,640]{1,0:T(8,128)(2,1)} %bitcast.43.x_ref, bf16[1024,640]{1,0:T(8,128)(2,1)} %bitcast.189, bf16[512,640]{1,0:T(8,128)(2,1)} %join.4.refs_0_, bf16[512,640]{1,0:T(8,128)(2,1)} %collective-permute-done.14.refs_1_, bf16[512,640]{1,0:T(8,128)(2,1)} %copy-done.40, ...), custom_call_target="tpu_custom_call" | custom-call | tf_op jit(solution)/shard_map/transposed/pallas_call | solution.py:708
  700.0 26.6 %collective-permute-done.71 = bf16[512,1536]{1,0:T(8,128)(2,1)S(1)} collective-permute-done((bf16[512,1536]{1,0:T(8,128)(2,1)S(1)}, bf16[512,1536]{1,0:T(8,128)(2,1)S(1)}, u32[]{:S(2)}, u32[]{:S(2)}) %collective-permute-start.71) | collective-permute-done | bytes 1572896 | tf_op jit(solution)/shard_map/ppermute | solution.py:22
  727.1 12.1 %collective-permute-done.82 = bf16[640,512]{1,0:T(8,128)(2,1)S(1)} collective-permute-done((bf16[640,512]{1,0:T(8,128)(2,1)S(1)}, bf16[640,512]{1,0:T(8,128)(2,1)S(1)}, u32[]{:S(2)}, u32[]{:S(2)}) %collective-permute-start.82) | collective-permute-done | bytes 655392 | tf_op jit(solution)/shard_map/ppermute | solution.py:22
  742.3 19.3 %collective-permute-done.72 = bf16[512,768]{1,0:T(8,128)(2,1)S(1)} collective-permute-done((bf16[512,768]{1,0:T(8,128)(2,1)S(1)}, bf16[512,768]{1,0:T(8,128)(2,1)S(1)}, u32[]{:S(2)}, u32[]{:S(2)}) %collective-permute-start.72) | collective-permute-done | bytes 786464 | tf_op jit(solution)/shard_map/ppermute | solution.py:22
  770.2 8.5 %collective-permute-done.84 = bf16[512,640]{1,0:T(8,128)(2,1)S(1)} collective-permute-done((bf16[512,640]{1,0:T(8,128)(2,1)S(1)}, bf16[512,640]{1,0:T(8,128)(2,1)S(1)}, u32[]{:S(2)}, u32[]{:S(2)}) %collective-permute-start.84) | collective-permute-done | bytes 655392 | tf_op jit(solution)/shard_map/ppermute | solution.py:22
  781.7 23.2 %collective-permute-done.73 = bf16[256,2048]{1,0:T(8,128)(2,1)S(1)} collective-permute-done((bf16[256,2048]{1,0:T(8,128)(2,1)S(1)}, bf16[256,2048]{1,0:T(8,128)(2,1)S(1)}, u32[]{:S(2)}, u32[]{:S(2)}) %collective-permute-start.73) | collective-permute-done | bytes 1048608 | tf_op jit(solution)/shard_map/ppermute | solution.py:32
  (532 shorter events, 327.2 us)
Async XLA Ops:
  34.3 39.3 %collective-permute-start = (bf16[256,2048]{1,0:T(8,128)(2,1)S(1)}, bf16[256,2048]{1,0:T(8,128)(2,1)}, u32[]{:S(2)}, u32[]{:S(2)}) collective-permute-start(bf16[256,2048]{1,0:T(8,128)(2,1)S(1)} %get-tuple-element.103), channel_id=1, source_target_pairs={{0,1},{1,0},{2,3},{3,2},{4,5},{5,4},{6,7},{7,6},{8,9},{9,8},{10,11... | collective-permute-start | bytes 3145736 | tf_op jit(solution)/shard_map/ppermute | solution.py:32
  34.3 39.3 %collective-permute-start.5 = (bf16[256,2048]{1,0:T(8,128)(2,1)S(1)}, bf16[256,2048]{1,0:T(8,128)(2,1)}, u32[]{:S(2)}, u32[]{:S(2)}) collective-permute-start(bf16[256,2048]{1,0:T(8,128)(2,1)S(1)} %get-tuple-element.103), channel_id=1, source_target_pairs={{0,2},{1,3},{2,0},{3,1},{4,6},{5,7},{6,4},{7,5},{8,10},{9,11},{10,... | collective-permute-start | bytes 3145736 | tf_op jit(solution)/shard_map/ppermute | solution.py:32
  66.6 36.4 %collective-permute-start.15 = (bf16[512,640]{1,0:T(8,128)(2,1)}, bf16[512,640]{1,0:T(8,128)(2,1)S(1)}, u32[]{:S(2)}, u32[]{:S(2)}) collective-permute-start(bf16[512,640]{1,0:T(8,128)(2,1)} %join.4.refs_0_), channel_id=1, source_target_pairs={{0,8},{8,0},{1,9},{9,1},{2,10},{10,2},{3,11},{11,3},{4,12},{12,4},... | collective-permute-start | bytes 1966088 | tf_op jit(solution)/shard_map/ppermute | solution.py:22
  193.4 47.1 %collective-permute-start.33 = (bf16[256,2048]{1,0:T(8,128)(2,1)}, bf16[256,2048]{1,0:T(8,128)(2,1)}, u32[]{:S(2)}, u32[]{:S(2)}) collective-permute-start(bf16[256,2048]{1,0:T(8,128)(2,1)} %collective-permute-done.26), channel_id=1, source_target_pairs={{0,1},{1,0},{2,3},{3,2},{4,5},{5,4},{6,7},{7,6},{8,9},{9,8},{10,11... | collective-permute-start | bytes 3145736 | tf_op jit(solution)/shard_map/ppermute | solution.py:32
  194.0 38.1 %collective-permute-start.37 = (bf16[512,768]{1,0:T(8,128)(2,1)}, bf16[512,768]{1,0:T(8,128)(2,1)}, u32[]{:S(2)}, u32[]{:S(2)}) collective-permute-start(bf16[512,768]{1,0:T(8,128)(2,1)} %refs_0_), channel_id=1, source_target_pairs={{0,4},{4,0},{1,5},{5,1},{2,6},{6,2},{3,7},{7,3},{8,12},{12,8},{9,1... | collective-permute-start | bytes 2359304 | tf_op jit(solution)/shard_map/ppermute | solution.py:22
  219.5 51.2 %collective-permute-start.32 = (bf16[256,2048]{1,0:T(8,128)(2,1)S(1)}, bf16[256,2048]{1,0:T(8,128)(2,1)}, u32[]{:S(2)}, u32[]{:S(2)}) collective-permute-start(bf16[256,2048]{1,0:T(8,128)(2,1)S(1)} %add_convert_fusion.13), channel_id=1, source_target_pairs={{0,2},{1,3},{2,0},{3,1},{4,6},{5,7},{6,4},{7,5},{8,10},{9,11},{10,... | collective-permute-start | bytes 3145736 | tf_op jit(solution)/shard_map/ppermute | solution.py:32
  220.6 50.1 %collective-permute-start.31 = (bf16[256,2048]{1,0:T(8,128)(2,1)}, bf16[256,2048]{1,0:T(8,128)(2,1)}, u32[]{:S(2)}, u32[]{:S(2)}) collective-permute-start(bf16[256,2048]{1,0:T(8,128)(2,1)} %get-tuple-element.123), channel_id=1, source_target_pairs={{0,1},{1,0},{2,3},{3,2},{4,5},{5,4},{6,7},{7,6},{8,9},{9,8},{10,11... | collective-permute-start | bytes 3145736 | tf_op jit(solution)/shard_map/ppermute | solution.py:32
  222.0 51.3 %collective-permute-start.41 = (bf16[512,768]{1,0:T(8,128)(2,1)}, bf16[512,768]{1,0:T(8,128)(2,1)}, u32[]{:S(2)}, u32[]{:S(2)}) collective-permute-start(bf16[512,768]{1,0:T(8,128)(2,1)} %refs_0_.1), channel_id=1, source_target_pairs={{0,4},{4,0},{1,5},{5,1},{2,6},{6,2},{3,7},{7,3},{8,12},{12,8},{9,1... | collective-permute-start | bytes 2359304 | tf_op jit(solution)/shard_map/ppermute | solution.py:22
  234.4 41.5 %collective-permute-start.38 = (bf16[512,1536]{1,0:T(8,128)(2,1)}, bf16[512,1536]{1,0:T(8,128)(2,1)}, u32[]{:S(2)}, u32[]{:S(2)}) collective-permute-start(bf16[512,1536]{1,0:T(8,128)(2,1)} %join.6.refs_0_), channel_id=1, source_target_pairs={{0,16},{16,0},{1,17},{17,1},{2,18},{18,2},{3,19},{19,3},{4,20},{20... | collective-permute-start | bytes 4718600 | tf_op jit(solution)/shard_map/ppermute | solution.py:22
  277.1 42.4 %collective-permute-start.42 = (bf16[512,1536]{1,0:T(8,128)(2,1)S(1)}, bf16[512,1536]{1,0:T(8,128)(2,1)S(1)}, u32[]{:S(2)}, u32[]{:S(2)}) collective-permute-start(bf16[512,1536]{1,0:T(8,128)(2,1)S(1)} %copy-done.8), channel_id=1, source_target_pairs={{0,16},{16,0},{1,17},{17,1},{2,18},{18,2},{3,19},{19,3},{4,20},{20... | collective-permute-start | bytes 4718600 | tf_op jit(solution)/shard_map/ppermute | solution.py:22
  277.6 41.7 %collective-permute-start.35 = (bf16[256,2048]{1,0:T(8,128)(2,1)S(1)}, bf16[256,2048]{1,0:T(8,128)(2,1)S(1)}, u32[]{:S(2)}, u32[]{:S(2)}) collective-permute-start(bf16[256,2048]{1,0:T(8,128)(2,1)S(1)} %multiply_convert_fusion), channel_id=1, source_target_pairs={{0,2},{1,3},{2,0},{3,1},{4,6},{5,7},{6,4},{7,5},{8,10},{9,11},{10,... | collective-permute-start | bytes 3145736 | tf_op jit(solution)/shard_map/ppermute | solution.py:32
  277.7 39.4 %collective-permute-start.45 = (bf16[768,512]{1,0:T(8,128)(2,1)S(1)}, bf16[768,512]{1,0:T(8,128)(2,1)S(1)}, u32[]{:S(2)}, u32[]{:S(2)}) collective-permute-start(bf16[768,512]{1,0:T(8,128)(2,1)S(1)} %copy-done.54), channel_id=1, source_target_pairs={{0,4},{4,0},{1,5},{5,1},{2,6},{6,2},{3,7},{7,3},{8,12},{12,8},{9,1... | collective-permute-start | bytes 2359304 | tf_op jit(solution)/shard_map/ppermute | solution.py:22
  279.5 41.7 %collective-permute-start.34 = (bf16[256,2048]{1,0:T(8,128)(2,1)S(1)}, bf16[256,2048]{1,0:T(8,128)(2,1)S(1)}, u32[]{:S(2)}, u32[]{:S(2)}) collective-permute-start(bf16[256,2048]{1,0:T(8,128)(2,1)S(1)} %multiply_convert_fusion), channel_id=1, source_target_pairs={{0,1},{1,0},{2,3},{3,2},{4,5},{5,4},{6,7},{7,6},{8,9},{9,8},{10,11... | collective-permute-start | bytes 3145736 | tf_op jit(solution)/shard_map/ppermute | solution.py:32
  281.1 42.1 %collective-permute-start.39 = (bf16[512,1536]{1,0:T(8,128)(2,1)S(1)}, bf16[512,1536]{1,0:T(8,128)(2,1)S(1)}, u32[]{:S(2)}, u32[]{:S(2)}) collective-permute-start(bf16[512,1536]{1,0:T(8,128)(2,1)S(1)} %copy-done.7), channel_id=1, source_target_pairs={{0,8},{8,0},{1,9},{9,1},{2,10},{10,2},{3,11},{11,3},{4,12},{12,4},... | collective-permute-start | bytes 4718600 | tf_op jit(solution)/shard_map/ppermute | solution.py:22
  319.4 35.4 %collective-permute-start.46 = (bf16[1536,512]{1,0:T(8,128)(2,1)S(1)}, bf16[1536,512]{1,0:T(8,128)(2,1)S(1)}, u32[]{:S(2)}, u32[]{:S(2)}) collective-permute-start(bf16[1536,512]{1,0:T(8,128)(2,1)S(1)} %pad_maximum_fusion.4.refs_8_.refs_0_), channel_id=1, source_target_pairs={{0,16},{16,0},{1,17},{17,1},{2,18},{18,2},{3,19},{19,3},{4,20},{20... | collective-permute-start | bytes 4718600 | tf_op jit(solution)/shard_map/ppermute | solution.py:22
  427.1 42.2 %collective-permute-start.52 = (bf16[1024,1536]{1,0:T(8,128)(2,1)}, bf16[1024,1536]{1,0:T(8,128)(2,1)S(1)}, u32[]{:S(2)}, u32[]{:S(2)}) collective-permute-start(bf16[1024,1536]{1,0:T(8,128)(2,1)} %convolution_convert_fusion.3), channel_id=1, source_target_pairs={{0,8},{8,0},{1,9},{9,1},{2,10},{10,2},{3,11},{11,3},{4,12},{12,4},... | collective-permute-start | bytes 9437192 | tf_op jit(solution)/shard_map/ppermute | solution.py:22
  427.2 44.7 %collective-permute-start.56 = (bf16[1536,1024]{1,0:T(8,128)(2,1)}, bf16[1536,1024]{1,0:T(8,128)(2,1)S(1)}, u32[]{:S(2)}, u32[]{:S(2)}) collective-permute-start(bf16[1536,1024]{1,0:T(8,128)(2,1)} %convolution_convert_fusion.5), channel_id=1, source_target_pairs={{0,8},{8,0},{1,9},{9,1},{2,10},{10,2},{3,11},{11,3},{4,12},{12,4},... | collective-permute-start | bytes 9437192 | tf_op jit(solution)/shard_map/ppermute | solution.py:22
  455.1 75.3 %collective-permute-start.60 = (bf16[1024,1536]{1,0:T(8,128)(2,1)}, bf16[1024,1536]{1,0:T(8,128)(2,1)}, u32[]{:S(2)}, u32[]{:S(2)}) collective-permute-start(bf16[1024,1536]{1,0:T(8,128)(2,1)} %convolution_convert_fusion), channel_id=1, source_target_pairs={{0,8},{8,0},{1,9},{9,1},{2,10},{10,2},{3,11},{11,3},{4,12},{12,4},... | collective-permute-start | bytes 9437192 | tf_op jit(solution)/shard_map/ppermute | solution.py:22
  473.7 34.9 %collective-permute-start.57 = (bf16[1536,512]{1,0:T(8,128)(2,1)S(1)}, bf16[1536,512]{1,0:T(8,128)(2,1)S(1)}, u32[]{:S(2)}, u32[]{:S(2)}) collective-permute-start(bf16[1536,512]{1,0:T(8,128)(2,1)S(1)} %slice.598), channel_id=1, source_target_pairs={{0,16},{16,0},{1,17},{17,1},{2,18},{18,2},{3,19},{19,3},{4,20},{20... | collective-permute-start | bytes 4718600 | tf_op jit(solution)/shard_map/ppermute | solution.py:22
  502.2 36.2 %collective-permute-start.55 = (bf16[256,2048]{1,0:T(8,128)(2,1)}, bf16[256,2048]{1,0:T(8,128)(2,1)}, u32[]{:S(2)}, u32[]{:S(2)}) collective-permute-start(bf16[256,2048]{1,0:T(8,128)(2,1)} %collective-permute-done.54), channel_id=1, source_target_pairs={{0,1},{1,0},{2,3},{3,2},{4,5},{5,4},{6,7},{7,6},{8,9},{9,8},{10,11... | collective-permute-start | bytes 3145736 | tf_op jit(solution)/shard_map/ppermute | solution.py:32
  511.6 56.1 %collective-permute-start.58 = (bf16[512,1536]{1,0:T(8,128)(2,1)}, bf16[512,1536]{1,0:T(8,128)(2,1)}, u32[]{:S(2)}, u32[]{:S(2)}) collective-permute-start(bf16[512,1536]{1,0:T(8,128)(2,1)} %slice.480), channel_id=1, source_target_pairs={{0,16},{16,0},{1,17},{17,1},{2,18},{18,2},{3,19},{19,3},{4,20},{20... | collective-permute-start | bytes 4718600 | tf_op jit(solution)/shard_map/ppermute | solution.py:22
  597.6 94.7 %collective-permute-start.62 = (bf16[256,2048]{1,0:T(8,128)(2,1)}, bf16[256,2048]{1,0:T(8,128)(2,1)}, u32[]{:S(2)}, u32[]{:S(2)}) collective-permute-start(bf16[256,2048]{1,0:T(8,128)(2,1)} %get-tuple-element.149), channel_id=1, source_target_pairs={{0,1},{1,0},{2,3},{3,2},{4,5},{5,4},{6,7},{7,6},{8,9},{9,8},{10,11... | collective-permute-start | bytes 3145736 | tf_op jit(solution)/shard_map/ppermute | solution.py:32
  651.2 38.1 %collective-permute-start.68 = (bf16[512,768]{1,0:T(8,128)(2,1)}, bf16[512,768]{1,0:T(8,128)(2,1)}, u32[]{:S(2)}, u32[]{:S(2)}) collective-permute-start(bf16[512,768]{1,0:T(8,128)(2,1)} %slice.504), channel_id=1, source_target_pairs={{0,4},{4,0},{1,5},{5,1},{2,6},{6,2},{3,7},{7,3},{8,12},{12,8},{9,1... | collective-permute-start | bytes 2359304 | tf_op jit(solution)/shard_map/ppermute | solution.py:22
  652.4 42.4 %collective-permute-start.66 = (bf16[256,2048]{1,0:T(8,128)(2,1)}, bf16[256,2048]{1,0:T(8,128)(2,1)}, u32[]{:S(2)}, u32[]{:S(2)}) collective-permute-start(bf16[256,2048]{1,0:T(8,128)(2,1)} %add_convert_fusion.11), channel_id=1, source_target_pairs={{0,2},{1,3},{2,0},{3,1},{4,6},{5,7},{6,4},{7,5},{8,10},{9,11},{10,... | collective-permute-start | bytes 3145736 | tf_op jit(solution)/shard_map/ppermute | solution.py:32
  689.2 37.3 %collective-permute-start.71 = (bf16[512,1536]{1,0:T(8,128)(2,1)S(1)}, bf16[512,1536]{1,0:T(8,128)(2,1)S(1)}, u32[]{:S(2)}, u32[]{:S(2)}) collective-permute-start(bf16[512,1536]{1,0:T(8,128)(2,1)S(1)} %copy-done.45), channel_id=1, source_target_pairs={{0,16},{16,0},{1,17},{17,1},{2,18},{18,2},{3,19},{19,3},{4,20},{20... | collective-permute-start | bytes 4718600 | tf_op jit(solution)/shard_map/ppermute | solution.py:22
  695.0 46.3 %collective-permute-start.69 = (bf16[256,2048]{1,0:T(8,128)(2,1)S(1)}, bf16[256,2048]{1,0:T(8,128)(2,1)S(1)}, u32[]{:S(2)}, u32[]{:S(2)}) collective-permute-start(bf16[256,2048]{1,0:T(8,128)(2,1)S(1)} %get-tuple-element.278), channel_id=1, source_target_pairs={{0,1},{1,0},{2,3},{3,2},{4,5},{5,4},{6,7},{7,6},{8,9},{9,8},{10,11... | collective-permute-start | bytes 3145736 | tf_op jit(solution)/shard_map/ppermute | solution.py:32
  698.9 40.3 %collective-permute-start.82 = (bf16[640,512]{1,0:T(8,128)(2,1)S(1)}, bf16[640,512]{1,0:T(8,128)(2,1)S(1)}, u32[]{:S(2)}, u32[]{:S(2)}) collective-permute-start(bf16[640,512]{1,0:T(8,128)(2,1)S(1)} %slice.623), channel_id=1, source_target_pairs={{0,16},{16,0},{1,17},{17,1},{2,18},{18,2},{3,19},{19,3},{4,20},{20... | collective-permute-start | bytes 1966088 | tf_op jit(solution)/shard_map/ppermute | solution.py:22
  741.4 40.3 %collective-permute-start.70 = (bf16[256,2048]{1,0:T(8,128)(2,1)S(1)}, bf16[256,2048]{1,0:T(8,128)(2,1)S(1)}, u32[]{:S(2)}, u32[]{:S(2)}) collective-permute-start(bf16[256,2048]{1,0:T(8,128)(2,1)S(1)} %get-tuple-element.168), channel_id=1, source_target_pairs={{0,1},{1,0},{2,3},{3,2},{4,5},{5,4},{6,7},{7,6},{8,9},{9,8},{10,11... | collective-permute-start | bytes 3145736 | tf_op jit(solution)/shard_map/ppermute | solution.py:32
  761.6 43.2 %collective-permute-start.73 = (bf16[256,2048]{1,0:T(8,128)(2,1)S(1)}, bf16[256,2048]{1,0:T(8,128)(2,1)S(1)}, u32[]{:S(2)}, u32[]{:S(2)}) collective-permute-start(bf16[256,2048]{1,0:T(8,128)(2,1)S(1)} %add_convert_fusion.9), channel_id=1, source_target_pairs={{0,2},{1,3},{2,0},{3,1},{4,6},{5,7},{6,4},{7,5},{8,10},{9,11},{10,... | collective-permute-start | bytes 3145736 | tf_op jit(solution)/shard_map/ppermute | solution.py:32
  765.6 44.9 %collective-permute-start.87 = (bf16[320,512]{1,0:T(8,128)(2,1)S(1)}, bf16[320,512]{1,0:T(8,128)(2,1)S(1)}, u32[]{:S(2)}, u32[]{:S(2)}) collective-permute-start(bf16[320,512]{1,0:T(8,128)(2,1)S(1)} %slice.629), channel_id=1, source_target_pairs={{0,4},{4,0},{1,5},{5,1},{2,6},{6,2},{3,7},{7,3},{8,12},{12,8},{9,1... | collective-permute-start | bytes 983048 | tf_op jit(solution)/shard_map/ppermute | solution.py:22
  768.6 38.7 %collective-permute-start.86 = (bf16[512,320]{1,0:T(8,128)(2,1)S(1)}, bf16[512,320]{1,0:T(8,128)(2,1)S(1)}, u32[]{:S(2)}, u32[]{:S(2)}) collective-permute-start(bf16[512,320]{1,0:T(8,128)(2,1)S(1)} %slice.627), channel_id=1, source_target_pairs={{0,4},{4,0},{1,5},{5,1},{2,6},{6,2},{3,7},{7,3},{8,12},{12,8},{9,1... | collective-permute-start | bytes 983048 | tf_op jit(solution)/shard_map/ppermute | solution.py:22
  779.3 53.4 %collective-permute-start.85 = (bf16[512,320]{1,0:T(8,128)(2,1)S(1)}, bf16[512,320]{1,0:T(8,128)(2,1)S(1)}, u32[]{:S(2)}, u32[]{:S(2)}) collective-permute-start(bf16[512,320]{1,0:T(8,128)(2,1)S(1)} %slice.625), channel_id=1, source_target_pairs={{0,4},{4,0},{1,5},{5,1},{2,6},{6,2},{3,7},{7,3},{8,12},{12,8},{9,1... | collective-permute-start | bytes 983048 | tf_op jit(solution)/shard_map/ppermute | solution.py:22
  (143 other events, 2431.9 us)

commit v4 on v3

--- a/solution.py
+++ b/solution.py
@@ -160,6 +160,7 @@
         count, mine = lax.axis_size(axis), lax.axis_index(axis)
         items = around(summary, axis)
         if axis == "co":
+            mark = items[1]
             items = [chunk_roll(item, r) for r, item in enumerate(items)]
         if count == 2:
             mate = items[1]
@@ -177,7 +178,7 @@
                 inner = jnp.where(ahead, compose(inner, item, rows), inner)
             outer = compose(inner, outer, rows)
             summary = total
-    return outer
+    return outer, mark
 
 
 def matmul(left, right):
@@ -681,8 +682,9 @@
     return jnp.clip(step - i * per, 0, per - 1)
 
 
-def product_call(x, pieces):
-    tokens, depth = x.shape
+def product_call(x, pieces, size=None, at=0):
+    depth = x.shape[1]
+    tokens = size or x.shape[0]
     wide = pieces[0].shape[1]
     tile = tile_of(wide, 512)
     per, count = wide // tile, len(pieces)
@@ -690,7 +692,7 @@
         functools.partial(product_kernel, count, per),
         out_shape=jax.ShapeDtypeStruct((tokens, wide * count), BF),
         grid=(per * count,),
-        in_specs=[whole(x.shape)]
+        in_specs=[pl.BlockSpec((tokens, depth), lambda s: (at, 0))]
         + [
             pl.BlockSpec((depth, tile), lambda s, i=i: (0, clipped(s, per, i)))
             for i in range(count)
@@ -700,8 +702,9 @@
     )(x, *pieces)
 
 
-def transposed_call(x, y, first, second):
-    tokens, depth = x.shape
+def transposed_call(x, y, first, second, size=None, at=0):
+    depth = x.shape[1]
+    tokens = size or x.shape[0]
     wide = first[0].shape[0]
     tile = tile_of(wide, 256)
     per, count = wide // tile, len(first)
@@ -709,7 +712,7 @@
         functools.partial(transposed_kernel, count, per),
         out_shape=jax.ShapeDtypeStruct((tokens, wide * count), BF),
         grid=(per * count,),
-        in_specs=[whole(x.shape), whole(y.shape)]
+        in_specs=[pl.BlockSpec((tokens, depth), lambda s: (at, 0))] * 2
         + [
             pl.BlockSpec((tile, depth), lambda s, i=i: (clipped(s, per, i), 0))
             for i in range(count)
@@ -793,22 +796,26 @@
     both = jnp.stack([recur_gate, input_gate]).reshape(-1, span)
     lines, lists = both.shape[0], vectors.shape[0]
     gains = jnp.stack([norm_gain, mlp_gain])
+    gains_got = [peer(gains, k) for k in range(1, PEER)]
     packed = jnp.concatenate(
         [
             both,
             jnp.pad(vectors, ((0, 0), (0, span - part))),
             jnp.pad(
-                jnp.concatenate([gains] + [peer(gains, k) for k in range(1, PEER)], axis=0),
+                jnp.concatenate([gains] + gains_got, axis=0),
                 ((0, 0), (0, span - unit)),
             ),
         ],
         axis=0,
     )
-    table = around(after(packed, border)[None], "co")
+    x_near = peer(after(mine, *gains_got), 1)
+    table = around(packed[None], "co")
+    x_far = peer(after(mine, *gains_got), 2)
+    x_across = peer(after(x_far, x_near), 1)
+    table = around(jnp.concatenate(table, axis=0), "sx")
     ready = table[1:]
     table = jnp.concatenate(table, axis=0)
-    for axis in ("sx", "sc"):
-        table = jnp.concatenate(around(table, axis), axis=0)
+    table = jnp.concatenate(around(table, "sc"), axis=0)
 
     links = {"co": ready, "sx": ready}
 
@@ -821,16 +828,17 @@
         return over_die(travel(join_columns(travel(shard, "co"), 1), "sx"))
 
     recur_chunks = travel(recur_proj, "co")
-    x_group = peer_rows(mine, (border,))
-    x_all = jnp.stack(x_group)
-    recur_pieces = over_die(travel(join_columns(recur_chunks, 1), "sx"))
-    branch_chunks = travel(after(branch_proj, x_group[2]), "co")
+    x_all = [mine, x_near, x_far, x_across]
+    recur_rows = travel(join_columns(recur_chunks, 1), "sx")
+    recur_pieces = over_die(recur_rows)
+    branch_chunks = travel(branch_proj, "co")
     out_chunks = travel(out_proj, "co")
     grad_mine = owned(cotangent)
-    grad_near = peer(after(grad_mine, x_group[1]), 1)
-    grad_far = peer(after(grad_mine, *out_chunks[1:]), 2)
-    grad_group = [grad_mine, grad_near, grad_far, peer(grad_far, 1)]
-    grad_full = jnp.concatenate(grad_group, axis=0)
+    grad_near = peer(after(grad_mine, x_across), 1)
+    x_all = after(jnp.stack(x_all), *branch_chunks[1:])
+    branch_chunks[1:] = [after(item, *recur_rows[1:]) for item in branch_chunks[1:]]
+    branch_rows = travel(join_columns(branch_chunks, 1), "sx")
+    branch_pieces = over_die(branch_rows)
 
     gains = table[:, lines + lists :, :unit].reshape(-1, PEER, 2 * unit)
     gains = jnp.swapaxes(gains, 0, 1).reshape(-1, 2 * unit)
@@ -871,39 +879,40 @@
     normal_in, u, v, ra, ri, decay, drive, u_before, summary = gates_call(
         place, x_all, border, gain_one, tail_start, gate, vec, recur_pieces, rows
     )
-    branch_chunks = [branch_chunks[0]] + [after(item, recur_pieces[-1]) for item in branch_chunks[1:]]
-    branch_pieces = over_die(travel(join_columns(branch_chunks, 1), "sx"))
+    ends = u[PEER - 1, own - lag * rows :]
+    outer, mark = other_blocks(after(summary, *branch_rows[1:]), rows, False)
+    enter = outer[:rows] * state_start + outer[rows:]
+    out_rows = travel(jnp.concatenate(out_chunks, axis=0), "sx")
+    out_pieces = over_die(out_rows)
     yp = branch_call(normal_in, branch_pieces)
-    ends = u[PEER - 1, own - lag * rows :]
-    outer = other_blocks(summary, rows, False)
-    enter = outer[:rows] * state_start + outer[rows:]
-    enter = after(enter, grad_near, grad_far)
-
-    out_chunks = [out_chunks[0]] + [after(item, enter) for item in out_chunks[1:]]
-    out_pieces = over_die(travel(jnp.concatenate(out_chunks, axis=0), "sx"))
+    grad_far = peer(after(grad_mine, mark), 2)
+    grad_full = jnp.concatenate([grad_mine, grad_near, grad_far, peer(grad_far, 1)], axis=0)
+
     gate_chunks, up_chunks, down_chunks = (
-        around(after(shard, enter), "co") for shard in (gate_proj, up_proj, down_proj)
-    )
-
-    h, z, h_before, h_end = states_call(place, decay, drive, yp, enter)
-    z_rows = z.reshape(group, width)
-    branch = product_call(z_rows, out_pieces)
-    terms = cut(branch, PEER, 0)
+        around(after(shard, mark), "co") for shard in (gate_proj, up_proj, down_proj)
+    )
+
+    h, z, h_before, h_end = states_call(place, decay, drive, yp, after(enter, grad_near, *out_rows[1:]))
+    z_rows = after(z, *gate_chunks[1:]).reshape(group, width)
+    last_term = product_call(z_rows, out_pieces, own, PEER - 1)
+    z_rows, last_term = lax.optimization_barrier((z_rows, last_term))
+    branch = product_call(z_rows, out_pieces, own * (PEER - 1))
+    terms = cut(branch, PEER - 1, 0) + [last_term]
     cross = peer(terms[3], 1)
     near = peer(after(terms[1], cross), 1)
-    far = peer((terms[2].astype(F32) + cross.astype(F32)).astype(BF), 2)
-    gate_chunks[1:] = [after(item, branch) for item in gate_chunks[1:]]
+    relay = (terms[2].astype(F32) + cross.astype(F32)).astype(BF)
+    far = peer(after(relay, *up_chunks[1:]), 2)
     gate_pieces = over_die(travel(join_columns(gate_chunks, 1), "sx"))
     resid = mine.astype(F32) + terms[0].astype(F32) + near.astype(F32) + far.astype(F32)
-    resid = after(resid, grad_full)
-    up_chunks[1:] = [after(item, resid) for item in up_chunks[1:]]
     up_pieces = over_die(travel(join_columns(up_chunks, 1), "sx"))
 
     inv_two = inverse_rms(resid)
     normed_two = resid * inv_two
-    normal_group = peer_rows((normed_two * gain_two).astype(BF))
+    normal_mine = after((normed_two * gain_two).astype(BF), *down_chunks[1:])
+    normal_near, normal_far = peer(normal_mine, 1), peer(normal_mine, 2)
+    normal_across = peer(after(normal_far, normal_near, grad_full), 1)
+    normal_group = [normal_mine, normal_near, normal_far, normal_across]
     normal_mid = jnp.concatenate(normal_group, axis=0)
-    down_chunks[1:] = [after(item, normal_group[2]) for item in down_chunks[1:]]
     down_pieces = over_die(travel(jnp.concatenate(down_chunks, axis=0), "sx"))
     hidden, grad_gate, grad_up = mlp_call(
         normal_mid, grad_full, gate_pieces, up_pieces, down_pieces
@@ -917,34 +926,46 @@
     def over_chunks(grad, axis, *hold):
         return sum_around(cut(grad, nco, axis), "co", hold)
 
-    down_grad = weight_grad(hidden, grad_full, 1)
-    grad_gate, grad_up, down_sent = lax.optimization_barrier((grad_gate, grad_up, down_grad[1]))
-    down_grad = over_cores([down_grad[0], down_sent])
-    mid = transposed_call(grad_gate, grad_up, gate_pieces, up_pieces)
-    mid_sum = peer_sum(cut(mid, PEER, 0))
-
-    up_grad = over_cores(weight_grad(normal_mid, grad_up, 0))
-    gate_grad = over_cores(weight_grad(normal_mid, grad_gate, 0))
+    down_grad = over_cores(weight_grad(hidden, grad_full, 1))
+    grad_gate, grad_up, down_grad = lax.optimization_barrier((grad_gate, grad_up, down_grad))
+    last_term = transposed_call(
+        grad_gate, grad_up, gate_pieces, up_pieces, own, PEER - 1
+    )
+    grad_gate, last_term = lax.optimization_barrier((grad_gate, last_term))
+    mid = transposed_call(grad_gate, grad_up, gate_pieces, up_pieces, own * (PEER - 1))
+    terms = cut(mid, PEER - 1, 0) + [last_term]
+    cross = peer(terms[3], 1)
+    relay = (terms[2].astype(F32) + cross.astype(F32)).astype(BF)
+    down_grad = over_chips(down_grad, 1)
+    near = peer(after(terms[1], cross), 1)
+    far = peer(relay, 2)
+    normal_late = after(normal_mid, cross)
+    up_grad = over_cores(weight_grad(normal_late, grad_up, 0))
+    gate_grad = over_cores(weight_grad(normal_late, grad_gate, 0))
+    up_grad = over_chips(after(up_grad, down_grad), 0)
+    down_last = around_back(cut(down_grad, nco, 0), "co")
+    mid_sum = terms[0].astype(F32) + near.astype(F32) + far.astype(F32)
+    mid_sum = after(mid_sum, gate_grad, down_grad)
     mlp = product_call(after(hidden, mid_sum), down_pieces)
-    down_grad = over_chips(down_grad, 1)
-    mid_sum = after(mid_sum, up_grad)
+    gate_grad = over_chips(after(gate_grad, up_grad), 0)
     gain_two_part = jnp.sum(mid_sum * normed_two, axis=0, keepdims=True)
     resid_grad = grad_mine.astype(F32) + norm_back(mid_sum, normed_two, inv_two, gain_two)
-    resid_group = peer_rows(resid_grad.astype(BF))
-    resid_all = jnp.stack(resid_group)
-    up_grad = over_chips(after(up_grad, down_grad), 0)
-    down_out = over_chunks(after(down_grad, resid_group[2]), 0)
-    resid_all = after(resid_all, up_grad, down_out, gate_grad)
+    resid_mine = resid_grad.astype(BF)
+    resid_near, resid_far = peer(resid_mine, 1), peer(resid_mine, 2)
+    resid_across = peer(after(resid_far, resid_near), 1)
+    resid_all = jnp.stack([resid_mine, resid_near, resid_far, resid_across])
 
     dh, grad_branch, local_end = back_call(place, resid_all, yp, h, decay, out_pieces, rows)
     mlp_terms = cut(after(mlp, resid_all), PEER, 0)
     mlp_cross = peer(mlp_terms[3], 1)
     mlp_near = peer(after(mlp_terms[1], mlp_cross), 1)
-    local_end = after(local_end, mlp_cross)
-    late = other_blocks(jnp.concatenate([summary[:rows], local_end], axis=0), rows, True)[rows:]
-    gate_grad = over_chips(after(gate_grad, late), 0)
+    local_end = after(local_end, mlp_cross, gate_grad)
+    late, mark = other_blocks(jnp.concatenate([summary[:rows], local_end], axis=0), rows, True)
+    late = late[rows:]
     relay = (mlp_terms[2].astype(F32) + mlp_cross.astype(F32)).astype(BF)
-    mlp_far = peer(after(relay, late), 2)
+    mlp_far = peer(after(relay, mark), 2)
+    up_last = around_back(cut(after(up_grad, mark), nco, 1), "co")
+    gate_last = around_back(cut(after(gate_grad, mlp_far), nco, 1), "co")
     mlp_sum = mlp_terms[0].astype(F32) + mlp_near.astype(F32) + mlp_far.astype(F32)
     mixed = (resid + mlp_sum).astype(BF)
     gates_low, grad_u, edge_out, last, sums, start_grad = grads_call(
@@ -952,7 +973,7 @@
     )
     edge_in = chunk_roll(block_shift(edge_out, -1), -1)
     grad_branch, resid_late = lax.optimization_barrier(
-        (grad_branch, resid_all, edge_out, mlp_cross)
+        (grad_branch, resid_all, edge_out, mlp_far)
     )[:2]
     grad_branch = grad_branch.reshape(group, width)
     normal_rows = normal_in.reshape(group, model)
@@ -962,33 +983,40 @@
     grad_u = lax.dynamic_update_slice(
         grad_u, fixed, (lax.bitwise_xor(ci, PEER - 1), own - lag * rows, 0)
     )
-    grad_u = grad_u.reshape(group, width)
-    back = transposed_call(grad_u, grad_branch, recur_pieces, branch_pieces)
-    up_last = around_back(cut(after(up_grad, late), nco, 1), "co")
-    gate_last = around_back(cut(after(gate_grad, late), nco, 1), "co")
-    terms = cut(after(back, mlp_near, mlp_far, *up_last[1:]), PEER, 0)
+    grad_u = after(grad_u, mlp_near, *up_last[1:]).reshape(group, width)
+    last_term = transposed_call(grad_u, grad_branch, recur_pieces, branch_pieces, own, PEER - 1)
+    grad_u, last_term = lax.optimization_barrier((grad_u, last_term))
+    back = transposed_call(
+        grad_u, grad_branch, recur_pieces, branch_pieces, own * (PEER - 1)
+    )
+    terms = cut(back, PEER - 1, 0) + [last_term]
     cross = peer(terms[3], 1)
-    near = peer(after(terms[1], cross), 1)
+    near = peer(after(terms[1], cross, out_grad, branch_grad), 1)
     relay = (terms[2].astype(F32) + cross.astype(F32)).astype(BF)
-    far = peer(after(relay, *gate_last[1:]), 2)
+    out_grad = over_chips(out_grad, 1)
+    far = peer(relay, 2)
+    out_last = around_back(cut(out_grad, nco, 0), "co")
     back_sum = terms[0].astype(F32) + near.astype(F32) + far.astype(F32)
+    back_sum = after(back_sum, *out_last[1:])
     both_grad = over_tokens(v.reshape(group, width), gates_low.reshape(group, 2 * width))
-    recur_grad = over_cores(weight_grad(normal_rows, grad_u, 0))
+    recur_grad = over_cores(weight_grad(normal_rows, after(grad_u, cross), 0))
     value = mine.astype(F32)
     inv_one = inverse_rms(value)
     normed_one = value * inv_one
-    x_value = after(x_all, late).astype(F32)
-    gain_one_part = jnp.sum(
-        back.reshape(PEER, own, model).astype(F32) * (x_value * inverse_rms(x_value)), axis=(0, 1)
-    )[None]
+    x_value = after(x_all, cross).astype(F32)
+    x_value = x_value * inverse_rms(x_value)
+    gain_one_part = sum(
+        jnp.sum(terms[k].astype(F32) * x_value[k], axis=0, keepdims=True) for k in range(PEER)
+    )
     tokens_grad = resid_grad + norm_back(back_sum, normed_one, inv_one, gain_one)
 
+    down_out = sum(after(item, late).astype(F32) for item in down_last)
     up_out = sum(item.astype(F32) for item in up_last)
-    gate_out = sum(item.astype(F32) for item in gate_last)
-    out_grad = over_chips(out_grad, 1)
-    branch_grad = over_chips(after(branch_grad, out_grad), 0)
-    out_out = over_chunks(out_grad, 0, back_sum)
-    recur_grad = over_chips(after(recur_grad, branch_grad), 0)
+    gate_out = sum(after(item, far).astype(F32) for item in gate_last)
+    branch_grad = over_chips(branch_grad, 0)
+    out_out = sum(item.astype(F32) for item in out_last)
+    held = recur_grad
+    recur_grad = over_chips(recur_grad, 0)
     branch_out = over_chunks(branch_grad, 1, back_sum)
     recur_out = over_chunks(recur_grad, 1)
 
@@ -1029,18 +1057,25 @@
     small = packed[lines:, :part]
 
     total = feature_restore(jnp.concatenate([gain_one_part, gain_two_part], axis=0))
-    for axis in ("sc", "sx", "cb", "ca", "co"):
+    for axis in ("sc", "sx", "cb", "ca"):
         if axis == "cb":
             total = after(total, back_sum)
         total = sum(around(total, axis)[1:], total)
+    finish = jnp.concatenate([h_end, ends.astype(F32)], axis=0)
+    reach = finish[:, :chunk]
+    fill = -reach.size % model
+    gathered = total
+    for r in range(1, nco):
+        piece = finish[:, (nco - r) * chunk : (nco - r + 1) * chunk].reshape(1, -1)
+        piece = jnp.pad(piece, ((0, 0), (0, fill))).reshape(-1, model)
+        got = shift(jnp.concatenate([total, piece], axis=0), "co", r)
+        gathered = gathered + got[:2]
+        piece = got[2:].reshape(-1)[: reach.size].reshape(reach.shape)
+        reach = jnp.where(co == r - 1, piece, reach)
+    total = gathered
     start = (lax.axis_index(("co", "ca", "cb")) * nseq + sx * nsc + sc) * unit
     gain_out = lax.dynamic_slice_in_dim(total, start, unit, 1)
 
-    finish = after(jnp.concatenate([h_end, ends.astype(F32)], axis=0), hidden)
-    reach = jnp.where(co == nco - 1, finish[:, :chunk], 0.0)
-    for k in range(1, nco):
-        piece = finish[:, (nco - k) * chunk : (nco - k + 1) * chunk]
-        reach = reach + lax.ppermute(piece, "co", [(nco - 1, k - 1)])
     group_states = reach[:rows][None]
     group_tails = jnp.swapaxes(reach[rows:].reshape(lag, rows, chunk), 0, 1).astype(BF)[None]
 

time: 839 us -> 746 us (0.89)
  waiting for transfers between devices: 400 us -> 296 us
  Pallas kernels: 147 us -> 165 us
  matrix products: 56.5 us -> 48 us
    ppermute x59, waiting for transfers between devices: 240 us -> 153 us  [shift(): lax.ppermute(value, axis, [(i, (i + step) % count) for i in range(count)])]
    ppermute x27, waiting for transfers between devices: 156 us -> 133 us  [peer(): return lax.ppermute(value, PEERS, [(i, i ^ step) for i in range(PEER)])]
    pallas_call x2 -> x4, Pallas kernels: 33.7 us -> 47.9 us  [transposed_call(): pl.pallas_call(functools.partial(transposed_kernel, count, per), out_shap...]
    ppermute x27, starting transfers between devices: 28.3 us -> 40.1 us  [peer(): return lax.ppermute(value, PEERS, [(i, i ^ step) for i in range(PEER)])]
    ppermute x59, starting transfers between devices: 61.4 us -> 50.8 us  [shift(): lax.ppermute(value, axis, [(i, (i + step) % count) for i in range(count)])]
    ppermute x1, waiting for transfers between devices: 0.01 us -> 9.35 us  [block_shift(): return lax.ppermute(value, BLOCKS, route)]
    dot_general x13, matrix products: 56.3 us -> 47.8 us  [over_tokens(): lax.dot_general(left, right, (((0,), (0,)), ((), ())), preferred_element_...]
    pallas_call x2 -> x3, Pallas kernels: 19.6 us -> 23.1 us  [product_call(): pl.pallas_call(functools.partial(product_kernel, count, per), out_shape=j...]
  transfers between devices with their start and end apart: 92 -> 91, of which waited for: 42 -> 36; matrix products, arithmetic and copies ran while one was open for 19% -> 20% of each run, Pallas kernels for 11% -> 15%
where the time goes in v4:
time: 746 us; the launch traced here: 739 us
  waiting for transfers between devices  296 us (40%)
  Pallas kernels  165 us (22%)
  starting transfers between devices  96 us (13%)
  other arithmetic  82.9 us (11%)
  local copies, waits for them, and re-layouts  48.4 us (6%)
  matrix products  48 us (6%)
    ppermute x59, waiting for transfers between devices, shift(): lax.ppermute(value, axis, [(i, (i + step) % count) for i in range(count)])  153 us
    ppermute x27, waiting for transfers between devices, peer(): return lax.ppermute(value, PEERS, [(i, i ^ step) for i in range(PEER)])  133 us
    ppermute x59, starting transfers between devices, shift(): lax.ppermute(value, axis, [(i, (i + step) % count) for i in range(count)])  50.8 us
    pallas_call x4, Pallas kernels, transposed_call(): pl.pallas_call(functools.partial(transposed_kernel, count, per), out_shap...  47.9 us
    dot_general x13, matrix products, over_tokens(): lax.dot_general(left, right, (((0,), (0,)), ((), ())), preferred_element_...  47.8 us
    ppermute x27, starting transfers between devices, peer(): return lax.ppermute(value, PEERS, [(i, i ^ step) for i in range(PEER)])  40.1 us
    pallas_call x1, Pallas kernels, mlp_call(): pl.pallas_call(functools.partial(mlp_kernel, count), out_shape=[jax.Shape...  27.4 us
    pallas_call x3, Pallas kernels, product_call(): pl.pallas_call(functools.partial(product_kernel, count, per), out_shape=j...  23.1 us
  transfers between devices with their start and end apart: 91, of which 36 were waited for; matrix products, arithmetic and copies ran while one was open for 20% of the time, Pallas kernels for 15%

profile of v4, /device:TPU:0, one launch (start us, length us, event | category | flops | bytes accessed | tf_op | source)
XLA Modules:
  0.0 739.1 jit_solution(10535761018439351153)
XLA Ops:
  28.7 7.1 collective-permute-start.3
  48.5 10.6 %collective-permute-done.4 = bf16[256,2048]{1,0:T(8,128)(2,1)} collective-permute-done((bf16[256,2048]{1,0:T(8,128)(2,1)S(1)}, bf16[256,2048]{1,0:T(8,128)(2,1)}, u32[]{:S(2)}, u32[]{:S(2)}) %collective-permute-start.4) | collective-permute-done | bytes 1048608 | tf_op jit(solution)/shard_map/ppermute | solution.py:32
  59.1 7.8 %collective-permute-start.5 = (bf16[256,2048]{1,0:T(8,128)(2,1)}, bf16[256,2048]{1,0:T(8,128)(2,1)}, u32[]{:S(2)}, u32[]{:S(2)}) collective-permute-start(bf16[256,2048]{1,0:T(8,128)(2,1)} %collective-permute-done.4), channel_id=1, source_target_pairs={{0,1},{1,0},{2,3},{3,2},{4,5},{5,4},{6,7},{7,6},{8,9},{9,8},{10,11... | collective-permute-start | bytes 3145736 | tf_op jit(solution)/shard_map/ppermute | solution.py:32
  78.9 12.7 %collective-permute-done.9.refs_1_ = bf16[512,320]{1,0:T(8,128)(2,1)} collective-permute-done((bf16[512,320]{1,0:T(8,128)(2,1)}, bf16[512,320]{1,0:T(8,128)(2,1)}, u32[]{:S(2)}, u32[]{:S(2)}) %collective-permute-start.9) | collective-permute-done | bytes 327712 | tf_op jit(solution)/shard_map/ppermute | solution.py:22
  105.5 16.0 %gates.1 = (bf16[4,256,2048]{2,1,0:T(8,128)(2,1)}, bf16[4,256,640]{2,1,0:T(8,128)(2,1)}, bf16[4,256,640]{2,1,0:T(8,128)(2,1)}, f32[4,256,640]{2,1,0:T(8,128)}, f...) custom-call(s32[2]{0:T(128)} %pad_add_fusion.here.place, ...), custom_call_target="tpu_custom_call" | custom-call | tf_op jit(solution)/shard_map/gates/pallas_call | solution.py:486
  131.0 11.9 %collective-permute-done.23 = f32[16,640]{1,0:T(8,128)S(1)} collective-permute-done((f32[16,640]{1,0:T(8,128)S(1)}, f32[16,640]{1,0:T(8,128)S(1)}, u32[]{:S(2)}, u32[]{:S(2)}) %collective-permute-start.23) | collective-permute-done | bytes 40992 | tf_op jit(solution)/shard_map/ppermute | solution.py:22
  146.2 7.4 branch.1.yp_ref
  153.6 6.6 states.1
  186.2 9.1 %collective-permute-done.30 = bf16[256,2048]{1,0:T(8,128)(2,1)} collective-permute-done((bf16[256,2048]{1,0:T(8,128)(2,1)}, bf16[256,2048]{1,0:T(8,128)(2,1)}, u32[]{:S(2)}, u32[]{:S(2)}) %collective-permute-start.30) | collective-permute-done | bytes 1048608 | tf_op jit(solution)/shard_map/ppermute | solution.py:32
  198.2 10.2 %collective-permute-done.32.refs_1_ = bf16[512,768]{1,0:T(8,128)(2,1)} collective-permute-done((bf16[512,768]{1,0:T(8,128)(2,1)}, bf16[512,768]{1,0:T(8,128)(2,1)}, u32[]{:S(2)}, u32[]{:S(2)}) %collective-permute-start.32) | collective-permute-done | bytes 786464 | tf_op jit(solution)/shard_map/ppermute | solution.py:22
  214.6 20.2 %collective-permute-done.37 = bf16[256,2048]{1,0:T(8,128)(2,1)} collective-permute-done((bf16[256,2048]{1,0:T(8,128)(2,1)}, bf16[256,2048]{1,0:T(8,128)(2,1)}, u32[]{:S(2)}, u32[]{:S(2)}) %collective-permute-start.37) | collective-permute-done | bytes 1048608 | tf_op jit(solution)/shard_map/ppermute | solution.py:32
  237.0 18.8 %collective-permute-done.33 = bf16[256,2048]{1,0:T(8,128)(2,1)} collective-permute-done((bf16[256,2048]{1,0:T(8,128)(2,1)}, bf16[256,2048]{1,0:T(8,128)(2,1)}, u32[]{:S(2)}, u32[]{:S(2)}) %collective-permute-start.33) | collective-permute-done | bytes 1048608 | tf_op jit(solution)/shard_map/ppermute | solution.py:32
  262.3 9.2 %pad_maximum_fusion.1.dy_ref = bf16[1024,2048]{1,0:T(8,128)(2,1)} fusion(bf16[256,2048]{1,0:T(8,128)(2,1)S(1)} %collective-permute-done.38, bf16[256,2048]{1,0:T(8,128)(2,1)} %collective-permute-done.37, bf16[256,2048]{1,0:T(8,128)(2,1)} %collective-permute-done.24, bf16[256,512]{1,0:T(8,128)(2,1)S(1)} %copy-done.41, bf16[256,512]{1,0:T(8,128)(2,1)S(1)} %copy-done.43, ...), kind=kLoop, calls=%fused_computation.7 | loop fusion | flops 29360128 | bytes 8388608 | tf_op jit(solution)/shard_map/concatenate | solution.py:889
  271.4 11.4 %collective-permute-done.35 = bf16[256,2048]{1,0:T(8,128)(2,1)S(1)} collective-permute-done((bf16[256,2048]{1,0:T(8,128)(2,1)S(1)}, bf16[256,2048]{1,0:T(8,128)(2,1)S(1)}, u32[]{:S(2)}, u32[]{:S(2)}) %collective-permute-start.35) | collective-permute-done | bytes 1048608 | tf_op jit(solution)/shard_map/ppermute | solution.py:32
  285.3 21.4 %collective-permute-done.39 = bf16[256,2048]{1,0:T(8,128)(2,1)S(1)} collective-permute-done((bf16[256,2048]{1,0:T(8,128)(2,1)S(1)}, bf16[256,2048]{1,0:T(8,128)(2,1)S(1)}, u32[]{:S(2)}, u32[]{:S(2)}) %collective-permute-start.39) | collective-permute-done | bytes 1048608 | tf_op jit(solution)/shard_map/ppermute | solution.py:32
  314.1 27.4 %mlp.1 = (bf16[1024,1536]{1,0:T(8,128)(2,1)}, bf16[1024,1536]{1,0:T(8,128)(2,1)}, bf16[1024,1536]{1,0:T(8,128)(2,1)}) custom-call(bf16[1024,2048]{1,0:T(8,128)(2,1)} %copy-done.25, bf16[1024,2048]{1,0:T(8,128)(2,1)} %pad_maximum_fusion.1.dy_ref, bf16[512,1536]{1,0:T(8,128)(2,1)} %join.6.refs_0_, bf16[512,1536]{1,0:T(8,128)(2,1)} %copy-done.10, ...), custom_call_target="tpu_custom_call" | custom-call | tf_op jit(solution)/shard_map/mlp/pallas_call | solution.py:669
  356.7 11.4 %transposed.4 = bf16[256,2048]{1,0:T(8,128)(2,1)} custom-call(bf16[1024,1536]{1,0:T(8,128)(2,1)} %get-tuple-element.144.x_ref, bf16[1024,1536]{1,0:T(8,128)(2,1)} %get-tuple-element.143.y_ref, bf16[512,1536]{1,0:T(8,128)(2,1)} %join.6.refs_0_, bf16[512,1536]{1,0:T(8,128)(2,1)} %copy-done.10, bf16[512,1536]{1,0:T(8,128)(2,1)} %copy-done.12, ...), custom_call_target="tpu_custom_call" | custom-call | tf_op jit(solution)/shard_map/transposed/pallas_call | solution.py:711
  368.7 17.3 %transposed.5 = bf16[768,2048]{1,0:T(8,128)(2,1)} custom-call(bf16[1024,1536]{1,0:T(8,128)(2,1)} %get-tuple-element.144.x_ref, bf16[1024,1536]{1,0:T(8,128)(2,1)} %get-tuple-element.143.y_ref, bf16[512,1536]{1,0:T(8,128)(2,1)} %join.6.refs_0_, bf16[512,1536]{1,0:T(8,128)(2,1)} %copy-done.10, bf16[512,1536]{1,0:T(8,128)(2,1)} %copy-done.12, ...), custom_call_target="tpu_custom_call" | custom-call | tf_op jit(solution)/shard_map/transposed/pallas_call | solution.py:711
  393.6 6.8 convolution_convert_fusion.2
  416.2 9.0 %collective-permute-done.54 = bf16[1536,512]{1,0:T(8,128)(2,1)S(1)} collective-permute-done((bf16[1536,512]{1,0:T(8,128)(2,1)S(1)}, bf16[1536,512]{1,0:T(8,128)(2,1)S(1)}, u32[]{:S(2)}, u32[]{:S(2)}) %collective-permute-start.54) | collective-permute-done | bytes 1572896 | tf_op jit(solution)/shard_map/ppermute | solution.py:22
  441.2 21.3 %collective-permute-done.56 = bf16[256,2048]{1,0:T(8,128)(2,1)} collective-permute-done((bf16[256,2048]{1,0:T(8,128)(2,1)S(1)}, bf16[256,2048]{1,0:T(8,128)(2,1)}, u32[]{:S(2)}, u32[]{:S(2)}) %collective-permute-start.56) | collective-permute-done | bytes 1048608 | tf_op jit(solution)/shard_map/ppermute | solution.py:32
  476.0 12.1 %product.5 = bf16[1024,2048]{1,0:T(8,128)(2,1)} custom-call(bf16[1024,1536]{1,0:T(8,128)(2,1)} %get-tuple-element.150.x_ref, bf16[1536,512]{1,0:T(8,128)(2,1)} %copy-done.9, bf16[1536,512]{1,0:T(8,128)(2,1)} %copy-done.30, bf16[1536,512]{1,0:T(8,128)(2,1)} %copy-done.31, bf16[1536,512]{1,0:T(8,128)(2,1)} %collective-permute-done.48.refs_11_.refs_3_), custom_call_target="tpu_custom_call" | custom-call | tf_op jit(solution)/shard_map/product/pallas_call | solution.py:691
  499.9 10.8 %back.1 = (f32[4,256,640]{2,1,0:T(8,128)}, bf16[4,256,640]{2,1,0:T(8,128)(2,1)}, f32[8,640]{1,0:T(8,128)}) custom-call(s32[2]{0:T(128)} %pad_add_fusion.here.place, bf16[4,256,2048]{2,1,0:T(8,128)(2,1)} %pad_maximum_fusion.2.g_ref, f32[4,256,640]{2,1,0:T(8,128)} %branch.1.yp_ref, f32[4,256,640]{2,1,0:T(8,128)} %get-tuple-element.154.h_ref, ...), custom_call_target="tpu_custom_call" | custom-call | tf_op jit(solution)/shard_map/back/pallas_call | solution.py:579
  523.0 12.5 %collective-permute-done.63 = f32[16,640]{1,0:T(8,128)S(1)} collective-permute-done((f32[16,640]{1,0:T(8,128)S(1)}, f32[16,640]{1,0:T(8,128)S(1)}, u32[]{:S(2)}, u32[]{:S(2)}) %collective-permute-start.63) | collective-permute-done | bytes 40992 | tf_op jit(solution)/shard_map/ppermute | solution.py:22
  543.7 14.4 %grads.1 = (bf16[4,256,1280]{2,1,0:T(8,128)(2,1)}, bf16[4,256,640]{2,1,0:T(8,128)(2,1)}, f32[24,640]{1,0:T(8,128)}, f32[24,640]{1,0:T(8,128)}, f32[64,640]{1,0:T(8,128)}, /*index=5*/f32[8,640]{1,0:T(8,128)}) custom-call(s32[2]{0:T(128)} %pad_add_fusion.here.place, f32[4,256,640]{2,1,0:T(8,128)} %get-tuple-element.160.dh_ref, ...), custom_call_target="tpu_custom_call" | custom-call | tf_op jit(solution)/shard_map/grads/pallas_call | solution.py:612
  571.6 9.4 %collective-permute-done.67 = f32[24,640]{1,0:T(8,128)} collective-permute-done((f32[24,640]{1,0:T(8,128)}, f32[24,640]{1,0:T(8,128)}, u32[]{:S(2)}, u32[]{:S(2)}) %collective-permute-start.67) | collective-permute-done | bytes 61472 | tf_op jit(solution)/shard_map/ppermute | solution.py:28
  598.4 8.3 %transposed.6 = bf16[256,2048]{1,0:T(8,128)(2,1)} custom-call(bf16[1024,640]{1,0:T(8,128)(2,1)} %bitcast.194, bf16[1024,640]{1,0:T(8,128)(2,1)} %bitcast.190, bf16[512,640]{1,0:T(8,128)(2,1)} %join.4.refs_0_, bf16[512,640]{1,0:T(8,128)(2,1)} %copy-done.32, bf16[512,640]{1,0:T(8,128)(2,1)} %collective-permute-done.16.refs_2_, ...), custom_call_target="tpu_custom_call" | custom-call | tf_op jit(solution)/shard_map/transposed/pallas_call | solution.py:711
  607.5 10.9 %transposed.7 = bf16[768,2048]{1,0:T(8,128)(2,1)} custom-call(bf16[1024,640]{1,0:T(8,128)(2,1)} %bitcast.195, bf16[1024,640]{1,0:T(8,128)(2,1)} %bitcast.191, bf16[512,640]{1,0:T(8,128)(2,1)} %join.4.refs_0_, bf16[512,640]{1,0:T(8,128)(2,1)} %copy-done.32, bf16[512,640]{1,0:T(8,128)(2,1)} %collective-permute-done.16.refs_2_, ...), custom_call_target="tpu_custom_call" | custom-call | tf_op jit(solution)/shard_map/transposed/pallas_call | solution.py:711
  644.3 13.1 %collective-permute-done.74 = bf16[640,512]{1,0:T(8,128)(2,1)S(1)} collective-permute-done((bf16[640,512]{1,0:T(8,128)(2,1)S(1)}, bf16[640,512]{1,0:T(8,128)(2,1)S(1)}, u32[]{:S(2)}, u32[]{:S(2)}) %collective-permute-start.74) | collective-permute-done | bytes 655392 | tf_op jit(solution)/shard_map/ppermute | solution.py:22
  658.9 11.8 %collective-permute-done.84 = bf16[512,640]{1,0:T(8,128)(2,1)S(1)} collective-permute-done((bf16[512,640]{1,0:T(8,128)(2,1)S(1)}, bf16[512,640]{1,0:T(8,128)(2,1)S(1)}, u32[]{:S(2)}, u32[]{:S(2)}) %collective-permute-start.84) | collective-permute-done | bytes 655392 | tf_op jit(solution)/shard_map/ppermute | solution.py:22
  680.6 17.0 %collective-permute-done.75 = bf16[320,512]{1,0:T(8,128)(2,1)S(1)} collective-permute-done((bf16[320,512]{1,0:T(8,128)(2,1)S(1)}, bf16[320,512]{1,0:T(8,128)(2,1)S(1)}, u32[]{:S(2)}, u32[]{:S(2)}) %collective-permute-start.75) | collective-permute-done | bytes 327712 | tf_op jit(solution)/shard_map/ppermute | solution.py:22
  723.0 14.5 %collective-permute-done.83 = bf16[512,320]{1,0:T(8,128)(2,1)S(1)} collective-permute-done((bf16[512,320]{1,0:T(8,128)(2,1)S(1)}, bf16[512,320]{1,0:T(8,128)(2,1)S(1)}, u32[]{:S(2)}, u32[]{:S(2)}) %collective-permute-start.83) | collective-permute-done | bytes 327712 | tf_op jit(solution)/shard_map/ppermute | solution.py:22
  (558 shorter events, 328.0 us)
Async XLA Ops:
  28.3 30.8 %collective-permute-start.4 = (bf16[256,2048]{1,0:T(8,128)(2,1)S(1)}, bf16[256,2048]{1,0:T(8,128)(2,1)}, u32[]{:S(2)}, u32[]{:S(2)}) collective-permute-start(bf16[256,2048]{1,0:T(8,128)(2,1)S(1)} %get-tuple-element.107), channel_id=1, source_target_pairs={{0,2},{1,3},{2,0},{3,1},{4,6},{5,7},{6,4},{7,5},{8,10},{9,11},{10,... | collective-permute-start | bytes 3145736 | tf_op jit(solution)/shard_map/ppermute | solution.py:32
  28.7 30.5 %collective-permute-start.3 = (bf16[256,2048]{1,0:T(8,128)(2,1)S(1)}, bf16[256,2048]{1,0:T(8,128)(2,1)}, u32[]{:S(2)}, u32[]{:S(2)}) collective-permute-start(bf16[256,2048]{1,0:T(8,128)(2,1)S(1)} %get-tuple-element.107), channel_id=1, source_target_pairs={{0,1},{1,0},{2,3},{3,2},{4,5},{5,4},{6,7},{7,6},{8,9},{9,8},{10,11... | collective-permute-start | bytes 3145736 | tf_op jit(solution)/shard_map/ppermute | solution.py:32
  59.1 42.1 %collective-permute-start.5 = (bf16[256,2048]{1,0:T(8,128)(2,1)}, bf16[256,2048]{1,0:T(8,128)(2,1)}, u32[]{:S(2)}, u32[]{:S(2)}) collective-permute-start(bf16[256,2048]{1,0:T(8,128)(2,1)} %collective-permute-done.4), channel_id=1, source_target_pairs={{0,1},{1,0},{2,3},{3,2},{4,5},{5,4},{6,7},{7,6},{8,9},{9,8},{10,11... | collective-permute-start | bytes 3145736 | tf_op jit(solution)/shard_map/ppermute | solution.py:32
  93.9 27.6 %collective-permute-start.18 = (bf16[512,640]{1,0:T(8,128)(2,1)}, bf16[512,640]{1,0:T(8,128)(2,1)}, u32[]{:S(2)}, u32[]{:S(2)}) collective-permute-start(bf16[512,640]{1,0:T(8,128)(2,1)} %join.5.refs_0_.refs_4_), channel_id=1, source_target_pairs={{0,16},{16,0},{1,17},{17,1},{2,18},{18,2},{3,19},{19,3},{4,20},{20... | collective-permute-start | bytes 1966088 | tf_op jit(solution)/shard_map/ppermute | solution.py:22
  101.3 29.7 %collective-permute-start.19 = (bf16[512,640]{1,0:T(8,128)(2,1)S(1)}, bf16[512,640]{1,0:T(8,128)(2,1)}, u32[]{:S(2)}, u32[]{:S(2)}) collective-permute-start(bf16[512,640]{1,0:T(8,128)(2,1)S(1)} %copy-done.22), channel_id=1, source_target_pairs={{0,8},{8,0},{1,9},{9,1},{2,10},{10,2},{3,11},{11,3},{4,12},{12,4},... | collective-permute-start | bytes 1966088 | tf_op jit(solution)/shard_map/ppermute | solution.py:22
  125.8 27.8 %collective-permute-start.24 = (bf16[256,2048]{1,0:T(8,128)(2,1)}, bf16[256,2048]{1,0:T(8,128)(2,1)}, u32[]{:S(2)}, u32[]{:S(2)}) collective-permute-start(bf16[256,2048]{1,0:T(8,128)(2,1)} %pad_maximum_fusion.5), channel_id=1, source_target_pairs={{0,1},{1,0},{2,3},{3,2},{4,5},{5,4},{6,7},{7,6},{8,9},{9,8},{10,11... | collective-permute-start | bytes 3145736 | tf_op jit(solution)/shard_map/ppermute | solution.py:32
  127.8 38.0 %collective-permute-start.27 = (bf16[512,768]{1,0:T(8,128)(2,1)}, bf16[512,768]{1,0:T(8,128)(2,1)}, u32[]{:S(2)}, u32[]{:S(2)}) collective-permute-start(bf16[512,768]{1,0:T(8,128)(2,1)} %refs_0_), channel_id=1, source_target_pairs={{0,4},{4,0},{1,5},{5,1},{2,6},{6,2},{3,7},{7,3},{8,12},{12,8},{9,1... | collective-permute-start | bytes 2359304 | tf_op jit(solution)/shard_map/ppermute | solution.py:22
  131.0 34.9 %collective-permute-start.28 = (bf16[640,512]{1,0:T(8,128)(2,1)S(1)}, bf16[640,512]{1,0:T(8,128)(2,1)}, u32[]{:S(2)}, u32[]{:S(2)}) collective-permute-start(bf16[640,512]{1,0:T(8,128)(2,1)S(1)} %pad_maximum_fusion.12.refs_0_), channel_id=1, source_target_pairs={{0,8},{8,0},{1,9},{9,1},{2,10},{10,2},{3,11},{11,3},{4,12},{12,4},... | collective-permute-start | bytes 1966088 | tf_op jit(solution)/shard_map/ppermute | solution.py:22
  171.3 37.0 %collective-permute-start.32 = (bf16[512,768]{1,0:T(8,128)(2,1)}, bf16[512,768]{1,0:T(8,128)(2,1)}, u32[]{:S(2)}, u32[]{:S(2)}) collective-permute-start(bf16[512,768]{1,0:T(8,128)(2,1)} %refs_0_.1), channel_id=1, source_target_pairs={{0,4},{4,0},{1,5},{5,1},{2,6},{6,2},{3,7},{7,3},{8,12},{12,8},{9,1... | collective-permute-start | bytes 2359304 | tf_op jit(solution)/shard_map/ppermute | solution.py:22
  173.6 37.9 %collective-permute-start.40 = (bf16[512,1536]{1,0:T(8,128)(2,1)}, bf16[512,1536]{1,0:T(8,128)(2,1)S(1)}, u32[]{:S(2)}, u32[]{:S(2)}) collective-permute-start(bf16[512,1536]{1,0:T(8,128)(2,1)} %join.6.refs_0_), channel_id=1, source_target_pairs={{0,16},{16,0},{1,17},{17,1},{2,18},{18,2},{3,19},{19,3},{4,20},{20... | collective-permute-start | bytes 4718600 | tf_op jit(solution)/shard_map/ppermute | solution.py:22
  175.2 59.6 %collective-permute-start.37 = (bf16[256,2048]{1,0:T(8,128)(2,1)}, bf16[256,2048]{1,0:T(8,128)(2,1)}, u32[]{:S(2)}, u32[]{:S(2)}) collective-permute-start(bf16[256,2048]{1,0:T(8,128)(2,1)} %pad_maximum_fusion.5), channel_id=1, source_target_pairs={{0,2},{1,3},{2,0},{3,1},{4,6},{5,7},{6,4},{7,5},{8,10},{9,11},{10,... | collective-permute-start | bytes 3145736 | tf_op jit(solution)/shard_map/ppermute | solution.py:32
  208.3 47.4 %collective-permute-start.33 = (bf16[256,2048]{1,0:T(8,128)(2,1)}, bf16[256,2048]{1,0:T(8,128)(2,1)}, u32[]{:S(2)}, u32[]{:S(2)}) collective-permute-start(bf16[256,2048]{1,0:T(8,128)(2,1)} %add_convert_fusion.12), channel_id=1, source_target_pairs={{0,2},{1,3},{2,0},{3,1},{4,6},{5,7},{6,4},{7,5},{8,10},{9,11},{10,... | collective-permute-start | bytes 3145736 | tf_op jit(solution)/shard_map/ppermute | solution.py:32
  208.4 47.4 %collective-permute-start.31 = (bf16[256,2048]{1,0:T(8,128)(2,1)}, bf16[256,2048]{1,0:T(8,128)(2,1)}, u32[]{:S(2)}, u32[]{:S(2)}) collective-permute-start(bf16[256,2048]{1,0:T(8,128)(2,1)} %slice.600), channel_id=1, source_target_pairs={{0,1},{1,0},{2,3},{3,2},{4,5},{5,4},{6,7},{7,6},{8,9},{9,8},{10,11... | collective-permute-start | bytes 3145736 | tf_op jit(solution)/shard_map/ppermute | solution.py:32
  211.6 49.5 %collective-permute-start.43 = (bf16[512,1536]{1,0:T(8,128)(2,1)}, bf16[512,1536]{1,0:T(8,128)(2,1)}, u32[]{:S(2)}, u32[]{:S(2)}) collective-permute-start(bf16[512,1536]{1,0:T(8,128)(2,1)} %join.7.refs_4_), channel_id=1, source_target_pairs={{0,16},{16,0},{1,17},{17,1},{2,18},{18,2},{3,19},{19,3},{4,20},{20... | collective-permute-start | bytes 4718600 | tf_op jit(solution)/shard_map/ppermute | solution.py:22
  212.8 45.8 %collective-permute-start.34 = (bf16[768,512]{1,0:T(8,128)(2,1)}, bf16[768,512]{1,0:T(8,128)(2,1)S(1)}, u32[]{:S(2)}, u32[]{:S(2)}) collective-permute-start(bf16[768,512]{1,0:T(8,128)(2,1)} %param.28), channel_id=1, source_target_pairs={{0,4},{4,0},{1,5},{5,1},{2,6},{6,2},{3,7},{7,3},{8,12},{12,8},{9,1... | collective-permute-start | bytes 2359304 | tf_op jit(solution)/shard_map/ppermute | solution.py:22
  234.8 27.5 %collective-permute-start.38 = (bf16[256,2048]{1,0:T(8,128)(2,1)}, bf16[256,2048]{1,0:T(8,128)(2,1)S(1)}, u32[]{:S(2)}, u32[]{:S(2)}) collective-permute-start(bf16[256,2048]{1,0:T(8,128)(2,1)} %collective-permute-done.37), channel_id=1, source_target_pairs={{0,1},{1,0},{2,3},{3,2},{4,5},{5,4},{6,7},{7,6},{8,9},{9,8},{10,11... | collective-permute-start | bytes 3145736 | tf_op jit(solution)/shard_map/ppermute | solution.py:32
  261.0 45.7 %collective-permute-start.46 = (bf16[1536,512]{1,0:T(8,128)(2,1)S(1)}, bf16[1536,512]{1,0:T(8,128)(2,1)S(1)}, u32[]{:S(2)}, u32[]{:S(2)}) collective-permute-start(bf16[1536,512]{1,0:T(8,128)(2,1)S(1)} %pad_maximum_fusion.3.refs_8_.refs_0_), channel_id=1, source_target_pairs={{0,16},{16,0},{1,17},{17,1},{2,18},{18,2},{3,19},{19,3},{4,20},{20... | collective-permute-start | bytes 4718600 | tf_op jit(solution)/shard_map/ppermute | solution.py:22
  389.0 36.2 %collective-permute-start.54 = (bf16[1536,512]{1,0:T(8,128)(2,1)S(1)}, bf16[1536,512]{1,0:T(8,128)(2,1)S(1)}, u32[]{:S(2)}, u32[]{:S(2)}) collective-permute-start(bf16[1536,512]{1,0:T(8,128)(2,1)S(1)} %slice.487), channel_id=1, source_target_pairs={{0,16},{16,0},{1,17},{17,1},{2,18},{18,2},{3,19},{19,3},{4,20},{20... | collective-permute-start | bytes 4718600 | tf_op jit(solution)/shard_map/ppermute | solution.py:22
  404.1 28.2 %collective-permute-start.53 = (bf16[1024,1536]{1,0:T(8,128)(2,1)}, bf16[1024,1536]{1,0:T(8,128)(2,1)S(1)}, u32[]{:S(2)}, u32[]{:S(2)}) collective-permute-start(bf16[1024,1536]{1,0:T(8,128)(2,1)} %convolution_convert_fusion.2), channel_id=1, source_target_pairs={{0,8},{8,0},{1,9},{9,1},{2,10},{10,2},{3,11},{11,3},{4,12},{12,4},... | collective-permute-start | bytes 9437192 | tf_op jit(solution)/shard_map/ppermute | solution.py:22
  435.7 35.6 %collective-permute-start.61 = (bf16[512,1536]{1,0:T(8,128)(2,1)S(1)}, bf16[512,1536]{1,0:T(8,128)(2,1)S(1)}, u32[]{:S(2)}, u32[]{:S(2)}) collective-permute-start(bf16[512,1536]{1,0:T(8,128)(2,1)S(1)} %slice.494), channel_id=1, source_target_pairs={{0,16},{16,0},{1,17},{17,1},{2,18},{18,2},{3,19},{19,3},{4,20},{20... | collective-permute-start | bytes 4718600 | tf_op jit(solution)/shard_map/ppermute | solution.py:22
  474.1 36.6 %collective-permute-start.62 = (bf16[512,1536]{1,0:T(8,128)(2,1)}, bf16[512,1536]{1,0:T(8,128)(2,1)}, u32[]{:S(2)}, u32[]{:S(2)}) collective-permute-start(bf16[512,1536]{1,0:T(8,128)(2,1)} %slice.496), channel_id=1, source_target_pairs={{0,16},{16,0},{1,17},{17,1},{2,18},{18,2},{3,19},{19,3},{4,20},{20... | collective-permute-start | bytes 4718600 | tf_op jit(solution)/shard_map/ppermute | solution.py:22
  498.5 62.8 %collective-permute-start.87 = (bf16[768,512]{1,0:T(8,128)(2,1)}, bf16[768,512]{1,0:T(8,128)(2,1)}, u32[]{:S(2)}, u32[]{:S(2)}) collective-permute-start(bf16[768,512]{1,0:T(8,128)(2,1)} %get-tuple-element.297), channel_id=1, source_target_pairs={{0,4},{4,0},{1,5},{5,1},{2,6},{6,2},{3,7},{7,3},{8,12},{12,8},{9,1... | collective-permute-start | bytes 2359304 | tf_op jit(solution)/shard_map/ppermute | solution.py:22
  518.6 71.2 %collective-permute-start.59 = (bf16[256,2048]{1,0:T(8,128)(2,1)}, bf16[256,2048]{1,0:T(8,128)(2,1)}, u32[]{:S(2)}, u32[]{:S(2)}) collective-permute-start(bf16[256,2048]{1,0:T(8,128)(2,1)} %get-tuple-element.153), channel_id=1, source_target_pairs={{0,1},{1,0},{2,3},{3,2},{4,5},{5,4},{6,7},{7,6},{8,9},{9,8},{10,11... | collective-permute-start | bytes 3145736 | tf_op jit(solution)/shard_map/ppermute | solution.py:32
  535.9 54.0 %collective-permute-start.64 = (bf16[256,2048]{1,0:T(8,128)(2,1)}, bf16[256,2048]{1,0:T(8,128)(2,1)}, u32[]{:S(2)}, u32[]{:S(2)}) collective-permute-start(bf16[256,2048]{1,0:T(8,128)(2,1)} %add_convert_fusion.10), channel_id=1, source_target_pairs={{0,2},{1,3},{2,0},{3,1},{4,6},{5,7},{6,4},{7,5},{8,10},{9,11},{10,... | collective-permute-start | bytes 3145736 | tf_op jit(solution)/shard_map/ppermute | solution.py:32
  536.9 52.9 %collective-permute-start.68 = (bf16[512,768]{1,0:T(8,128)(2,1)}, bf16[512,768]{1,0:T(8,128)(2,1)}, u32[]{:S(2)}, u32[]{:S(2)}) collective-permute-start(bf16[512,768]{1,0:T(8,128)(2,1)} %slice.514), channel_id=1, source_target_pairs={{0,4},{4,0},{1,5},{5,1},{2,6},{6,2},{3,7},{7,3},{8,12},{12,8},{9,1... | collective-permute-start | bytes 2359304 | tf_op jit(solution)/shard_map/ppermute | solution.py:22
  627.9 45.8 %collective-permute-start.86 = (bf16[512,768]{1,0:T(8,128)(2,1)}, bf16[512,768]{1,0:T(8,128)(2,1)}, u32[]{:S(2)}, u32[]{:S(2)}) collective-permute-start(bf16[512,768]{1,0:T(8,128)(2,1)} %get-tuple-element.299), channel_id=1, source_target_pairs={{0,4},{4,0},{1,5},{5,1},{2,6},{6,2},{3,7},{7,3},{8,12},{12,8},{9,1... | collective-permute-start | bytes 2359304 | tf_op jit(solution)/shard_map/ppermute | solution.py:22
  636.0 41.3 %collective-permute-start.73 = (bf16[256,2048]{1,0:T(8,128)(2,1)S(1)}, bf16[256,2048]{1,0:T(8,128)(2,1)S(1)}, u32[]{:S(2)}, u32[]{:S(2)}) collective-permute-start(bf16[256,2048]{1,0:T(8,128)(2,1)S(1)} %get-tuple-element.291), channel_id=1, source_target_pairs={{0,2},{1,3},{2,0},{3,1},{4,6},{5,7},{6,4},{7,5},{8,10},{9,11},{10,... | collective-permute-start | bytes 3145736 | tf_op jit(solution)/shard_map/ppermute | solution.py:32
  641.4 29.3 %collective-permute-start.84 = (bf16[512,640]{1,0:T(8,128)(2,1)S(1)}, bf16[512,640]{1,0:T(8,128)(2,1)S(1)}, u32[]{:S(2)}, u32[]{:S(2)}) collective-permute-start(bf16[512,640]{1,0:T(8,128)(2,1)S(1)} %slice.649), channel_id=1, source_target_pairs={{0,16},{16,0},{1,17},{17,1},{2,18},{18,2},{3,19},{19,3},{4,20},{20... | collective-permute-start | bytes 1966088 | tf_op jit(solution)/shard_map/ppermute | solution.py:22
  644.2 57.3 %collective-permute-start.81 = (bf16[1024,640]{1,0:T(8,128)(2,1)S(1)}, bf16[1024,640]{1,0:T(8,128)(2,1)S(1)}, u32[]{:S(2)}, u32[]{:S(2)}) collective-permute-start(bf16[1024,640]{1,0:T(8,128)(2,1)S(1)} %fusion.45), channel_id=1, source_target_pairs={{0,8},{8,0},{1,9},{9,1},{2,10},{10,2},{3,11},{11,3},{4,12},{12,4},... | collective-permute-start | bytes 3932168 | tf_op jit(solution)/shard_map/ppermute | solution.py:22
  657.4 41.2 %collective-permute-start.72 = (bf16[256,2048]{1,0:T(8,128)(2,1)S(1)}, bf16[256,2048]{1,0:T(8,128)(2,1)S(1)}, u32[]{:S(2)}, u32[]{:S(2)}) collective-permute-start(bf16[256,2048]{1,0:T(8,128)(2,1)S(1)} %slice.628), channel_id=1, source_target_pairs={{0,1},{1,0},{2,3},{3,2},{4,5},{5,4},{6,7},{7,6},{8,9},{9,8},{10,11... | collective-permute-start | bytes 3145736 | tf_op jit(solution)/shard_map/ppermute | solution.py:32
  670.7 26.9 %collective-permute-start.75 = (bf16[320,512]{1,0:T(8,128)(2,1)S(1)}, bf16[320,512]{1,0:T(8,128)(2,1)S(1)}, u32[]{:S(2)}, u32[]{:S(2)}) collective-permute-start(bf16[320,512]{1,0:T(8,128)(2,1)S(1)} %slice.636), channel_id=1, source_target_pairs={{0,4},{4,0},{1,5},{5,1},{2,6},{6,2},{3,7},{7,3},{8,12},{12,8},{9,1... | collective-permute-start | bytes 983048 | tf_op jit(solution)/shard_map/ppermute | solution.py:22
  673.7 32.3 %collective-permute-start.85 = (bf16[512,320]{1,0:T(8,128)(2,1)S(1)}, bf16[512,320]{1,0:T(8,128)(2,1)S(1)}, u32[]{:S(2)}, u32[]{:S(2)}) collective-permute-start(bf16[512,320]{1,0:T(8,128)(2,1)S(1)} %slice.651), channel_id=1, source_target_pairs={{0,4},{4,0},{1,5},{5,1},{2,6},{6,2},{3,7},{7,3},{8,12},{12,8},{9,1... | collective-permute-start | bytes 983048 | tf_op jit(solution)/shard_map/ppermute | solution.py:22
  (150 other events, 2253.9 us)

commit v5 on v4

--- a/solution.py
+++ b/solution.py
@@ -997,9 +997,10 @@
     far = peer(relay, 2)
     out_last = around_back(cut(out_grad, nco, 0), "co")
     back_sum = terms[0].astype(F32) + near.astype(F32) + far.astype(F32)
-    back_sum = after(back_sum, *out_last[1:])
     both_grad = over_tokens(v.reshape(group, width), gates_low.reshape(group, 2 * width))
     recur_grad = over_cores(weight_grad(normal_rows, after(grad_u, cross), 0))
+    branch_grad = over_chips(branch_grad, 0)
+    back_sum = after(back_sum, branch_grad, recur_grad)
     value = mine.astype(F32)
     inv_one = inverse_rms(value)
     normed_one = value * inv_one
@@ -1013,7 +1014,6 @@
     down_out = sum(after(item, late).astype(F32) for item in down_last)
     up_out = sum(item.astype(F32) for item in up_last)
     gate_out = sum(after(item, far).astype(F32) for item in gate_last)
-    branch_grad = over_chips(branch_grad, 0)
     out_out = sum(item.astype(F32) for item in out_last)
     held = recur_grad
     recur_grad = over_chips(recur_grad, 0)
@@ -1059,7 +1059,7 @@
     total = feature_restore(jnp.concatenate([gain_one_part, gain_two_part], axis=0))
     for axis in ("sc", "sx", "cb", "ca"):
         if axis == "cb":
-            total = after(total, back_sum)
+            total = after(total, back_sum, *out_last[1:])
         total = sum(around(total, axis)[1:], total)
     finish = jnp.concatenate([h_end, ends.astype(F32)], axis=0)
     reach = finish[:, :chunk]

time: 746 us -> 744 us (level)
  waiting for transfers between devices: 296 us -> 284 us
    ppermute x59, waiting for transfers between devices: 153 us -> 140 us  [shift(): lax.ppermute(value, axis, [(i, (i + step) % count) for i in range(count)])]
  transfers between devices with their start and end apart: 91 -> 91, of which waited for: 36 -> 35; matrix products, arithmetic and copies ran while one was open for 20% -> 22% of each run, Pallas kernels for 15% -> 15%
where the time goes in v5:
time: 744 us; the launch traced here: 737 us
  waiting for transfers between devices  284 us (38%)
  Pallas kernels  166 us (22%)
  starting transfers between devices  99 us (13%)
  other arithmetic  87.4 us (12%)
  matrix products  49.5 us (7%)
  local copies, waits for them, and re-layouts  48.8 us (7%)
    ppermute x59, waiting for transfers between devices, shift(): lax.ppermute(value, axis, [(i, (i + step) % count) for i in range(count)])  140 us
    ppermute x27, waiting for transfers between devices, peer(): return lax.ppermute(value, PEERS, [(i, i ^ step) for i in range(PEER)])  135 us
    ppermute x59, starting transfers between devices, shift(): lax.ppermute(value, axis, [(i, (i + step) % count) for i in range(count)])  51.6 us
    dot_general x13, matrix products, over_tokens(): lax.dot_general(left, right, (((0,), (0,)), ((), ())), preferred_element_...  49.3 us
    pallas_call x4, Pallas kernels, transposed_call(): pl.pallas_call(functools.partial(transposed_kernel, count, per), out_shap...  48 us
    ppermute x27, starting transfers between devices, peer(): return lax.ppermute(value, PEERS, [(i, i ^ step) for i in range(PEER)])  42.2 us
    pallas_call x1, Pallas kernels, mlp_call(): pl.pallas_call(functools.partial(mlp_kernel, count), out_shape=[jax.Shape...  27.6 us
    pallas_call x3, Pallas kernels, product_call(): pl.pallas_call(functools.partial(product_kernel, count, per), out_shape=j...  22.9 us
  transfers between devices with their start and end apart: 91, of which 35 were waited for; matrix products, arithmetic and copies ran while one was open for 22% of the time, Pallas kernels for 15%

profile of v5, /device:TPU:0, one launch (start us, length us, event | category | flops | bytes accessed | tf_op | source)
XLA Modules:
  0.0 737.1 jit_solution(17287970879025069669)
XLA Ops:
  28.6 7.1 collective-permute-start.3
  48.5 10.6 %collective-permute-done.4 = bf16[256,2048]{1,0:T(8,128)(2,1)} collective-permute-done((bf16[256,2048]{1,0:T(8,128)(2,1)S(1)}, bf16[256,2048]{1,0:T(8,128)(2,1)}, u32[]{:S(2)}, u32[]{:S(2)}) %collective-permute-start.4) | collective-permute-done | bytes 1048608 | tf_op jit(solution)/shard_map/ppermute | solution.py:32
  59.1 7.8 %collective-permute-start.5 = (bf16[256,2048]{1,0:T(8,128)(2,1)}, bf16[256,2048]{1,0:T(8,128)(2,1)}, u32[]{:S(2)}, u32[]{:S(2)}) collective-permute-start(bf16[256,2048]{1,0:T(8,128)(2,1)} %collective-permute-done.4), channel_id=1, source_target_pairs={{0,1},{1,0},{2,3},{3,2},{4,5},{5,4},{6,7},{7,6},{8,9},{9,8},{10,11... | collective-permute-start | bytes 3145736 | tf_op jit(solution)/shard_map/ppermute | solution.py:32
  78.9 12.7 %collective-permute-done.9.refs_1_ = bf16[512,320]{1,0:T(8,128)(2,1)} collective-permute-done((bf16[512,320]{1,0:T(8,128)(2,1)}, bf16[512,320]{1,0:T(8,128)(2,1)}, u32[]{:S(2)}, u32[]{:S(2)}) %collective-permute-start.9) | collective-permute-done | bytes 327712 | tf_op jit(solution)/shard_map/ppermute | solution.py:22
  105.5 16.0 %gates.1 = (bf16[4,256,2048]{2,1,0:T(8,128)(2,1)}, bf16[4,256,640]{2,1,0:T(8,128)(2,1)}, bf16[4,256,640]{2,1,0:T(8,128)(2,1)}, f32[4,256,640]{2,1,0:T(8,128)}, f...) custom-call(s32[2]{0:T(128)} %pad_add_fusion.here.place, ...), custom_call_target="tpu_custom_call" | custom-call | tf_op jit(solution)/shard_map/gates/pallas_call | solution.py:486
  131.0 11.8 %collective-permute-done.23 = f32[16,640]{1,0:T(8,128)S(1)} collective-permute-done((f32[16,640]{1,0:T(8,128)S(1)}, f32[16,640]{1,0:T(8,128)S(1)}, u32[]{:S(2)}, u32[]{:S(2)}) %collective-permute-start.23) | collective-permute-done | bytes 40992 | tf_op jit(solution)/shard_map/ppermute | solution.py:22
  146.2 7.4 branch.1.yp_ref
  186.0 9.2 %collective-permute-done.30 = bf16[256,2048]{1,0:T(8,128)(2,1)} collective-permute-done((bf16[256,2048]{1,0:T(8,128)(2,1)}, bf16[256,2048]{1,0:T(8,128)(2,1)}, u32[]{:S(2)}, u32[]{:S(2)}) %collective-permute-start.30) | collective-permute-done | bytes 1048608 | tf_op jit(solution)/shard_map/ppermute | solution.py:32
  198.1 10.2 %collective-permute-done.32.refs_1_ = bf16[512,768]{1,0:T(8,128)(2,1)} collective-permute-done((bf16[512,768]{1,0:T(8,128)(2,1)}, bf16[512,768]{1,0:T(8,128)(2,1)}, u32[]{:S(2)}, u32[]{:S(2)}) %collective-permute-start.32) | collective-permute-done | bytes 786464 | tf_op jit(solution)/shard_map/ppermute | solution.py:22
  214.5 20.2 %collective-permute-done.37 = bf16[256,2048]{1,0:T(8,128)(2,1)} collective-permute-done((bf16[256,2048]{1,0:T(8,128)(2,1)}, bf16[256,2048]{1,0:T(8,128)(2,1)}, u32[]{:S(2)}, u32[]{:S(2)}) %collective-permute-start.37) | collective-permute-done | bytes 1048608 | tf_op jit(solution)/shard_map/ppermute | solution.py:32
  237.0 18.8 %collective-permute-done.33 = bf16[256,2048]{1,0:T(8,128)(2,1)} collective-permute-done((bf16[256,2048]{1,0:T(8,128)(2,1)}, bf16[256,2048]{1,0:T(8,128)(2,1)}, u32[]{:S(2)}, u32[]{:S(2)}) %collective-permute-start.33) | collective-permute-done | bytes 1048608 | tf_op jit(solution)/shard_map/ppermute | solution.py:32
  262.3 9.2 %pad_maximum_fusion.1.dy_ref = bf16[1024,2048]{1,0:T(8,128)(2,1)} fusion(bf16[256,2048]{1,0:T(8,128)(2,1)S(1)} %collective-permute-done.38, bf16[256,2048]{1,0:T(8,128)(2,1)} %collective-permute-done.37, bf16[256,2048]{1,0:T(8,128)(2,1)} %collective-permute-done.24, bf16[256,512]{1,0:T(8,128)(2,1)S(1)} %copy-done.42, bf16[256,512]{1,0:T(8,128)(2,1)S(1)} %copy-done.44, ...), kind=kLoop, calls=%fused_computation.7 | loop fusion | flops 29360128 | bytes 8388608 | tf_op jit(solution)/shard_map/concatenate | solution.py:889
  271.4 11.4 %collective-permute-done.35 = bf16[256,2048]{1,0:T(8,128)(2,1)S(1)} collective-permute-done((bf16[256,2048]{1,0:T(8,128)(2,1)S(1)}, bf16[256,2048]{1,0:T(8,128)(2,1)S(1)}, u32[]{:S(2)}, u32[]{:S(2)}) %collective-permute-start.35) | collective-permute-done | bytes 1048608 | tf_op jit(solution)/shard_map/ppermute | solution.py:32
  285.3 21.4 %collective-permute-done.39 = bf16[256,2048]{1,0:T(8,128)(2,1)S(1)} collective-permute-done((bf16[256,2048]{1,0:T(8,128)(2,1)S(1)}, bf16[256,2048]{1,0:T(8,128)(2,1)S(1)}, u32[]{:S(2)}, u32[]{:S(2)}) %collective-permute-start.39) | collective-permute-done | bytes 1048608 | tf_op jit(solution)/shard_map/ppermute | solution.py:32
  314.1 27.6 %mlp.1 = (bf16[1024,1536]{1,0:T(8,128)(2,1)}, bf16[1024,1536]{1,0:T(8,128)(2,1)}, bf16[1024,1536]{1,0:T(8,128)(2,1)}) custom-call(bf16[1024,2048]{1,0:T(8,128)(2,1)} %copy-done.24, bf16[1024,2048]{1,0:T(8,128)(2,1)} %pad_maximum_fusion.1.dy_ref, bf16[512,1536]{1,0:T(8,128)(2,1)} %join.6.refs_0_, bf16[512,1536]{1,0:T(8,128)(2,1)} %copy-done.9, ...), custom_call_target="tpu_custom_call" | custom-call | tf_op jit(solution)/shard_map/mlp/pallas_call | solution.py:669
  356.9 11.4 %transposed.4 = bf16[256,2048]{1,0:T(8,128)(2,1)} custom-call(bf16[1024,1536]{1,0:T(8,128)(2,1)} %get-tuple-element.144.x_ref, bf16[1024,1536]{1,0:T(8,128)(2,1)} %get-tuple-element.143.y_ref, bf16[512,1536]{1,0:T(8,128)(2,1)} %join.6.refs_0_, bf16[512,1536]{1,0:T(8,128)(2,1)} %copy-done.9, bf16[512,1536]{1,0:T(8,128)(2,1)} %copy-done.11, ...), custom_call_target="tpu_custom_call" | custom-call | tf_op jit(solution)/shard_map/transposed/pallas_call | solution.py:711
  369.0 17.3 %transposed.5 = bf16[768,2048]{1,0:T(8,128)(2,1)} custom-call(bf16[1024,1536]{1,0:T(8,128)(2,1)} %get-tuple-element.144.x_ref, bf16[1024,1536]{1,0:T(8,128)(2,1)} %get-tuple-element.143.y_ref, bf16[512,1536]{1,0:T(8,128)(2,1)} %join.6.refs_0_, bf16[512,1536]{1,0:T(8,128)(2,1)} %copy-done.9, bf16[512,1536]{1,0:T(8,128)(2,1)} %copy-done.11, ...), custom_call_target="tpu_custom_call" | custom-call | tf_op jit(solution)/shard_map/transposed/pallas_call | solution.py:711
  393.8 6.7 convolution_convert_fusion.2
  416.2 9.3 %collective-permute-done.54 = bf16[1536,512]{1,0:T(8,128)(2,1)S(1)} collective-permute-done((bf16[1536,512]{1,0:T(8,128)(2,1)S(1)}, bf16[1536,512]{1,0:T(8,128)(2,1)S(1)}, u32[]{:S(2)}, u32[]{:S(2)}) %collective-permute-start.54) | collective-permute-done | bytes 1572896 | tf_op jit(solution)/shard_map/ppermute | solution.py:22
  441.4 21.3 %collective-permute-done.56 = bf16[256,2048]{1,0:T(8,128)(2,1)} collective-permute-done((bf16[256,2048]{1,0:T(8,128)(2,1)S(1)}, bf16[256,2048]{1,0:T(8,128)(2,1)}, u32[]{:S(2)}, u32[]{:S(2)}) %collective-permute-start.56) | collective-permute-done | bytes 1048608 | tf_op jit(solution)/shard_map/ppermute | solution.py:32
  476.2 12.1 %product.5 = bf16[1024,2048]{1,0:T(8,128)(2,1)} custom-call(bf16[1024,1536]{1,0:T(8,128)(2,1)} %get-tuple-element.150.x_ref, bf16[1536,512]{1,0:T(8,128)(2,1)} %copy-done.8, bf16[1536,512]{1,0:T(8,128)(2,1)} %copy-done.29, bf16[1536,512]{1,0:T(8,128)(2,1)} %copy-done.30, bf16[1536,512]{1,0:T(8,128)(2,1)} %collective-permute-done.48.refs_11_.refs_3_), custom_call_target="tpu_custom_call" | custom-call | tf_op jit(solution)/shard_map/product/pallas_call | solution.py:691
  500.1 11.0 %back.1 = (f32[4,256,640]{2,1,0:T(8,128)}, bf16[4,256,640]{2,1,0:T(8,128)(2,1)}, f32[8,640]{1,0:T(8,128)}) custom-call(s32[2]{0:T(128)} %pad_add_fusion.here.place, bf16[4,256,2048]{2,1,0:T(8,128)(2,1)} %pad_maximum_fusion.2.g_ref, f32[4,256,640]{2,1,0:T(8,128)} %branch.1.yp_ref, f32[4,256,640]{2,1,0:T(8,128)} %get-tuple-element.154.h_ref, ...), custom_call_target="tpu_custom_call" | custom-call | tf_op jit(solution)/shard_map/back/pallas_call | solution.py:579
  523.2 12.6 %collective-permute-done.63 = f32[16,640]{1,0:T(8,128)S(1)} collective-permute-done((f32[16,640]{1,0:T(8,128)S(1)}, f32[16,640]{1,0:T(8,128)S(1)}, u32[]{:S(2)}, u32[]{:S(2)}) %collective-permute-start.63) | collective-permute-done | bytes 40992 | tf_op jit(solution)/shard_map/ppermute | solution.py:22
  543.8 14.4 %grads.1 = (bf16[4,256,1280]{2,1,0:T(8,128)(2,1)}, bf16[4,256,640]{2,1,0:T(8,128)(2,1)}, f32[24,640]{1,0:T(8,128)}, f32[24,640]{1,0:T(8,128)}, f32[64,640]{1,0:T(8,128)}, /*index=5*/f32[8,640]{1,0:T(8,128)}) custom-call(s32[2]{0:T(128)} %pad_add_fusion.here.place, f32[4,256,640]{2,1,0:T(8,128)} %get-tuple-element.160.dh_ref, ...), custom_call_target="tpu_custom_call" | custom-call | tf_op jit(solution)/shard_map/grads/pallas_call | solution.py:612
  571.7 9.4 %collective-permute-done.67 = f32[24,640]{1,0:T(8,128)} collective-permute-done((f32[24,640]{1,0:T(8,128)}, f32[24,640]{1,0:T(8,128)}, u32[]{:S(2)}, u32[]{:S(2)}) %collective-permute-start.67) | collective-permute-done | bytes 61472 | tf_op jit(solution)/shard_map/ppermute | solution.py:28
  590.0 8.4 %transposed.6 = bf16[256,2048]{1,0:T(8,128)(2,1)} custom-call(bf16[1024,640]{1,0:T(8,128)(2,1)} %bitcast.194, bf16[1024,640]{1,0:T(8,128)(2,1)} %bitcast.190, bf16[512,640]{1,0:T(8,128)(2,1)} %join.4.refs_0_, bf16[512,640]{1,0:T(8,128)(2,1)} %copy-done.31, bf16[512,640]{1,0:T(8,128)(2,1)} %collective-permute-done.16.refs_2_, ...), custom_call_target="tpu_custom_call" | custom-call | tf_op jit(solution)/shard_map/transposed/pallas_call | solution.py:711
  611.5 11.0 %transposed.7 = bf16[768,2048]{1,0:T(8,128)(2,1)} custom-call(bf16[1024,640]{1,0:T(8,128)(2,1)} %bitcast.195, bf16[1024,640]{1,0:T(8,128)(2,1)} %bitcast.191, bf16[512,640]{1,0:T(8,128)(2,1)} %join.4.refs_0_, bf16[512,640]{1,0:T(8,128)(2,1)} %copy-done.31, bf16[512,640]{1,0:T(8,128)(2,1)} %collective-permute-done.16.refs_2_, ...), custom_call_target="tpu_custom_call" | custom-call | tf_op jit(solution)/shard_map/transposed/pallas_call | solution.py:711
  649.6 9.8 %collective-permute-done.74 = bf16[512,640]{1,0:T(8,128)(2,1)S(1)} collective-permute-done((bf16[512,640]{1,0:T(8,128)(2,1)S(1)}, bf16[512,640]{1,0:T(8,128)(2,1)S(1)}, u32[]{:S(2)}, u32[]{:S(2)}) %collective-permute-start.74) | collective-permute-done | bytes 655392 | tf_op jit(solution)/shard_map/ppermute | solution.py:22
  660.1 11.8 %collective-permute-done.78 = bf16[640,512]{1,0:T(8,128)(2,1)S(1)} collective-permute-done((bf16[640,512]{1,0:T(8,128)(2,1)S(1)}, bf16[640,512]{1,0:T(8,128)(2,1)S(1)}, u32[]{:S(2)}, u32[]{:S(2)}) %collective-permute-start.78) | collective-permute-done | bytes 655392 | tf_op jit(solution)/shard_map/ppermute | solution.py:22
  675.6 8.3 %collective-permute-done.73 = bf16[256,2048]{1,0:T(8,128)(2,1)S(1)} collective-permute-done((bf16[256,2048]{1,0:T(8,128)(2,1)S(1)}, bf16[256,2048]{1,0:T(8,128)(2,1)S(1)}, u32[]{:S(2)}, u32[]{:S(2)}) %collective-permute-start.73) | collective-permute-done | bytes 1048608 | tf_op jit(solution)/shard_map/ppermute | solution.py:32
  687.1 12.3 %collective-permute-done.79 = bf16[320,512]{1,0:T(8,128)(2,1)S(1)} collective-permute-done((bf16[320,512]{1,0:T(8,128)(2,1)S(1)}, bf16[320,512]{1,0:T(8,128)(2,1)S(1)}, u32[]{:S(2)}, u32[]{:S(2)}) %collective-permute-start.79) | collective-permute-done | bytes 327712 | tf_op jit(solution)/shard_map/ppermute | solution.py:22
  725.1 10.6 %collective-permute-done.84 = bf16[512,320]{1,0:T(8,128)(2,1)S(1)} collective-permute-done((bf16[512,320]{1,0:T(8,128)(2,1)S(1)}, bf16[512,320]{1,0:T(8,128)(2,1)S(1)}, u32[]{:S(2)}, u32[]{:S(2)}) %collective-permute-start.84) | collective-permute-done | bytes 327712 | tf_op jit(solution)/shard_map/ppermute | solution.py:22
  (564 shorter events, 335.3 us)
Async XLA Ops:
  28.3 30.8 %collective-permute-start.4 = (bf16[256,2048]{1,0:T(8,128)(2,1)S(1)}, bf16[256,2048]{1,0:T(8,128)(2,1)}, u32[]{:S(2)}, u32[]{:S(2)}) collective-permute-start(bf16[256,2048]{1,0:T(8,128)(2,1)S(1)} %get-tuple-element.107), channel_id=1, source_target_pairs={{0,2},{1,3},{2,0},{3,1},{4,6},{5,7},{6,4},{7,5},{8,10},{9,11},{10,... | collective-permute-start | bytes 3145736 | tf_op jit(solution)/shard_map/ppermute | solution.py:32
  28.6 30.5 %collective-permute-start.3 = (bf16[256,2048]{1,0:T(8,128)(2,1)S(1)}, bf16[256,2048]{1,0:T(8,128)(2,1)}, u32[]{:S(2)}, u32[]{:S(2)}) collective-permute-start(bf16[256,2048]{1,0:T(8,128)(2,1)S(1)} %get-tuple-element.107), channel_id=1, source_target_pairs={{0,1},{1,0},{2,3},{3,2},{4,5},{5,4},{6,7},{7,6},{8,9},{9,8},{10,11... | collective-permute-start | bytes 3145736 | tf_op jit(solution)/shard_map/ppermute | solution.py:32
  59.1 42.1 %collective-permute-start.5 = (bf16[256,2048]{1,0:T(8,128)(2,1)}, bf16[256,2048]{1,0:T(8,128)(2,1)}, u32[]{:S(2)}, u32[]{:S(2)}) collective-permute-start(bf16[256,2048]{1,0:T(8,128)(2,1)} %collective-permute-done.4), channel_id=1, source_target_pairs={{0,1},{1,0},{2,3},{3,2},{4,5},{5,4},{6,7},{7,6},{8,9},{9,8},{10,11... | collective-permute-start | bytes 3145736 | tf_op jit(solution)/shard_map/ppermute | solution.py:32
  93.9 27.6 %collective-permute-start.18 = (bf16[512,640]{1,0:T(8,128)(2,1)}, bf16[512,640]{1,0:T(8,128)(2,1)}, u32[]{:S(2)}, u32[]{:S(2)}) collective-permute-start(bf16[512,640]{1,0:T(8,128)(2,1)} %join.5.refs_0_.refs_4_), channel_id=1, source_target_pairs={{0,16},{16,0},{1,17},{17,1},{2,18},{18,2},{3,19},{19,3},{4,20},{20... | collective-permute-start | bytes 1966088 | tf_op jit(solution)/shard_map/ppermute | solution.py:22
  101.3 29.7 %collective-permute-start.19 = (bf16[512,640]{1,0:T(8,128)(2,1)S(1)}, bf16[512,640]{1,0:T(8,128)(2,1)}, u32[]{:S(2)}, u32[]{:S(2)}) collective-permute-start(bf16[512,640]{1,0:T(8,128)(2,1)S(1)} %copy-done.21), channel_id=1, source_target_pairs={{0,8},{8,0},{1,9},{9,1},{2,10},{10,2},{3,11},{11,3},{4,12},{12,4},... | collective-permute-start | bytes 1966088 | tf_op jit(solution)/shard_map/ppermute | solution.py:22
  125.8 27.7 %collective-permute-start.24 = (bf16[256,2048]{1,0:T(8,128)(2,1)}, bf16[256,2048]{1,0:T(8,128)(2,1)}, u32[]{:S(2)}, u32[]{:S(2)}) collective-permute-start(bf16[256,2048]{1,0:T(8,128)(2,1)} %pad_maximum_fusion.5), channel_id=1, source_target_pairs={{0,1},{1,0},{2,3},{3,2},{4,5},{5,4},{6,7},{7,6},{8,9},{9,8},{10,11... | collective-permute-start | bytes 3145736 | tf_op jit(solution)/shard_map/ppermute | solution.py:32
  127.8 38.0 %collective-permute-start.27 = (bf16[512,768]{1,0:T(8,128)(2,1)}, bf16[512,768]{1,0:T(8,128)(2,1)}, u32[]{:S(2)}, u32[]{:S(2)}) collective-permute-start(bf16[512,768]{1,0:T(8,128)(2,1)} %refs_0_), channel_id=1, source_target_pairs={{0,4},{4,0},{1,5},{5,1},{2,6},{6,2},{3,7},{7,3},{8,12},{12,8},{9,1... | collective-permute-start | bytes 2359304 | tf_op jit(solution)/shard_map/ppermute | solution.py:22
  130.9 34.8 %collective-permute-start.28 = (bf16[640,512]{1,0:T(8,128)(2,1)S(1)}, bf16[640,512]{1,0:T(8,128)(2,1)}, u32[]{:S(2)}, u32[]{:S(2)}) collective-permute-start(bf16[640,512]{1,0:T(8,128)(2,1)S(1)} %pad_maximum_fusion.12.refs_0_), channel_id=1, source_target_pairs={{0,8},{8,0},{1,9},{9,1},{2,10},{10,2},{3,11},{11,3},{4,12},{12,4},... | collective-permute-start | bytes 1966088 | tf_op jit(solution)/shard_map/ppermute | solution.py:22
  171.3 37.0 %collective-permute-start.32 = (bf16[512,768]{1,0:T(8,128)(2,1)}, bf16[512,768]{1,0:T(8,128)(2,1)}, u32[]{:S(2)}, u32[]{:S(2)}) collective-permute-start(bf16[512,768]{1,0:T(8,128)(2,1)} %refs_0_.1), channel_id=1, source_target_pairs={{0,4},{4,0},{1,5},{5,1},{2,6},{6,2},{3,7},{7,3},{8,12},{12,8},{9,1... | collective-permute-start | bytes 2359304 | tf_op jit(solution)/shard_map/ppermute | solution.py:22
  173.6 37.9 %collective-permute-start.40 = (bf16[512,1536]{1,0:T(8,128)(2,1)}, bf16[512,1536]{1,0:T(8,128)(2,1)S(1)}, u32[]{:S(2)}, u32[]{:S(2)}) collective-permute-start(bf16[512,1536]{1,0:T(8,128)(2,1)} %join.6.refs_0_), channel_id=1, source_target_pairs={{0,16},{16,0},{1,17},{17,1},{2,18},{18,2},{3,19},{19,3},{4,20},{20... | collective-permute-start | bytes 4718600 | tf_op jit(solution)/shard_map/ppermute | solution.py:22
  175.2 59.6 %collective-permute-start.37 = (bf16[256,2048]{1,0:T(8,128)(2,1)}, bf16[256,2048]{1,0:T(8,128)(2,1)}, u32[]{:S(2)}, u32[]{:S(2)}) collective-permute-start(bf16[256,2048]{1,0:T(8,128)(2,1)} %pad_maximum_fusion.5), channel_id=1, source_target_pairs={{0,2},{1,3},{2,0},{3,1},{4,6},{5,7},{6,4},{7,5},{8,10},{9,11},{10,... | collective-permute-start | bytes 3145736 | tf_op jit(solution)/shard_map/ppermute | solution.py:32
  208.3 47.4 %collective-permute-start.33 = (bf16[256,2048]{1,0:T(8,128)(2,1)}, bf16[256,2048]{1,0:T(8,128)(2,1)}, u32[]{:S(2)}, u32[]{:S(2)}) collective-permute-start(bf16[256,2048]{1,0:T(8,128)(2,1)} %add_convert_fusion.12), channel_id=1, source_target_pairs={{0,2},{1,3},{2,0},{3,1},{4,6},{5,7},{6,4},{7,5},{8,10},{9,11},{10,... | collective-permute-start | bytes 3145736 | tf_op jit(solution)/shard_map/ppermute | solution.py:32
  208.3 47.4 %collective-permute-start.31 = (bf16[256,2048]{1,0:T(8,128)(2,1)}, bf16[256,2048]{1,0:T(8,128)(2,1)}, u32[]{:S(2)}, u32[]{:S(2)}) collective-permute-start(bf16[256,2048]{1,0:T(8,128)(2,1)} %slice.600), channel_id=1, source_target_pairs={{0,1},{1,0},{2,3},{3,2},{4,5},{5,4},{6,7},{7,6},{8,9},{9,8},{10,11... | collective-permute-start | bytes 3145736 | tf_op jit(solution)/shard_map/ppermute | solution.py:32
  211.5 49.5 %collective-permute-start.43 = (bf16[512,1536]{1,0:T(8,128)(2,1)}, bf16[512,1536]{1,0:T(8,128)(2,1)}, u32[]{:S(2)}, u32[]{:S(2)}) collective-permute-start(bf16[512,1536]{1,0:T(8,128)(2,1)} %join.7.refs_4_), channel_id=1, source_target_pairs={{0,16},{16,0},{1,17},{17,1},{2,18},{18,2},{3,19},{19,3},{4,20},{20... | collective-permute-start | bytes 4718600 | tf_op jit(solution)/shard_map/ppermute | solution.py:22
  212.8 45.8 %collective-permute-start.34 = (bf16[768,512]{1,0:T(8,128)(2,1)}, bf16[768,512]{1,0:T(8,128)(2,1)S(1)}, u32[]{:S(2)}, u32[]{:S(2)}) collective-permute-start(bf16[768,512]{1,0:T(8,128)(2,1)} %param.28), channel_id=1, source_target_pairs={{0,4},{4,0},{1,5},{5,1},{2,6},{6,2},{3,7},{7,3},{8,12},{12,8},{9,1... | collective-permute-start | bytes 2359304 | tf_op jit(solution)/shard_map/ppermute | solution.py:22
  261.0 45.7 %collective-permute-start.46 = (bf16[1536,512]{1,0:T(8,128)(2,1)S(1)}, bf16[1536,512]{1,0:T(8,128)(2,1)S(1)}, u32[]{:S(2)}, u32[]{:S(2)}) collective-permute-start(bf16[1536,512]{1,0:T(8,128)(2,1)S(1)} %pad_maximum_fusion.3.refs_8_.refs_0_), channel_id=1, source_target_pairs={{0,16},{16,0},{1,17},{17,1},{2,18},{18,2},{3,19},{19,3},{4,20},{20... | collective-permute-start | bytes 4718600 | tf_op jit(solution)/shard_map/ppermute | solution.py:22
  389.2 36.2 %collective-permute-start.54 = (bf16[1536,512]{1,0:T(8,128)(2,1)S(1)}, bf16[1536,512]{1,0:T(8,128)(2,1)S(1)}, u32[]{:S(2)}, u32[]{:S(2)}) collective-permute-start(bf16[1536,512]{1,0:T(8,128)(2,1)S(1)} %slice.487), channel_id=1, source_target_pairs={{0,16},{16,0},{1,17},{17,1},{2,18},{18,2},{3,19},{19,3},{4,20},{20... | collective-permute-start | bytes 4718600 | tf_op jit(solution)/shard_map/ppermute | solution.py:22
  404.3 28.2 %collective-permute-start.53 = (bf16[1024,1536]{1,0:T(8,128)(2,1)}, bf16[1024,1536]{1,0:T(8,128)(2,1)S(1)}, u32[]{:S(2)}, u32[]{:S(2)}) collective-permute-start(bf16[1024,1536]{1,0:T(8,128)(2,1)} %convolution_convert_fusion.2), channel_id=1, source_target_pairs={{0,8},{8,0},{1,9},{9,1},{2,10},{10,2},{3,11},{11,3},{4,12},{12,4},... | collective-permute-start | bytes 9437192 | tf_op jit(solution)/shard_map/ppermute | solution.py:22
  435.9 35.6 %collective-permute-start.61 = (bf16[512,1536]{1,0:T(8,128)(2,1)S(1)}, bf16[512,1536]{1,0:T(8,128)(2,1)S(1)}, u32[]{:S(2)}, u32[]{:S(2)}) collective-permute-start(bf16[512,1536]{1,0:T(8,128)(2,1)S(1)} %slice.494), channel_id=1, source_target_pairs={{0,16},{16,0},{1,17},{17,1},{2,18},{18,2},{3,19},{19,3},{4,20},{20... | collective-permute-start | bytes 4718600 | tf_op jit(solution)/shard_map/ppermute | solution.py:22
  474.3 36.8 %collective-permute-start.62 = (bf16[512,1536]{1,0:T(8,128)(2,1)}, bf16[512,1536]{1,0:T(8,128)(2,1)}, u32[]{:S(2)}, u32[]{:S(2)}) collective-permute-start(bf16[512,1536]{1,0:T(8,128)(2,1)} %slice.496), channel_id=1, source_target_pairs={{0,16},{16,0},{1,17},{17,1},{2,18},{18,2},{3,19},{19,3},{4,20},{20... | collective-permute-start | bytes 4718600 | tf_op jit(solution)/shard_map/ppermute | solution.py:22
  498.7 62.7 %collective-permute-start.87 = (bf16[768,512]{1,0:T(8,128)(2,1)}, bf16[768,512]{1,0:T(8,128)(2,1)}, u32[]{:S(2)}, u32[]{:S(2)}) collective-permute-start(bf16[768,512]{1,0:T(8,128)(2,1)} %get-tuple-element.297), channel_id=1, source_target_pairs={{0,4},{4,0},{1,5},{5,1},{2,6},{6,2},{3,7},{7,3},{8,12},{12,8},{9,1... | collective-permute-start | bytes 2359304 | tf_op jit(solution)/shard_map/ppermute | solution.py:22
  518.8 71.2 %collective-permute-start.59 = (bf16[256,2048]{1,0:T(8,128)(2,1)}, bf16[256,2048]{1,0:T(8,128)(2,1)}, u32[]{:S(2)}, u32[]{:S(2)}) collective-permute-start(bf16[256,2048]{1,0:T(8,128)(2,1)} %get-tuple-element.153), channel_id=1, source_target_pairs={{0,1},{1,0},{2,3},{3,2},{4,5},{5,4},{6,7},{7,6},{8,9},{9,8},{10,11... | collective-permute-start | bytes 3145736 | tf_op jit(solution)/shard_map/ppermute | solution.py:32
  536.1 53.9 %collective-permute-start.64 = (bf16[256,2048]{1,0:T(8,128)(2,1)}, bf16[256,2048]{1,0:T(8,128)(2,1)}, u32[]{:S(2)}, u32[]{:S(2)}) collective-permute-start(bf16[256,2048]{1,0:T(8,128)(2,1)} %add_convert_fusion.10), channel_id=1, source_target_pairs={{0,2},{1,3},{2,0},{3,1},{4,6},{5,7},{6,4},{7,5},{8,10},{9,11},{10,... | collective-permute-start | bytes 3145736 | tf_op jit(solution)/shard_map/ppermute | solution.py:32
  537.1 52.9 %collective-permute-start.68 = (bf16[512,768]{1,0:T(8,128)(2,1)}, bf16[512,768]{1,0:T(8,128)(2,1)}, u32[]{:S(2)}, u32[]{:S(2)}) collective-permute-start(bf16[512,768]{1,0:T(8,128)(2,1)} %slice.514), channel_id=1, source_target_pairs={{0,4},{4,0},{1,5},{5,1},{2,6},{6,2},{3,7},{7,3},{8,12},{12,8},{9,1... | collective-permute-start | bytes 2359304 | tf_op jit(solution)/shard_map/ppermute | solution.py:22
  598.4 29.4 %collective-permute-start.69 = (bf16[256,2048]{1,0:T(8,128)(2,1)}, bf16[256,2048]{1,0:T(8,128)(2,1)}, u32[]{:S(2)}, u32[]{:S(2)}) collective-permute-start(bf16[256,2048]{1,0:T(8,128)(2,1)} %transposed.6), channel_id=1, source_target_pairs={{0,1},{1,0},{2,3},{3,2},{4,5},{5,4},{6,7},{7,6},{8,9},{9,8},{10,11... | collective-permute-start | bytes 3145736 | tf_op jit(solution)/shard_map/ppermute | solution.py:32
  603.6 39.4 %collective-permute-start.70 = (bf16[640,1024]{1,0:T(8,128)(2,1)}, bf16[640,1024]{1,0:T(8,128)(2,1)}, u32[]{:S(2)}, u32[]{:S(2)}) collective-permute-start(bf16[640,1024]{1,0:T(8,128)(2,1)} %fusion.51), channel_id=1, source_target_pairs={{0,8},{8,0},{1,9},{9,1},{2,10},{10,2},{3,11},{11,3},{4,12},{12,4},... | collective-permute-start | bytes 3932168 | tf_op jit(solution)/shard_map/ppermute | solution.py:22
  606.6 33.3 %collective-permute-start.71 = (bf16[1024,640]{1,0:T(8,128)(2,1)}, bf16[1024,640]{1,0:T(8,128)(2,1)}, u32[]{:S(2)}, u32[]{:S(2)}) collective-permute-start(bf16[1024,640]{1,0:T(8,128)(2,1)} %fusion.42), channel_id=1, source_target_pairs={{0,8},{8,0},{1,9},{9,1},{2,10},{10,2},{3,11},{11,3},{4,12},{12,4},... | collective-permute-start | bytes 3932168 | tf_op jit(solution)/shard_map/ppermute | solution.py:22
  636.1 37.4 %collective-permute-start.86 = (bf16[512,768]{1,0:T(8,128)(2,1)S(1)}, bf16[512,768]{1,0:T(8,128)(2,1)S(1)}, u32[]{:S(2)}, u32[]{:S(2)}) collective-permute-start(bf16[512,768]{1,0:T(8,128)(2,1)S(1)} %copy-done.62), channel_id=1, source_target_pairs={{0,4},{4,0},{1,5},{5,1},{2,6},{6,2},{3,7},{7,3},{8,12},{12,8},{9,1... | collective-permute-start | bytes 2359304 | tf_op jit(solution)/shard_map/ppermute | solution.py:22
  636.3 47.6 %collective-permute-start.73 = (bf16[256,2048]{1,0:T(8,128)(2,1)S(1)}, bf16[256,2048]{1,0:T(8,128)(2,1)S(1)}, u32[]{:S(2)}, u32[]{:S(2)}) collective-permute-start(bf16[256,2048]{1,0:T(8,128)(2,1)S(1)} %get-tuple-element.291), channel_id=1, source_target_pairs={{0,2},{1,3},{2,0},{3,1},{4,6},{5,7},{6,4},{7,5},{8,10},{9,11},{10,... | collective-permute-start | bytes 3145736 | tf_op jit(solution)/shard_map/ppermute | solution.py:32
  647.6 52.7 %collective-permute-start.75 = (bf16[1024,640]{1,0:T(8,128)(2,1)S(1)}, bf16[1024,640]{1,0:T(8,128)(2,1)S(1)}, u32[]{:S(2)}, u32[]{:S(2)}) collective-permute-start(bf16[1024,640]{1,0:T(8,128)(2,1)S(1)} %fusion.45), channel_id=1, source_target_pairs={{0,8},{8,0},{1,9},{9,1},{2,10},{10,2},{3,11},{11,3},{4,12},{12,4},... | collective-permute-start | bytes 3932168 | tf_op jit(solution)/shard_map/ppermute | solution.py:22
  659.4 41.4 %collective-permute-start.72 = (bf16[256,2048]{1,0:T(8,128)(2,1)S(1)}, bf16[256,2048]{1,0:T(8,128)(2,1)S(1)}, u32[]{:S(2)}, u32[]{:S(2)}) collective-permute-start(bf16[256,2048]{1,0:T(8,128)(2,1)S(1)} %slice.628), channel_id=1, source_target_pairs={{0,1},{1,0},{2,3},{3,2},{4,5},{5,4},{6,7},{7,6},{8,9},{9,8},{10,11... | collective-permute-start | bytes 3145736 | tf_op jit(solution)/shard_map/ppermute | solution.py:32
  673.5 35.6 %collective-permute-start.85 = (bf16[512,320]{1,0:T(8,128)(2,1)S(1)}, bf16[512,320]{1,0:T(8,128)(2,1)S(1)}, u32[]{:S(2)}, u32[]{:S(2)}) collective-permute-start(bf16[512,320]{1,0:T(8,128)(2,1)S(1)} %slice.651), channel_id=1, source_target_pairs={{0,4},{4,0},{1,5},{5,1},{2,6},{6,2},{3,7},{7,3},{8,12},{12,8},{9,1... | collective-permute-start | bytes 983048 | tf_op jit(solution)/shard_map/ppermute | solution.py:22
  (153 other events, 2244.7 us)
